TPU v7x, 32 devices: a whole 2x2x4 slice. The times are simulated.
32 devices in a mesh: dp: 16 (over z, y, x), head: 2 (over core).
Axes of the slice: x: 2, y: 2, z: 4, core: 2. Of those that a mesh axis runs over, the one named last changes fastest.
Arguments:
- inputs: bfloat16 [16, 2, 512, 768], P('dp'), may hold values from -6 to 6
- cotangent: bfloat16 [16, 2, 512, 768], P('dp'), may hold values from -6 to 6
- seg_counts: int32 [16], P('dp'), may hold values from 1 to 2
- qkv_weight: float32 [3, 768, 768], P(None, 'dp', 'head'), may hold values from -0.3125 to 0.3125
- out_weight: float32 [768, 768], P('head', 'dp'), may hold values from -0.875 to 0.875
- up_weight: float32 [768, 3072], P('dp', 'head'), may hold values from -0.21875 to 0.21875
- down_weight: float32 [3072, 768], P('head', 'dp'), may hold values from -0.109375 to 0.109375
- head_bias: float32 [2, 2304], P('head'), may hold values from -3 to 3
- shared_params: float32 [16, 768], replicated, may hold values from -5 to 5
- qkv_first: float32 [3, 768, 768], P(None, 'dp', 'head'), may hold values from -0.00024414062 to 0.00024414062
- out_first: float32 [768, 768], P('head', 'dp'), may hold values from -0.00024414062 to 0.00024414062
- up_first: float32 [768, 3072], P('dp', 'head'), may hold values from -0.00024414062 to 0.00024414062
- down_first: float32 [3072, 768], P('head', 'dp'), may hold values from -0.00024414062 to 0.00024414062
- bias_first: float32 [2, 2304], P('head'), may hold values from -0.00024414062 to 0.00024414062
- shared_first: float32 [16, 768], replicated, may hold values from -0.00024414062 to 0.00024414062
- qkv_second: float32 [3, 768, 768], P(None, 'dp', 'head'), may hold values from 1.4094861e-10 to 5.6379446e-10
- out_second: float32 [768, 768], P('head', 'dp'), may hold values from 1.4094861e-10 to 5.6379446e-10
- up_second: float32 [768, 3072], P('dp', 'head'), may hold values from 1.4094861e-10 to 5.6379446e-10
- down_second: float32 [3072, 768], P('head', 'dp'), may hold values from 1.4094861e-10 to 5.6379446e-10
- bias_second: float32 [2, 2304], P('head'), may hold values from 1.4094861e-10 to 5.6379446e-10
- shared_second: float32 [16, 768], replicated, may hold values from 1.4094861e-10 to 5.6379446e-10
Outputs:
- outputs: bfloat16 [16, 2, 512, 768], P('dp')
- input_grad: bfloat16 [16, 2, 512, 768], P('dp')
- grad_norm: float32 [], replicated
- qkv_update: float32 [3, 768, 768], P(None, 'dp', 'head')
- out_update: float32 [768, 768], P('head', 'dp')
- up_update: float32 [768, 3072], P('dp', 'head')
- down_update: float32 [3072, 768], P('head', 'dp')
- bias_update: float32 [2, 2304], P('head')
- shared_update: float32 [16, 768], replicated
- qkv_moment: float32 [3, 768, 768], P(None, 'dp', 'head')
- out_moment: float32 [768, 768], P('head', 'dp')
- up_moment: float32 [768, 3072], P('dp', 'head')
- down_moment: float32 [3072, 768], P('head', 'dp')
- bias_moment: float32 [2, 2304], P('head')
- shared_moment: float32 [16, 768], replicated
- qkv_square: float32 [3, 768, 768], P(None, 'dp', 'head')
- out_square: float32 [768, 768], P('head', 'dp')
- up_square: float32 [768, 3072], P('dp', 'head')
- down_square: float32 [3072, 768], P('head', 'dp')
- bias_square: float32 [2, 2304], P('head')
- shared_square: float32 [16, 768], replicated
Inputs may be any that keep to these rules, and one draw needn't show every extreme that they name: `seg_counts`: a chain's slots 0 to its count minus 1 are live.
All inputs are finite; a program needn't handle non-finite values.
Results may differ from a plain program's by a relative error of at most 0.02.
The roundings to bfloat16 on the way count: a program that leaves them out, or rounds other values in their place, can miss the bound.
Values may be sent and summed in bfloat16 or wider, within the bound.
No kernel may reach another device: no remote copies, remote signals or barrier semaphores. Data moves between devices by JAX's collectives and lax.ppermute only.
A program may use at most 192 MiB of HBM per device.

v0:
```python
import functools
import math

import jax
import jax.numpy as jnp
from jax import lax
from jax.experimental import pallas as pl
from jax.experimental.pallas import tpu as pltpu
from jax.sharding import PartitionSpec as P

HD = 64
STEP = 10
EPSILON = 1e-06
BETA_ONE = 0.9
BETA_TWO = 0.999
LEARN_RATE = 0.1
VECTOR_RATE = 0.6
DECAY_RATE = 0.01
ADAM_EPSILON = 1e-08
CLIP_NORM = 1.0

BF = jnp.bfloat16
F32 = jnp.float32
LOG2E = math.log2(math.e)
NEG = -1e30
SLOTS = 16
PAD = 16
USED = 10
WIDE = 384
CHUNK = 256
LOW, CTX, H_LOW, ACTIVE, DF_LOW, DU, DA, DQKV = range(8)


def dot_nn(a, b):
    return lax.dot_general(a, b, (((1,), (0,)), ((), ())), preferred_element_type=F32)


def dot_nt(a, b):
    return lax.dot_general(a, b, (((1,), (1,)), ((), ())), preferred_element_type=F32)


def dot_tn(a, b):
    return lax.dot_general(a, b, (((0,), (0,)), ((), ())), preferred_element_type=F32)


def norm_stats(values):
    average = jnp.mean(values, axis=-1, keepdims=True)
    centered = values - average
    variance = jnp.mean(centered * centered, axis=-1, keepdims=True)
    scale = lax.rsqrt(variance + EPSILON)
    return centered * scale, scale


def norm_back(grad, gain, unit, scale):
    inner = grad * gain
    mean_one = jnp.mean(inner, axis=-1, keepdims=True)
    mean_two = jnp.mean(inner * unit, axis=-1, keepdims=True)
    return scale * (inner - mean_one - unit * mean_two)


def row_sum(values):
    return jnp.sum(values, axis=0, keepdims=True)


def call(kernel, outs, args, scalars=0, scratch=()):
    return pl.pallas_call(
        kernel,
        out_shape=[jax.ShapeDtypeStruct(s, d) for s, d in outs],
        in_specs=[pl.BlockSpec(memory_space=pltpu.SMEM)] * scalars
        + [pl.BlockSpec(memory_space=pltpu.VMEM)] * (len(args) - scalars),
        out_specs=[pl.BlockSpec(memory_space=pltpu.VMEM)] * len(outs),
        scratch_shapes=list(scratch),
        cost_estimate=pl.CostEstimate(flops=0, bytes_accessed=0, transcendentals=0),
        compiler_params=pltpu.CompilerParams(vmem_limit_bytes=16 << 20),
    )(*args)


def slot_of(kind, number):
    if kind[0] == "z":
        outer, mid, z = number // 8, number // 4 % 2, number % 4
        return (outer + 2 * mid if kind[1] == "a" else 2 * outer + mid) + 4 * z
    outer, z, inner = number // 8, number // 2 % 4, number % 2
    return (2 * outer + inner if kind[1] == "a" else outer + 2 * inner) + 4 * z


def assemble_kernel(kinds, counts, joined, me_ref, *refs):
    at = sum(counts)
    begin = 0
    for part, (kind, count) in enumerate(zip(kinds, counts)):
        target = refs[at] if joined else refs[at + part]
        block = target.shape[0] // SLOTS
        number = 0
        for source in refs[begin : begin + count]:
            length = source.shape[2]
            column = part * length if joined else 0
            for inner in range(source.shape[0]):
                place = lax.bitwise_xor(me_ref[0], slot_of(kind, number))
                start = pl.multiple_of(place * block, block)
                target[pl.ds(start, block), column : column + length] = source[inner]
                number += 1
        begin += count


def attn_rows(low_ref, qk_ref, vo_ref, bias_ref, part_ref, qkv_ref, lse_ref, ctx_ref):
    rows = low_ref.shape[0]
    width = vo_ref.shape[1] // 2
    seg = rows - 2 * PAD
    low = low_ref[...]
    qk = dot_nn(low, qk_ref[...])
    qkv_ref[:, :width] = (qk[:, :width] + bias_ref[:, :width]).astype(BF)
    qkv_ref[:, width : 2 * width] = qk[:, width:].astype(BF)
    v_all = dot_nn(low, vo_ref[:, :width])
    qkv_ref[:, 2 * width :] = (v_all + bias_ref[:, width : 2 * width]).astype(BF)
    key_at = lax.broadcasted_iota(jnp.int32, (1, rows), 1)
    dead = (key_at >= seg) & (((key_at - seg) & (PAD - 1)) >= USED)
    lane = lax.broadcasted_iota(jnp.int32, (rows, 128), 1)
    lse_ref[...] = jnp.zeros_like(lse_ref)

    def heads(pair, carry):
        at = pl.multiple_of(pair * 128, 128)
        q = qkv_ref[:, pl.ds(at, 128)]
        k = qkv_ref[:, pl.ds(width + at, 128)]
        v = qkv_ref[:, pl.ds(2 * width + at, 128)]
        outs = []
        for head in range(2):
            mine = (lane < 64) if head == 0 else (lane >= 64)
            s = dot_nt(jnp.where(mine, q, jnp.zeros_like(q)), k) * (HD**-0.5 * LOG2E)
            s = jnp.where(dead, NEG, s)
            top = jnp.max(s, axis=1, keepdims=True)
            e = jnp.exp2(s - top)
            total = jnp.sum(e, axis=1, keepdims=True)
            p = (e * (1.0 / total)).astype(BF)
            outs.append(dot_nn(p, v))
            lse_ref[...] = jnp.where(lane == 2 * pair + head, top + jnp.log2(total), lse_ref[...])
        ctx_ref[:, pl.ds(at, 128)] = jnp.where(lane < 64, outs[0], outs[1]).astype(BF)
        return carry

    lax.fori_loop(0, width // 128, heads, 0)
    part_ref[...] = dot_nt(ctx_ref[...], vo_ref[:, width:]).astype(BF)


def attn_forward_kernel(token_ref, mem_ref, qk_ref, vo_ref, bias_ref, part_ref, low_ref, qkv_ref, lse_ref, ctx_ref):
    seg = token_ref.shape[0]
    memory = mem_ref[...].astype(BF)
    low_ref[:seg, :] = token_ref[...]
    low_ref[seg : seg + PAD, :] = memory
    low_ref[seg + PAD :, :] = memory
    attn_rows(low_ref, qk_ref, vo_ref, bias_ref, part_ref, qkv_ref, lse_ref, ctx_ref)


def close_rows(first_ref, own_ref, other_ref, shared_ref):
    unit, unused = norm_stats(first_ref[...])
    hidden = unit * shared_ref[USED + 2 : USED + 3, :] + shared_ref[USED + 3 : USED + 4, :]
    return hidden + (own_ref[...].astype(F32) + other_ref[...].astype(F32)) + shared_ref[USED + 1 : USED + 2, :]


def attn_next_kernel(first_ref, own_ref, other_ref, shared_ref, alive_ref, keep_ref, token_ref, qk_ref, vo_ref, bias_ref,
                     out_ref, mem_ref, second_ref, part_ref, low_ref, qkv_ref, lse_ref, ctx_ref):
    seg = token_ref.shape[0]
    second = close_rows(first_ref, own_ref, other_ref, shared_ref)
    second_ref[...] = second
    unit, unused = norm_stats(second)
    result = unit * shared_ref[USED + 4 : USED + 5, :] + shared_ref[USED + 5 : USED + 6, :]
    out_ref[...] = (result[:seg] * alive_ref[...]).astype(BF)
    row = lax.broadcasted_iota(jnp.int32, mem_ref.shape, 0)
    fresh = jnp.where(row < USED, result[seg + PAD :], 0.0)
    memory = jnp.where(alive_ref[...] > 0.0, fresh, keep_ref[...])
    mem_ref[...] = memory
    low_ref[:seg, :] = token_ref[...]
    low_ref[seg : seg + PAD, :] = memory.astype(BF)
    low_ref[seg + PAD :, :] = memory.astype(BF)
    attn_rows(low_ref, qk_ref, vo_ref, bias_ref, part_ref, qkv_ref, lse_ref, ctx_ref)


def ffn_forward_kernel(token_ref, mem_ref, own_ref, other_ref, up_ref, down_ref, bias_ref, shared_ref,
                       part_ref, first_ref, low_ref, act_ref, slope_ref, total_ref):
    seg = token_ref.shape[0]
    hidden_units = up_ref.shape[1]
    begin = bias_ref.shape[1] - hidden_units
    attn = own_ref[...].astype(F32) + other_ref[...].astype(F32) + shared_ref[USED : USED + 1, :]
    first_ref[:seg, :] = token_ref[...].astype(F32) + attn[:seg]
    first_ref[seg : seg + PAD, :] = mem_ref[...] + attn[seg : seg + PAD]
    first_ref[seg + PAD :, :] = mem_ref[...] + attn[seg + PAD :]
    unit, unused = norm_stats(first_ref[...])
    hidden = unit * shared_ref[USED + 2 : USED + 3, :] + shared_ref[USED + 3 : USED + 4, :]
    low_ref[...] = hidden.astype(BF)
    total_ref[...] = jnp.zeros_like(total_ref)

    def units(step, carry):
        for piece in range(2):
            at = pl.multiple_of(step * (2 * WIDE) + piece * WIDE, 128)
            u = dot_nn(low_ref[...], up_ref[:, pl.ds(at, WIDE)]) + bias_ref[:, pl.ds(begin + at, WIDE)]
            cdf = 0.5 + 0.5 * lax.erf(u * (0.5**0.5))
            density = jnp.exp2(u * u * (-0.5 * LOG2E)) * ((2.0 * math.pi) ** -0.5)
            active = (u * cdf).astype(BF)
            act_ref[:, pl.ds(at, WIDE)] = active
            slope_ref[:, pl.ds(at, WIDE)] = (cdf + u * density).astype(BF)
            total_ref[...] += dot_nt(active, down_ref[:, pl.ds(at, WIDE)])
        return carry

    lax.fori_loop(0, hidden_units // (2 * WIDE), units, 0)
    part_ref[...] = total_ref[...].astype(BF)


def ffn_backward_rows(second, dmem, cot_ref, alive_ref, shared_ref, up_ref, down_ref, slope_ref,
                      part_ref, dsecond_ref, dlow_ref, du_ref, dbias_ref, dvec_ref, total_ref):
    unit, scale = norm_stats(second)
    dy = jnp.concatenate(
        [cot_ref[...].astype(F32) * alive_ref[...], jnp.zeros((PAD, unit.shape[1]), F32), dmem * alive_ref[...]], axis=0
    )
    dsecond = norm_back(dy, shared_ref[USED + 4 : USED + 5, :], unit, scale)
    dsecond_ref[...] = dsecond
    dvec_ref[0:1, :] = row_sum(dsecond)
    dvec_ref[1:2, :] = row_sum(dy * unit)
    dvec_ref[2:3, :] = row_sum(dy)
    dvec_ref[3:, :] = jnp.zeros((dvec_ref.shape[0] - 3, unit.shape[1]), F32)
    dlow_ref[...] = dsecond.astype(BF)
    total_ref[...] = jnp.zeros_like(total_ref)

    def units(step, carry):
        for piece in range(2):
            at = pl.multiple_of(step * (2 * WIDE) + piece * WIDE, 128)
            du = dot_nn(dlow_ref[...], down_ref[:, pl.ds(at, WIDE)]) * slope_ref[:, pl.ds(at, WIDE)].astype(F32)
            dbias_ref[:, pl.ds(at, WIDE)] = row_sum(du)
            du_low = du.astype(BF)
            du_ref[:, pl.ds(at, WIDE)] = du_low
            total_ref[...] += dot_nt(du_low, up_ref[:, pl.ds(at, WIDE)])
        return carry

    lax.fori_loop(0, up_ref.shape[1] // (2 * WIDE), units, 0)
    part_ref[...] = total_ref[...].astype(BF)


def ffn_last_kernel(first_ref, own_ref, other_ref, cot_ref, dmem_ref, alive_ref, shared_ref, up_ref, down_ref, slope_ref,
                    out_ref, *outs):
    second = close_rows(first_ref, own_ref, other_ref, shared_ref)
    unit, unused = norm_stats(second)
    result = unit * shared_ref[USED + 4 : USED + 5, :] + shared_ref[USED + 5 : USED + 6, :]
    out_ref[...] = (result[: out_ref.shape[0]] * alive_ref[...]).astype(BF)
    ffn_backward_rows(second, dmem_ref[...], cot_ref, alive_ref, shared_ref, up_ref, down_ref, slope_ref, *outs)


def input_rows(dfirst_ref, own_ref, other_ref, grad_ref, live, keep):
    seg = grad_ref.shape[0]
    dx = dfirst_ref[...] + (own_ref[...].astype(F32) + other_ref[...].astype(F32))
    grad_ref[...] = (dx[:seg] * live).astype(BF)
    return jnp.where(live > 0.0, dx[seg : seg + PAD] + dx[seg + PAD :], keep)


def ffn_before_kernel(dfirst_ref, own_ref, other_ref, live_ref, keep_ref, second_ref, cot_ref, alive_ref, shared_ref, up_ref, down_ref,
                      slope_ref, grad_ref, dmem_ref, *outs):
    dmem = input_rows(dfirst_ref, own_ref, other_ref, grad_ref, live_ref[...], keep_ref[...])
    dmem_ref[...] = dmem
    ffn_backward_rows(second_ref[...], dmem, cot_ref, alive_ref, shared_ref, up_ref, down_ref, slope_ref, *outs)


def input_grad_kernel(dfirst_ref, own_ref, other_ref, live_ref, keep_ref, grad_ref, dmem_ref):
    dmem_ref[...] = input_rows(dfirst_ref, own_ref, other_ref, grad_ref, live_ref[...], keep_ref[...])


def attn_backward_kernel(dsecond_ref, own_ref, other_ref, first_ref, shared_ref, qk_ref, vo_ref, qkv_ref, lse_ref,
                         part_ref, dfirst_ref, da_ref, dqkv_ref, dhead_ref, dvec_ref, dctx_ref, lse_t_ref):
    rows = first_ref.shape[0]
    width = vo_ref.shape[1] // 2
    seg = rows - 2 * PAD
    dhidden = dsecond_ref[...] + (own_ref[...].astype(F32) + other_ref[...].astype(F32))
    unit, scale = norm_stats(first_ref[...])
    dfirst = norm_back(dhidden, shared_ref[USED + 2 : USED + 3, :], unit, scale)
    dfirst_ref[...] = dfirst
    dvec_ref[0:1, :] = row_sum(dfirst)
    dvec_ref[1:2, :] = row_sum(dhidden * unit)
    dvec_ref[2:3, :] = row_sum(dhidden)
    dvec_ref[3:, :] = jnp.zeros((dvec_ref.shape[0] - 3, unit.shape[1]), F32)
    da_ref[...] = dfirst.astype(BF)
    dctx_ref[...] = dot_nn(da_ref[...], vo_ref[:, width:]).astype(BF)
    lse_t_ref[...] = jnp.transpose(lse_ref[...])
    key_at = lax.broadcasted_iota(jnp.int32, (rows, 1), 0)
    dead = (key_at >= seg) & (((key_at - seg) & (PAD - 1)) >= USED)
    lane = lax.broadcasted_iota(jnp.int32, (rows, 128), 1)
    sub = lax.broadcasted_iota(jnp.int32, (128, rows), 0)

    def heads(pair, carry):
        at = pl.multiple_of(pair * 128, 128)
        q = qkv_ref[:, pl.ds(at, 128)]
        k = qkv_ref[:, pl.ds(width + at, 128)]
        v = qkv_ref[:, pl.ds(2 * width + at, 128)]
        dc = dctx_ref[:, pl.ds(at, 128)]
        dq_t, dk, dv = [], None, None
        for head in range(2):
            mine = (lane < 64) if head == 0 else (lane >= 64)
            q_one = jnp.where(mine, q, jnp.zeros_like(q))
            dc_one = jnp.where(mine, dc, jnp.zeros_like(dc))
            s_t = dot_nt(k, q_one) * (HD**-0.5 * LOG2E)
            lse_row = lse_t_ref[pl.ds(2 * pair + head, 1), :]
            p_t = jnp.where(dead, 0.0, jnp.exp2(s_t - lse_row))
            dp_t = dot_nt(v, dc_one)
            dv_one = dot_nn(p_t.astype(BF), dc_one)
            inner = row_sum(p_t * dp_t)
            ds_t = (p_t * (dp_t - inner)).astype(BF)
            dk_one = dot_nn(ds_t, q_one)
            dq_t.append(dot_tn(k, ds_t))
            dv = dv_one if dv is None else dv + dv_one
            dk = dk_one if dk is None else dk + dk_one
        dq = jnp.transpose(jnp.where(sub < 64, dq_t[0], dq_t[1])) * (HD**-0.5)
        dk = dk * (HD**-0.5)
        dhead_ref[:, pl.ds(at, 128)] = row_sum(dq)
        dhead_ref[:, pl.ds(width + at, 128)] = row_sum(dv)
        dqkv_ref[:, pl.ds(at, 128)] = dq.astype(BF)
        dqkv_ref[:, pl.ds(width + at, 128)] = dk.astype(BF)
        dqkv_ref[:, pl.ds(2 * width + at, 128)] = dv.astype(BF)
        return carry

    lax.fori_loop(0, width // 128, heads, 0)
    part = dot_nt(dqkv_ref[:, : 2 * width], qk_ref[...]) + dot_nt(dqkv_ref[:, 2 * width :], vo_ref[:, :width])
    part_ref[...] = part.astype(BF)


def grad_close_kernel(lines, *refs):
    count = 3 * lines
    outs = refs[-4:]
    squares = None
    for matrix in range(3):
        total = refs[matrix * lines][...].astype(F32)
        for other in refs[matrix * lines + 1 : (matrix + 1) * lines]:
            total = total + other[...].astype(F32)
        outs[matrix][...] = total
        square = jnp.sum(total * total, keepdims=True)
        squares = square if squares is None else squares + square
    dmem_ref = refs[count]
    dvec_one, dvec_two, dhead, dbias = (refs[count + 1 + i : -4 : 4] for i in range(4))
    small = outs[3]
    model = small.shape[1]

    def total_of(group, row):
        total = group[0][row : row + 1, :]
        for ref in group[1:]:
            total = total + ref[row : row + 1, :]
        return total

    small[:PAD, :] = dmem_ref[...]
    for place, (group, row) in enumerate(((dvec_one, 0), (dvec_two, 0), (dvec_one, 1), (dvec_one, 2), (dvec_two, 1), (dvec_two, 2))):
        small[USED + place : USED + place + 1, :] = total_of(group, row)
    at = USED + 6
    for group in (dhead, dbias):
        whole = total_of(group, 0)
        for piece in range(whole.shape[1] // model):
            small[at : at + 1, :] = whole[:, piece * model : (piece + 1) * model]
            at += 1
    small[at:, :] = jnp.broadcast_to(squares, (small.shape[0] - at, model))


def adam_kernel(plan, small_ref, own_ref, other_ref, *refs):
    count = len(plan)
    grads = refs[:3]
    olds, news = refs[3 : 3 + 3 * count], refs[4 + 3 * count :]
    norm_ref = refs[3 + 3 * count]
    shared = small_ref[: USED + 6, :]
    norm = jnp.sqrt((own_ref[:1, :1] + other_ref[:1, :1]) + jnp.sum(shared * shared, keepdims=True))
    norm_ref[...] = norm
    factor = CLIP_NORM / jnp.maximum(norm, CLIP_NORM)
    for number, (source, row, column, rate, decay) in enumerate(plan):
        weight_ref, first_ref, second_ref = olds[3 * number : 3 * number + 3]
        height, length = weight_ref.shape[-2:]
        for index in range(math.prod(weight_ref.shape[:-2])):
            here = (index,) if weight_ref.ndim == 3 else ()
            if source is None and height == 1:
                model = small_ref.shape[1]
                gradient = jnp.concatenate([small_ref[row + i : row + i + 1, :] for i in range(length // model)], axis=1)
            elif source is None:
                gradient = small_ref[row : row + height, :]
            else:
                gradient = grads[source][:, column + index * length : column + (index + 1) * length]
            clipped = gradient * factor
            first = BETA_ONE * first_ref[here + (...,)] + (1.0 - BETA_ONE) * clipped
            second = BETA_TWO * second_ref[here + (...,)] + (1.0 - BETA_TWO) * clipped * clipped
            first_hat = first / (1.0 - BETA_ONE**STEP)
            second_hat = second / (1.0 - BETA_TWO**STEP)
            weight = weight_ref[here + (...,)]
            news[3 * number][here + (...,)] = weight - rate * (first_hat / (jnp.sqrt(second_hat) + ADAM_EPSILON) + decay * weight)
            news[3 * number + 1][here + (...,)] = first
            news[3 * number + 2][here + (...,)] = second


def weight_grad_kernel(plan, kinds, sizes, me_ref, *refs):
    count = len(kinds) * len(sizes)
    outs = refs[-count - 1 : -1]
    total_ref = refs[-1]
    block = total_ref.shape[0] // SLOTS
    for part, (kind, pieces) in enumerate(zip(kinds, plan)):
        at = 0
        for left, right, start, size in pieces:

            def rows_of(step, carry, left=left, right=right, start=start, size=size, at=at):
                begin = pl.multiple_of(step * CHUNK, CHUNK)
                total = None
                for one, two in zip(left, right):
                    add = dot_tn(refs[one][:, pl.ds(begin, CHUNK)], refs[two][:, start : start + size])
                    total = add if total is None else total + add
                total_ref[pl.ds(begin, CHUNK), at : at + size] = total
                return carry

            lax.fori_loop(0, total_ref.shape[0] // CHUNK, rows_of, 0)
            at += size
        number = 0
        for target in outs[part * len(sizes) : (part + 1) * len(sizes)]:
            for inner in range(target.shape[0]):
                place = lax.bitwise_xor(me_ref[0], slot_of(kind, number))
                begin = pl.multiple_of(place * block, block)
                target[inner] = total_ref[pl.ds(begin, block), :].astype(BF)
                number += 1


def exchange(values, axis, size, flip):
    return lax.ppermute(values, axis, [(i, i ^ flip) for i in range(size)])


def after(value, *others):
    return lax.optimization_barrier((value, *others))[0]


def add_low(*values):
    total = values[0].astype(F32)
    for value in values[1:]:
        total = total + value.astype(F32)
    return total


def canonical_split(full, kind, sizes):
    full = full.reshape(SLOTS, full.shape[0] // SLOTS, full.shape[1])
    full = jnp.stack([full[slot_of(kind, number)] for number in range(SLOTS)])
    ends = [sum(sizes[: i + 1]) for i in range(len(sizes))]
    return [full[end - size : end] for end, size in zip(ends, sizes)]


def canonical_join(pieces, kind):
    full = jnp.concatenate(pieces)
    order = [slot_of(kind, number) for number in range(SLOTS)]
    full = jnp.stack([full[order.index(d)] for d in range(SLOTS)])
    return full.reshape(-1, full.shape[-1])


def line_stage(own, size):
    return [own] + [exchange(own, "dp", size, 4 * j) for j in (1, 2, 3)]


def sum_all(values, axis, size):
    if size & (size - 1):
        return lax.psum(values, axis)
    flip = 1
    while flip < size:
        if flip * 4 <= size:
            near, far, both = [exchange(values, axis, size, flip * j) for j in (1, 2, 3)]
            values = (values + near) + (far + both)
            flip *= 4
        else:
            values = values + exchange(values, axis, size, flip)
            flip *= 2
    return values


def shards(
    size,
    pair,
    inputs,
    cotangent,
    seg_counts,
    qkv_weight,
    out_weight,
    up_weight,
    down_weight,
    head_bias,
    shared_params,
    qkv_first,
    out_first,
    up_first,
    down_first,
    bias_first,
    shared_first,
    qkv_second,
    out_second,
    up_second,
    down_second,
    bias_second,
    shared_second,
):
    unused, segments, seg, model = inputs.shape
    width = qkv_weight.shape[2]
    hidden = up_weight.shape[1]
    used = shared_params.shape[0] - 6
    pad = 16
    rows = seg + 2 * pad
    half = hidden // 2

    me = (lax.axis_index("dp") if size == SLOTS else jnp.int32(0)).astype(jnp.int32).reshape(1)
    qkv_low = qkv_weight.astype(BF)
    out_low = out_weight.T.astype(BF)
    up_low = up_weight.astype(BF)
    down_low = down_weight.T.astype(BF)
    own = [
        jnp.stack([jnp.concatenate([qkv_low[0], qkv_low[1]], axis=1), jnp.concatenate([qkv_low[2], out_low], axis=1)]),
        jnp.stack([up_low[:, :half], up_low[:, half:]]),
        jnp.stack([down_low[:, :half], down_low[:, half:]]),
    ]

    def assembled(kinds, pieces, joined):
        return call(
            functools.partial(assemble_kernel, kinds, [len(p) for p in pieces], joined),
            [((model, 2 * model), BF)] if joined else [((model, model), BF)] * 2,
            [me, *pieces[0], *pieces[1]],
            scalars=1,
        )

    z_first, z_mid = ("za", "zb"), ("xa", "xb")
    if size == SLOTS:

        def spread(lines):
            low_a = jnp.concatenate([lines[0], exchange(lines[0], "dp", size, 2)])
            low_b = jnp.concatenate([lines[1], exchange(lines[1], "dp", size, 1)])
            return low_a, low_b

        def finish(low_a, low_b):
            return exchange(low_a, "dp", size, 1), exchange(low_b, "dp", size, 2)

        pair_c = [jnp.stack([own[2][i], exchange(own[2][i], "dp", size, 1 + i)]) for i in range(2)]
        line_one = line_stage(own[0], size)
        line_two = line_stage(after(own[1], *line_one), size)
        low_one = spread([jnp.stack([v[i] for v in line_one]) for i in range(2)])
        line_three = line_stage(after(jnp.stack(pair_c), *line_two, *low_one), size)
        high_one = finish(*low_one)
        low_two = spread([after(jnp.stack([v[i] for v in line_two]), *high_one) for i in range(2)])
        high_two = finish(*low_two)
        low_c = [jnp.concatenate([v[i] for v in line_three]) for i in range(2)]
        low_c = [after(v, *high_two) for v in low_c]
        high_c = [exchange(low_c[i], "dp", size, 2 - i) for i in range(2)]
        high_one = [after(h, *low_two) for h in high_one]
        w_qk, w_vo = assembled(z_first, [[low_one[i], high_one[i]] for i in range(2)], False)
        (w_up,) = assembled(z_first, [[low_two[i], high_two[i]] for i in range(2)], True)
        (w_down,) = assembled(z_mid, [[low_c[i], high_c[i]] for i in range(2)], True)
    else:

        def whole(number, kinds, sizes):
            pieces = [lax.all_gather(own[number][i], "dp", axis=0, tiled=True) for i in range(2)]
            return assembled(kinds, [canonical_split(p, kind, sizes) for p, kind in zip(pieces, kinds)], number > 0)

        w_qk, w_vo = whole(0, z_first, (8, 8))
        (w_up,) = whole(1, z_first, (8, 8))
        (w_down,) = whole(2, z_mid, (8, 8))

    memory = jnp.concatenate([shared_params[:used], jnp.zeros((pad - used, model), F32)], axis=0)
    alive = [(slot < seg_counts).astype(F32).reshape(1, 1) for slot in range(segments)]
    memories, tokens_out, saved = [memory], [], []
    attn_outs = [((rows, model), BF), ((rows, model), BF), ((rows, 3 * width), BF), ((rows, 128), F32), ((rows, width), BF)]
    for slot in range(segments):
        tokens = inputs[0, slot]
        if slot == 0:
            part, *attn = call(attn_forward_kernel, attn_outs, [tokens, memory, w_qk, w_vo, head_bias])
        else:
            out_rows, memory, second_in, part, *attn = call(
                attn_next_kernel,
                [((seg, model), BF), ((pad, model), F32), ((rows, model), F32)] + attn_outs,
                [saved[-1][4], ffn_part, other, shared_params, alive[slot - 1], memory, tokens, w_qk, w_vo, head_bias],
            )
            tokens_out.append(out_rows)
            saved[-1] += (second_in,)
        other = exchange(part, "head", pair, 1)
        ffn_part, first_in, h_low, active, slope = call(
            ffn_forward_kernel,
            [((rows, model), BF), ((rows, model), F32), ((rows, model), BF), ((rows, hidden), BF), ((rows, hidden), BF)],
            [tokens, memory, part, other, w_up, w_down, head_bias, shared_params],
            scratch=[pltpu.VMEM((rows, model), F32)],
        )
        other = exchange(ffn_part, "head", pair, 1)
        saved.append((*attn, first_in, h_low, active, slope))

    count = segments

    def weight_grad(names, plan, kinds):
        sizes = (8, 8)
        operands = [stacks[s][n] for n in names for s in range(count)]
        at = {n: [i * count + s for s in range(count)] for i, n in enumerate(names)}
        steps = [[(at[a], at[b], start, length) for a, b, start, length in pieces] for pieces in plan]
        result = call(
            functools.partial(weight_grad_kernel, steps, kinds, sizes),
            [((length, model // SLOTS, model), BF) for kind in kinds for length in sizes],
            [me, *operands],
            scalars=1,
            scratch=[pltpu.VMEM((model, model), F32)],
        )
        return result[: len(sizes)], result[len(sizes) :]

    dmem = jnp.zeros((pad, model), F32)
    grads = [None] * segments
    stacks = [None] * segments
    smalls = []
    ffn_outs = [((rows, model), BF), ((rows, model), F32), ((rows, model), BF), ((rows, hidden), BF), ((1, hidden), F32), ((8, model), F32)]
    for slot in reversed(range(segments)):
        low, qkv, lse, ctx, first_in, h_low, active, slope = saved[slot][:8]
        weights = [alive[slot], shared_params, w_up, w_down, slope]
        scratch = [pltpu.VMEM((rows, model), F32)]
        if slot == segments - 1:
            out_rows, part, dsecond, df_low, du, dbias, dvec_two = call(
                ffn_last_kernel,
                [((seg, model), BF)] + ffn_outs,
                [first_in, ffn_part, other, cotangent[0, slot], dmem, *weights],
                scratch=scratch,
            )
            tokens_out.append(out_rows)
        else:
            grads[slot + 1], dmem, part, dsecond, df_low, du, dbias, dvec_two = call(
                ffn_before_kernel,
                [((seg, model), BF), ((pad, model), F32)] + ffn_outs,
                [dfirst, part, other, alive[slot + 1], dmem, saved[slot][8], cotangent[0, slot], *weights],
                scratch=scratch,
            )
        other = exchange(part, "head", pair, 1)
        stacks[slot] = (low, ctx, h_low, active, df_low, du)
        if slot == 0:
            dw_down = weight_grad((DF_LOW, ACTIVE), [[(DF_LOW, ACTIVE, 0, half)], [(DF_LOW, ACTIVE, half, half)]], z_first)
            dw_up = weight_grad((H_LOW, DU), [[(H_LOW, DU, 0, half)], [(H_LOW, DU, half, half)]], z_first)
            dsecond = after(dsecond, dw_down[0][0], dw_up[0][0])
        part, dfirst, da, dqkv, dhead, dvec_one = call(
            attn_backward_kernel,
            [((rows, model), BF), ((rows, model), F32), ((rows, model), BF), ((rows, 3 * width), BF), ((1, 2 * width), F32), ((8, model), F32)],
            [dsecond, part, other, first_in, shared_params, w_qk, w_vo, qkv, lse],
            scratch=[pltpu.VMEM((rows, width), BF), pltpu.VMEM((128, rows), F32)],
        )
        other = exchange(part, "head", pair, 1)
        stacks[slot] += (da, dqkv)
        smalls += [dvec_one, dvec_two, dhead, dbias]
    grads[0], dmem = call(
        input_grad_kernel,
        [((seg, model), BF), ((pad, model), F32)],
        [dfirst, part, other, alive[0], dmem],
    )
    outputs = jnp.stack(tokens_out)[None]
    input_grad = jnp.stack(grads)[None]

    def fallback(parts, kinds):
        full = [canonical_join(p, kind) for p, kind in zip(parts, kinds)]
        full = jnp.concatenate(full, axis=1)
        return lax.psum_scatter(full, "dp", scatter_dimension=0, tiled=True).astype(F32)

    def hop(blocks, flips):
        return [exchange(block, "dp", size, flip) for block, flip in zip(blocks, flips)]

    def add_halves(keep, got):
        return [add_low(k, g).astype(BF) for k, g in zip(keep, got)]

    def line_hop(four):
        return [exchange(four[j], "dp", size, 4 * j) for j in (1, 2, 3)]

    x_first, y_first = (1, 2), (2, 1)
    if size == SLOTS:
        got_down, got_up = hop([p[1] for p in dw_down], x_first), hop([p[1] for p in dw_up], x_first)
        stacks[0] = stacks[0][:DQKV] + (after(stacks[0][DQKV], *got_down),)
    dw_qkvo = weight_grad(
        (LOW, DQKV, DA, CTX),
        [[(LOW, DQKV, 0, 2 * width)], [(LOW, DQKV, 2 * width, width), (DA, CTX, 0, width)]],
        z_first,
    )
    if size == SLOTS:
        dw_qkvo = [[after(v, *got_up) for v in part] for part in dw_qkvo]
        got_qkvo = hop([p[1] for p in dw_qkvo], x_first)
        keep = [jnp.stack([dw_down[i][0], dw_up[i][0]], axis=1) for i in range(2)]
        got = [jnp.stack([after(got_down[i], dw_qkvo[0][0]), got_up[i]], axis=1) for i in range(2)]
        both = add_halves(keep, got)
        got = hop([v[4:] for v in both], y_first)
        both = add_halves([v[:4] for v in both], [after(g, *got_qkvo) for g in got])
        last = add_halves([p[0] for p in dw_qkvo], got_qkvo)
        last = add_halves([v[:4] for v in last], hop([v[4:] for v in last], y_first))
        both = jnp.concatenate(both, axis=3)
        got = line_hop(both)
        last = jnp.concatenate(last, axis=2)
        sums = [[both[0, i], *[g[i] for g in got]] for i in range(2)]
        sums.append([last[0], *line_hop(last)])
    else:
        sums = [[fallback(p, z_first)] for p in (dw_down, dw_up, dw_qkvo)]
    height, wide = sums[0][0].shape
    *matrices, small = call(
        functools.partial(grad_close_kernel, len(sums[0])),
        [((height, wide), F32)] * 3 + [((24, model), F32)],
        [*sums[0], *sums[1], *sums[2], dmem, *smalls],
    )
    small = sum_all(small, "dp", size)
    bias_grad = small[used + 6 : used + 9]
    squares = jnp.full((8, 128), small[used + 9, 0] + jnp.sum(bias_grad * bias_grad))
    other = exchange(squares, "head", pair, 1)
    plan = (
        (2, 0, 0, LEARN_RATE, DECAY_RATE),
        (2, 0, 3 * width, LEARN_RATE, DECAY_RATE),
        (1, 0, 0, LEARN_RATE, DECAY_RATE),
        (0, 0, 0, LEARN_RATE, DECAY_RATE),
        (None, used + 6, 0, VECTOR_RATE, 0.0),
        (None, 0, 0, VECTOR_RATE, 0.0),
    )
    olds = (
        (qkv_weight, qkv_first, qkv_second),
        (out_weight.T, out_first.T, out_second.T),
        (up_weight, up_first, up_second),
        (down_weight.T, down_first.T, down_second.T),
        (head_bias, bias_first, bias_second),
        (shared_params, shared_first, shared_second),
    )
    grad_norm, *news = call(
        functools.partial(adam_kernel, plan),
        [((1, 1), F32)] + [(o.shape, F32) for old in olds for o in old],
        [small, squares, other, *matrices, *[o for old in olds for o in old]],
    )
    results = [news[3 * i : 3 * i + 3] for i in range(6)]
    for number in (1, 3):
        results[number] = [r.T for r in results[number]]
    return (outputs, input_grad, grad_norm[0, 0]) + tuple(r[i] for i in range(3) for r in results)


def solution(mesh):
    weights = (P(None, "dp", "head"), P("head", "dp"), P("dp", "head"), P("head", "dp"), P("head", None), P())
    rows = P("dp", None, None, None)
    return jax.shard_map(
        functools.partial(shards, mesh.shape["dp"], mesh.shape["head"]),
        mesh=mesh,
        in_specs=(rows, rows, P("dp")) + weights * 3,
        out_specs=(rows, rows, P()) + weights * 3,
        check_vma=False,
    )
```

profile of v0, /device:TPU:0, one launch (start us, length us, event | category | flops | bytes accessed | tf_op | source)
XLA Modules:
  0.0 274.0 jit_solution(945060988835150648)
XLA Ops:
  3.3 5.0 %collective-permute-start.2 = (bf16[2,48,768]{2,1,0:T(8,128)(2,1)}, bf16[2,48,768]{2,1,0:T(8,128)(2,1)}, u32[]{:S(2)}, u32[]{:S(2)}) collective-permute-start(bf16[2,48,768]{2,1,0:T(8,128)(2,1)} %pad_maximum_fusion.9), channel_id=1, source_target_pairs={{0,24},{2,26},{4,28},{6,30},{8,16},{10,18},{12,20},{14,22},{16,8},... | collective-permute-start | bytes 442376 | tf_op jit(solution)/shard_map/ppermute | solution.py:414
  9.7 1.7 collective-permute-start.16
  17.1 4.1 %collective-permute-done.1 = bf16[2,48,768]{2,1,0:T(8,128)(2,1)} collective-permute-done((bf16[2,48,768]{2,1,0:T(8,128)(2,1)}, bf16[2,48,768]{2,1,0:T(8,128)(2,1)}, u32[]{:S(2)}, u32[]{:S(2)}) %collective-permute-start.1) | collective-permute-done | bytes 147488 | tf_op jit(solution)/shard_map/ppermute | solution.py:414
  21.2 2.7 collective-permute-start.7
  23.8 1.7 collective-permute-start.5
  28.5 1.6 collective-permute-start.3
  31.7 3.4 %collective-permute-done.6 = bf16[2,48,768]{2,1,0:T(8,128)(2,1)S(1)} collective-permute-done((bf16[2,48,768]{2,1,0:T(8,128)(2,1)S(1)}, bf16[2,48,768]{2,1,0:T(8,128)(2,1)S(1)}, u32[]{:S(2)}, u32[]{:S(2)}) %collective-permute-start.6) | collective-permute-done | bytes 147488 | tf_op jit(solution)/shard_map/ppermute | solution.py:414
  35.1 2.0 collective-permute-done.8
  39.3 2.5 collective-permute-start.19
  42.0 1.9 collective-permute-start.17
  43.9 5.9 %collective-permute-done.9.refs_3_ = bf16[8,48,768]{2,1,0:T(8,128)(2,1)S(1)} collective-permute-done((bf16[8,48,768]{2,1,0:T(8,128)(2,1)S(1)}, bf16[8,48,768]{2,1,0:T(8,128)(2,1)S(1)}, u32[]{:S(2)}, u32[]{:S(2)}) %collective-permute-start.9) | collective-permute-done | bytes 589856 | tf_op jit(solution)/shard_map/ppermute | solution.py:414
  53.5 4.5 %collective-permute-done.11 = bf16[4,48,768]{2,1,0:T(8,128)(2,1)S(1)} collective-permute-done((bf16[4,48,768]{2,1,0:T(8,128)(2,1)S(1)}, bf16[4,48,768]{2,1,0:T(8,128)(2,1)S(1)}, u32[]{:S(2)}, u32[]{:S(2)}) %collective-permute-start.11) | collective-permute-done | bytes 294944 | tf_op jit(solution)/shard_map/ppermute | solution.py:414
  58.6 3.5 %collective-permute-done.10 = bf16[4,48,768]{2,1,0:T(8,128)(2,1)S(1)} collective-permute-done((bf16[4,48,768]{2,1,0:T(8,128)(2,1)S(1)}, bf16[4,48,768]{2,1,0:T(8,128)(2,1)S(1)}, u32[]{:S(2)}, u32[]{:S(2)}) %collective-permute-start.10) | collective-permute-done | bytes 294944 | tf_op jit(solution)/shard_map/ppermute | solution.py:414
  62.2 1.7 collective-permute-done.18
  64.7 8.2 %shard_map.365 = (bf16[544,768]{1,0:T(8,128)(2,1)S(1)}, bf16[544,768]{1,0:T(8,128)(2,1)S(1)}, bf16[544,1152]{1,0:T(8,128)(2,1)S(1)}, f32[544,128]{1,0:T(8,128)S(1)}, bf16[544,384]{1,0:T(8,128)(2,1)S(1)}) custom-call(bf16[512,768]{1,0:T(8,128)(2,1)S(1)} %get-tuple-element.237.token_ref, f32[16,768]{1,0:T(8,128)S(1)} %broadcast_select_fusion.mem_ref.keep_ref, ...), custom_call_target="tpu_custom_call" | custom-call | tf_op jit(solution)/shard_map/pallas_call | solution.py:66
  75.0 13.9 %collective-permute-done.20.refs_1_ = bf16[8,48,768]{2,1,0:T(8,128)(2,1)S(1)} collective-permute-done((bf16[8,48,768]{2,1,0:T(8,128)(2,1)S(1)}, bf16[8,48,768]{2,1,0:T(8,128)(2,1)S(1)}, u32[]{:S(2)}, u32[]{:S(2)}) %collective-permute-start.20) | collective-permute-done | bytes 589856 | tf_op jit(solution)/shard_map/ppermute | solution.py:414
  90.0 5.8 %shard_map.368 = (bf16[544,768]{1,0:T(8,128)(2,1)S(1)}, f32[544,768]{1,0:T(8,128)S(1)}, bf16[544,768]{1,0:T(8,128)(2,1)S(1)}, bf16[544,1536]{1,0:T(8,128)(2,1)S(1)}, bf16[544,1536]{1,0:T(8,128)(2,1)S(1)}) custom-call(bf16[512,768]{1,0:T(8,128)(2,1)S(1)} %get-tuple-element.237.token_ref, f32[16,768]{1,0:T(8,128)S(1)} %broadcast_select_fusion.mem_ref.keep_ref, ...), custom_call_target="tpu_custom_call" | custom-call | tf_op jit(solution)/shard_map/pallas_call | solution.py:66
  96.5 1.7 collective-permute-done.22.other_ref
  98.2 8.8 %shard_map.369 = (bf16[512,768]{1,0:T(8,128)(2,1)S(1)}, f32[16,768]{1,0:T(8,128)S(1)}, f32[544,768]{1,0:T(8,128)S(1)}, bf16[544,768]{1,0:T(8,128)(2,1)S(1)}, bf1...) custom-call(f32[544,768]{1,0:T(8,128)S(1)} %get-tuple-element.139.fi, ...), custom_call_target="tpu_custom_call" | custom-call | tf_op jit(solution)/shard_map/pallas_call | solution.py:66
  107.3 2.2 collective-permute-done.23.other_ref
  109.5 6.0 %shard_map.370 = (bf16[544,768]{1,0:T(8,128)(2,1)S(1)}, f32[544,768]{1,0:T(8,128)S(1)}, bf16[544,768]{1,0:T(8,128)(2,1)S(1)}, bf16[544,1536]{1,0:T(8,128)(2,1)S(1)}, bf16[544,1536]{1,0:T(8,128)(2,1)S(1)}) custom-call(bf16[512,768]{1,0:T(8,128)(2,1)S(1)} %get-tuple-element.238.token_ref, f32[16,768]{1,0:T(8,128)S(1)} %get-tuple-element.142.mem_ref, ...), custom_call_target="tpu_custom_call" | custom-call | tf_op jit(solution)/shard_map/pallas_call | solution.py:66
  115.8 2.1 collective-permute-done.24.other_ref
  117.9 7.1 %shard_map.371 = (bf16[512,768]{1,0:T(8,128)(2,1)S(1)}, bf16[544,768]{1,0:T(8,128)(2,1)S(1)}, f32[544,768]{1,0:T(8,128)S(1)}, bf16[544,768]{1,0:T(8,128)(2,1)S(1...) custom-call(f32[544,768]{1,0:T(8,128)S(1)} %get-tuple-element.144.first_ref, ...), custom_call_target="tpu_custom_call" | custom-call | tf_op jit(solution)/shard_map/pallas_call | solution.py:66
  125.2 2.2 collective-permute-done.25.other_ref
  127.4 10.3 %shard_map.372 = (bf16[544,768]{1,0:T(8,128)(2,1)S(1)}, f32[544,768]{1,0:T(8,128)S(1)}, bf16[544,768]{1,0:T(8,128)(2,1)S(1)}, bf16[544,1152]{1,0:T(8,128)(2,1)S(...) custom-call(f32[544,768]{1,0:T(8,128)S(1)} %get-tuple-element.148.dsecond_ref, ...), custom_call_target="tpu_custom_call" | custom-call | tf_op jit(solution)/shard_map/pallas_call | solution.py:66
  137.9 2.2 collective-permute-done.26.other_ref
  140.1 6.9 %shard_map.373 = (bf16[512,768]{1,0:T(8,128)(2,1)S(1)}, f32[16,768]{1,0:T(8,128)S(1)}, bf16[544,768]{1,0:T(8,128)(2,1)S(1)}, f32[544,768]{1,0:T(8,128)S(1)}, bf1...) custom-call(f32[544,768]{1,0:T(8,128)S(1)} %get-tuple-element.152.dfirs, ...), custom_call_target="tpu_custom_call" | custom-call | tf_op jit(solution)/shard_map/pallas_call | solution.py:66
  147.3 5.1 %shard_map.374 = (bf16[8,48,768]{2,1,0:T(8,128)(2,1)S(1)}, bf16[8,48,768]{2,1,0:T(8,128)(2,1)S(1)}, bf16[8,48,768]{2,1,0:T(8,128)(2,1)S(1)}, bf16[8,48,768]{2,1,0:T(8,128)(2,1)S(1)}) custom-call(s32[1]{0:T(128)} %bitcast.1.me_ref, bf16[544,768]{1,0:T(8,128)(2,1)S(1)} %get-tuple-element.157.refs_0_, bf16[544,768]{1,0:T(8,128)(2,1)S(1)} %get-tuple-element.158.refs_1_, ...), custom_call_target="tpu_custom_call" | custom-call | tf_op jit(solution)/shard_map/pallas_call | solution.py:66
  153.9 5.1 %shard_map.375 = (bf16[8,48,768]{2,1,0:T(8,128)(2,1)S(1)}, bf16[8,48,768]{2,1,0:T(8,128)(2,1)S(1)}, bf16[8,48,768]{2,1,0:T(8,128)(2,1)S(1)}, bf16[8,48,768]{2,1,0:T(8,128)(2,1)S(1)}) custom-call(s32[1]{0:T(128)} %bitcast.1.me_ref, bf16[544,768]{1,0:T(8,128)(2,1)S(1)} %get-tuple-element.162.refs_0_, bf16[544,768]{1,0:T(8,128)(2,1)S(1)} %get-tuple-element.163.refs_1_, ...), custom_call_target="tpu_custom_call" | custom-call | tf_op jit(solution)/shard_map/pallas_call | solution.py:66
  161.7 10.3 %shard_map.376 = (bf16[544,768]{1,0:T(8,128)(2,1)S(1)}, f32[544,768]{1,0:T(8,128)S(1)}, bf16[544,768]{1,0:T(8,128)(2,1)S(1)}, bf16[544,1152]{1,0:T(8,128)(2,1)S(...) custom-call(f32[544,768]{1,0:T(8,128)S(1)} %get-tuple-element.167.dsecond_ref, ...), custom_call_target="tpu_custom_call" | custom-call | tf_op jit(solution)/shard_map/pallas_call | solution.py:66
  172.1 6.2 %shard_map.378 = (bf16[8,48,768]{2,1,0:T(8,128)(2,1)S(1)}, bf16[8,48,768]{2,1,0:T(8,128)(2,1)S(1)}, bf16[8,48,768]{2,1,0:T(8,128)(2,1)S(1)}, bf16[8,48,768]{2,1,0:T(8,128)(2,1)S(1)}) custom-call(s32[1]{0:T(128)} %bitcast.1.me_ref, bf16[544,768]{1,0:T(8,128)(2,1)S(1)} %get-tuple-element.177.refs_0_, bf16[544,768]{1,0:T(8,128)(2,1)S(1)} %get-tuple-element.178.refs_1_, ...), custom_call_target="tpu_custom_call" | custom-call | tf_op jit(solution)/shard_map/pallas_call | solution.py:66
  178.3 2.4 collective-permute-done.31
  182.2 1.6 collective-permute-start.36
  185.8 11.4 %collective-permute-done.35 = bf16[8,48,768]{2,1,0:T(8,128)(2,1)S(1)} collective-permute-done((bf16[8,48,768]{2,1,0:T(8,128)(2,1)S(1)}, bf16[8,48,768]{2,1,0:T(8,128)(2,1)S(1)}, u32[]{:S(2)}, u32[]{:S(2)}) %collective-permute-start.35) | collective-permute-done | bytes 589856 | tf_op jit(solution)/shard_map/ppermute | solution.py:414
  197.4 1.6 collective-permute-start.41
  199.0 12.2 %collective-permute-done.34 = bf16[8,48,768]{2,1,0:T(8,128)(2,1)S(1)} collective-permute-done((bf16[8,48,768]{2,1,0:T(8,128)(2,1)S(1)}, bf16[8,48,768]{2,1,0:T(8,128)(2,1)S(1)}, u32[]{:S(2)}, u32[]{:S(2)}) %collective-permute-start.34) | collective-permute-done | bytes 589856 | tf_op jit(solution)/shard_map/ppermute | solution.py:414
  212.9 2.4 collective-permute-start.39
  215.3 5.1 %collective-permute-start.37 = (bf16[2,48,1536]{2,1,0:T(8,128)(2,1)S(1)}, bf16[2,48,1536]{2,1,0:T(8,128)(2,1)S(1)}, u32[]{:S(2)}, u32[]{:S(2)}) collective-permute-start(bf16[2,48,1536]{2,1,0:T(8,128)(2,1)S(1)} %get-tuple-element.242), channel_id=1, source_target_pairs={{0,8},{2,10},{4,12},{6,14},{8,0},{10,2},{12,4},{14,6},{16,24},{18,... | collective-permute-start | bytes 884744 | tf_op jit(solution)/shard_map/ppermute | solution.py:414
  221.4 2.4 collective-permute-start.44
  223.8 1.6 collective-permute-start.42
  225.4 16.8 %collective-permute-start.43 = (bf16[48,1536]{1,0:T(8,128)(2,1)S(1)}, bf16[48,1536]{1,0:T(8,128)(2,1)S(1)}, u32[]{:S(2)}, u32[]{:S(2)}) collective-permute-start(bf16[48,1536]{1,0:T(8,128)(2,1)S(1)} %get-tuple-element.247), channel_id=1, source_target_pairs={{0,16},{2,18},{4,20},{6,22},{8,24},{10,26},{12,28},{14,30},{16,0},... | collective-permute-start | bytes 442376 | tf_op jit(solution)/shard_map/ppermute | solution.py:414
  242.2 5.9 %collective-permute-done.38 = bf16[2,48,1536]{2,1,0:T(8,128)(2,1)S(1)} collective-permute-done((bf16[2,48,1536]{2,1,0:T(8,128)(2,1)S(1)}, bf16[2,48,1536]{2,1,0:T(8,128)(2,1)S(1)}, u32[]{:S(2)}, u32[]{:S(2)}) %collective-permute-start.38) | collective-permute-done | bytes 294944 | tf_op jit(solution)/shard_map/ppermute | solution.py:414
  248.2 3.1 %collective-permute-done.43.refs_10_ = bf16[48,1536]{1,0:T(8,128)(2,1)S(1)} collective-permute-done((bf16[48,1536]{1,0:T(8,128)(2,1)S(1)}, bf16[48,1536]{1,0:T(8,128)(2,1)S(1)}, u32[]{:S(2)}, u32[]{:S(2)}) %collective-permute-start.43) | collective-permute-done | bytes 147488 | tf_op jit(solution)/shard_map/ppermute | solution.py:414
  251.8 1.6 collective-permute-start.47
  255.3 1.8 collective-permute-done.47
  258.9 2.4 collective-permute-start.50
  261.2 2.1 collective-permute-start.48
  271.3 2.3 shard_map.380
  (185 shorter events, 47.1 us)
Async XLA Ops:
  3.3 13.7 %collective-permute-start.2 = (bf16[2,48,768]{2,1,0:T(8,128)(2,1)}, bf16[2,48,768]{2,1,0:T(8,128)(2,1)}, u32[]{:S(2)}, u32[]{:S(2)}) collective-permute-start(bf16[2,48,768]{2,1,0:T(8,128)(2,1)} %pad_maximum_fusion.9), channel_id=1, source_target_pairs={{0,24},{2,26},{4,28},{6,30},{8,16},{10,18},{12,20},{14,22},{16,8},... | collective-permute-start | bytes 442376 | tf_op jit(solution)/shard_map/ppermute | solution.py:414
  8.4 12.8 %collective-permute-start.1 = (bf16[2,48,768]{2,1,0:T(8,128)(2,1)}, bf16[2,48,768]{2,1,0:T(8,128)(2,1)}, u32[]{:S(2)}, u32[]{:S(2)}) collective-permute-start(bf16[2,48,768]{2,1,0:T(8,128)(2,1)} %pad_maximum_fusion.9), channel_id=1, source_target_pairs={{0,16},{2,18},{4,20},{6,22},{8,24},{10,26},{12,28},{14,30},{16,0},... | collective-permute-start | bytes 442376 | tf_op jit(solution)/shard_map/ppermute | solution.py:414
  8.4 12.8 %collective-permute-start = (bf16[2,48,768]{2,1,0:T(8,128)(2,1)}, bf16[2,48,768]{2,1,0:T(8,128)(2,1)}, u32[]{:S(2)}, u32[]{:S(2)}) collective-permute-start(bf16[2,48,768]{2,1,0:T(8,128)(2,1)} %pad_maximum_fusion.9), channel_id=1, source_target_pairs={{0,8},{2,10},{4,12},{6,14},{8,0},{10,2},{12,4},{14,6},{16,24},{18,... | collective-permute-start | bytes 442376 | tf_op jit(solution)/shard_map/ppermute | solution.py:414
  9.7 4.7 %collective-permute-start.16 = (bf16[48,768]{1,0:T(8,128)(2,1)}, bf16[48,768]{1,0:T(8,128)(2,1)}, u32[]{:S(2)}, u32[]{:S(2)}) collective-permute-start(bf16[48,768]{1,0:T(8,128)(2,1)} %get-tuple-element.264), channel_id=1, source_target_pairs={{0,4},{2,6},{4,0},{6,2},{8,12},{10,14},{12,8},{14,10},{16,20},{18,... | collective-permute-start | bytes 221192 | tf_op jit(solution)/shard_map/ppermute | solution.py:414
  11.4 4.7 %collective-permute-start.15 = (bf16[48,768]{1,0:T(8,128)(2,1)}, bf16[48,768]{1,0:T(8,128)(2,1)}, u32[]{:S(2)}, u32[]{:S(2)}) collective-permute-start(bf16[48,768]{1,0:T(8,128)(2,1)} %get-tuple-element.265), channel_id=1, source_target_pairs={{0,2},{2,0},{4,6},{6,4},{8,10},{10,8},{12,14},{14,12},{16,18},{18,... | collective-permute-start | bytes 221192 | tf_op jit(solution)/shard_map/ppermute | solution.py:414
  21.2 10.5 %collective-permute-start.7 = (bf16[2,48,768]{2,1,0:T(8,128)(2,1)S(1)}, bf16[2,48,768]{2,1,0:T(8,128)(2,1)S(1)}, u32[]{:S(2)}, u32[]{:S(2)}) collective-permute-start(bf16[2,48,768]{2,1,0:T(8,128)(2,1)S(1)} %pad_maximum_fusion.10), channel_id=1, source_target_pairs={{0,24},{2,26},{4,28},{6,30},{8,16},{10,18},{12,20},{14,22},{16,8},... | collective-permute-start | bytes 442376 | tf_op jit(solution)/shard_map/ppermute | solution.py:414
  23.8 11.2 %collective-permute-start.6 = (bf16[2,48,768]{2,1,0:T(8,128)(2,1)S(1)}, bf16[2,48,768]{2,1,0:T(8,128)(2,1)S(1)}, u32[]{:S(2)}, u32[]{:S(2)}) collective-permute-start(bf16[2,48,768]{2,1,0:T(8,128)(2,1)S(1)} %pad_maximum_fusion.10), channel_id=1, source_target_pairs={{0,16},{2,18},{4,20},{6,22},{8,24},{10,26},{12,28},{14,30},{16,0},... | collective-permute-start | bytes 442376 | tf_op jit(solution)/shard_map/ppermute | solution.py:414
  23.8 15.4 %collective-permute-start.5 = (bf16[2,48,768]{2,1,0:T(8,128)(2,1)S(1)}, bf16[2,48,768]{2,1,0:T(8,128)(2,1)S(1)}, u32[]{:S(2)}, u32[]{:S(2)}) collective-permute-start(bf16[2,48,768]{2,1,0:T(8,128)(2,1)S(1)} %pad_maximum_fusion.10), channel_id=1, source_target_pairs={{0,8},{2,10},{4,12},{6,14},{8,0},{10,2},{12,4},{14,6},{16,24},{18,... | collective-permute-start | bytes 442376 | tf_op jit(solution)/shard_map/ppermute | solution.py:414
  28.5 9.2 %collective-permute-start.3 = (bf16[4,48,768]{2,1,0:T(8,128)(2,1)S(1)}, bf16[4,48,768]{2,1,0:T(8,128)(2,1)S(1)}, u32[]{:S(2)}, u32[]{:S(2)}) collective-permute-start(bf16[4,48,768]{2,1,0:T(8,128)(2,1)S(1)} %pad_maximum_fusion.2), channel_id=1, source_target_pairs={{0,4},{2,6},{4,0},{6,2},{8,12},{10,14},{12,8},{14,10},{16,20},{18,... | collective-permute-start | bytes 884744 | tf_op jit(solution)/shard_map/ppermute | solution.py:414
  30.1 7.0 %collective-permute-start.8 = (bf16[4,48,768]{2,1,0:T(8,128)(2,1)S(1)}, bf16[4,48,768]{2,1,0:T(8,128)(2,1)S(1)}, u32[]{:S(2)}, u32[]{:S(2)}) collective-permute-start(bf16[4,48,768]{2,1,0:T(8,128)(2,1)S(1)} %pad_maximum_fusion.4), channel_id=1, source_target_pairs={{0,2},{2,0},{4,6},{6,4},{8,10},{10,8},{12,14},{14,12},{16,18},{18,... | collective-permute-start | bytes 884744 | tf_op jit(solution)/shard_map/ppermute | solution.py:414
  37.1 12.7 %collective-permute-start.9 = (bf16[8,48,768]{2,1,0:T(8,128)(2,1)S(1)}, bf16[8,48,768]{2,1,0:T(8,128)(2,1)S(1)}, u32[]{:S(2)}, u32[]{:S(2)}) collective-permute-start(bf16[8,48,768]{2,1,0:T(8,128)(2,1)S(1)} %constant_dynamic-update-slice_fusion.5.refs_2_), channel_id=1, source_target_pairs={{0,4},{2,6},{4,0},{6,2},{8,12},{10,14},{12,8},{14,10},{16,20},{18,... | collective-permute-start | bytes 1769480 | tf_op jit(solution)/shard_map/ppermute | solution.py:414
  37.7 13.6 %collective-permute-start.4 = (bf16[8,48,768]{2,1,0:T(8,128)(2,1)S(1)}, bf16[8,48,768]{2,1,0:T(8,128)(2,1)S(1)}, u32[]{:S(2)}, u32[]{:S(2)}) collective-permute-start(bf16[8,48,768]{2,1,0:T(8,128)(2,1)S(1)} %constant_dynamic-update-slice_fusion.refs_0_), channel_id=1, source_target_pairs={{0,2},{2,0},{4,6},{6,4},{8,10},{10,8},{12,14},{14,12},{16,18},{18,... | collective-permute-start | bytes 1769480 | tf_op jit(solution)/shard_map/ppermute | solution.py:414
  39.3 13.4 %collective-permute-start.19 = (bf16[2,2,48,768]{3,2,1,0:T(8,128)(2,1)S(1)}, bf16[2,2,48,768]{3,2,1,0:T(8,128)(2,1)S(1)}, u32[]{:S(2)}, u32[]{:S(2)}) collective-permute-start(bf16[2,2,48,768]{3,2,1,0:T(8,128)(2,1)S(1)} %pad_maximum_fusion.6), channel_id=1, source_target_pairs={{0,24},{2,26},{4,28},{6,30},{8,16},{10,18},{12,20},{14,22},{16,8},... | collective-permute-start | bytes 884744 | tf_op jit(solution)/shard_map/ppermute | solution.py:414
  41.9 22.0 %collective-permute-start.18 = (bf16[2,2,48,768]{3,2,1,0:T(8,128)(2,1)S(1)}, bf16[2,2,48,768]{3,2,1,0:T(8,128)(2,1)S(1)}, u32[]{:S(2)}, u32[]{:S(2)}) collective-permute-start(bf16[2,2,48,768]{3,2,1,0:T(8,128)(2,1)S(1)} %pad_maximum_fusion.6), channel_id=1, source_target_pairs={{0,16},{2,18},{4,20},{6,22},{8,24},{10,26},{12,28},{14,30},{16,0},... | collective-permute-start | bytes 884744 | tf_op jit(solution)/shard_map/ppermute | solution.py:414
  42.0 22.0 %collective-permute-start.17 = (bf16[2,2,48,768]{3,2,1,0:T(8,128)(2,1)S(1)}, bf16[2,2,48,768]{3,2,1,0:T(8,128)(2,1)S(1)}, u32[]{:S(2)}, u32[]{:S(2)}) collective-permute-start(bf16[2,2,48,768]{3,2,1,0:T(8,128)(2,1)S(1)} %pad_maximum_fusion.6), channel_id=1, source_target_pairs={{0,8},{2,10},{4,12},{6,14},{8,0},{10,2},{12,4},{14,6},{16,24},{18,... | collective-permute-start | bytes 884744 | tf_op jit(solution)/shard_map/ppermute | solution.py:414
  51.3 6.7 %collective-permute-start.11 = (bf16[4,48,768]{2,1,0:T(8,128)(2,1)S(1)}, bf16[4,48,768]{2,1,0:T(8,128)(2,1)S(1)}, u32[]{:S(2)}, u32[]{:S(2)}) collective-permute-start(bf16[4,48,768]{2,1,0:T(8,128)(2,1)S(1)} %pad_maximum_fusion.5), channel_id=1, source_target_pairs={{0,2},{2,0},{4,6},{6,4},{8,10},{10,8},{12,14},{14,12},{16,18},{18,... | collective-permute-start | bytes 884744 | tf_op jit(solution)/shard_map/ppermute | solution.py:414
  52.8 9.3 %collective-permute-start.10 = (bf16[4,48,768]{2,1,0:T(8,128)(2,1)S(1)}, bf16[4,48,768]{2,1,0:T(8,128)(2,1)S(1)}, u32[]{:S(2)}, u32[]{:S(2)}) collective-permute-start(bf16[4,48,768]{2,1,0:T(8,128)(2,1)S(1)} %pad_maximum_fusion.3), channel_id=1, source_target_pairs={{0,4},{2,6},{4,0},{6,2},{8,12},{10,14},{12,8},{14,10},{16,20},{18,... | collective-permute-start | bytes 884744 | tf_op jit(solution)/shard_map/ppermute | solution.py:414
  58.0 15.1 %collective-permute-start.14 = (bf16[8,48,768]{2,1,0:T(8,128)(2,1)S(1)}, bf16[8,48,768]{2,1,0:T(8,128)(2,1)S(1)}, u32[]{:S(2)}, u32[]{:S(2)}) collective-permute-start(bf16[8,48,768]{2,1,0:T(8,128)(2,1)S(1)} %constant_dynamic-update-slice_fusion.12.refs_2_), channel_id=1, source_target_pairs={{0,4},{2,6},{4,0},{6,2},{8,12},{10,14},{12,8},{14,10},{16,20},{18,... | collective-permute-start | bytes 1769480 | tf_op jit(solution)/shard_map/ppermute | solution.py:414
  62.1 11.0 %collective-permute-start.13 = (bf16[8,48,768]{2,1,0:T(8,128)(2,1)S(1)}, bf16[8,48,768]{2,1,0:T(8,128)(2,1)S(1)}, u32[]{:S(2)}, u32[]{:S(2)}) collective-permute-start(bf16[8,48,768]{2,1,0:T(8,128)(2,1)S(1)} %constant_dynamic-update-slice_fusion.10.refs_0_), channel_id=1, source_target_pairs={{0,2},{2,0},{4,6},{6,4},{8,10},{10,8},{12,14},{14,12},{16,18},{18,... | collective-permute-start | bytes 1769480 | tf_op jit(solution)/shard_map/ppermute | solution.py:414
  72.9 17.1 %collective-permute-start.12 = (bf16[544,768]{1,0:T(8,128)(2,1)S(1)}, bf16[544,768]{1,0:T(8,128)(2,1)S(1)}, u32[]{:S(2)}, u32[]{:S(2)}) collective-permute-start(bf16[544,768]{1,0:T(8,128)(2,1)S(1)} %get-tuple-element.135.own_ref), channel_id=1, source_target_pairs={{0,1},{1,0},{2,3},{3,2},{4,5},{5,4},{6,7},{7,6},{8,9},{9,8},{10,11... | collective-permute-start | bytes 2506760 | tf_op jit(solution)/shard_map/ppermute | solution.py:414
  73.1 15.8 %collective-permute-start.20 = (bf16[8,48,768]{2,1,0:T(8,128)(2,1)S(1)}, bf16[8,48,768]{2,1,0:T(8,128)(2,1)S(1)}, u32[]{:S(2)}, u32[]{:S(2)}) collective-permute-start(bf16[8,48,768]{2,1,0:T(8,128)(2,1)S(1)} %pad_maximum_fusion.refs_0_), channel_id=1, source_target_pairs={{0,4},{2,6},{4,0},{6,2},{8,12},{10,14},{12,8},{14,10},{16,20},{18,... | collective-permute-start | bytes 1769480 | tf_op jit(solution)/shard_map/ppermute | solution.py:414
  74.3 15.4 %collective-permute-start.21 = (bf16[8,48,768]{2,1,0:T(8,128)(2,1)S(1)}, bf16[8,48,768]{2,1,0:T(8,128)(2,1)S(1)}, u32[]{:S(2)}, u32[]{:S(2)}) collective-permute-start(bf16[8,48,768]{2,1,0:T(8,128)(2,1)S(1)} %pad_maximum_fusion.1.refs_2_), channel_id=1, source_target_pairs={{0,2},{2,0},{4,6},{6,4},{8,10},{10,8},{12,14},{14,12},{16,18},{18,... | collective-permute-start | bytes 1769480 | tf_op jit(solution)/shard_map/ppermute | solution.py:414
  107.1 2.4 collective-permute-start.23
  115.5 2.4 collective-permute-start.24
  147.1 14.7 %collective-permute-start.27 = (bf16[544,768]{1,0:T(8,128)(2,1)S(1)}, bf16[544,768]{1,0:T(8,128)(2,1)S(1)}, u32[]{:S(2)}, u32[]{:S(2)}) collective-permute-start(bf16[544,768]{1,0:T(8,128)(2,1)S(1)} %get-tuple-element.168.own_ref), channel_id=1, source_target_pairs={{0,1},{1,0},{2,3},{3,2},{4,5},{5,4},{6,7},{7,6},{8,9},{9,8},{10,11... | collective-permute-start | bytes 2506760 | tf_op jit(solution)/shard_map/ppermute | solution.py:414
  152.4 19.7 %collective-permute-start.29 = (bf16[8,48,768]{2,1,0:T(8,128)(2,1)S(1)}, bf16[8,48,768]{2,1,0:T(8,128)(2,1)S(1)}, u32[]{:S(2)}, u32[]{:S(2)}) collective-permute-start(bf16[8,48,768]{2,1,0:T(8,128)(2,1)S(1)} %get-tuple-element.176), channel_id=1, source_target_pairs={{0,2},{2,0},{4,6},{6,4},{8,10},{10,8},{12,14},{14,12},{16,18},{18,... | collective-permute-start | bytes 1769480 | tf_op jit(solution)/shard_map/ppermute | solution.py:414
  153.0 19.1 %collective-permute-start.30 = (bf16[8,48,768]{2,1,0:T(8,128)(2,1)S(1)}, bf16[8,48,768]{2,1,0:T(8,128)(2,1)S(1)}, u32[]{:S(2)}, u32[]{:S(2)}) collective-permute-start(bf16[8,48,768]{2,1,0:T(8,128)(2,1)S(1)} %get-tuple-element.180), channel_id=1, source_target_pairs={{0,4},{2,6},{4,0},{6,2},{8,12},{10,14},{12,8},{14,10},{16,20},{18,... | collective-permute-start | bytes 1769480 | tf_op jit(solution)/shard_map/ppermute | solution.py:414
  159.0 21.7 %collective-permute-start.31 = (bf16[8,48,768]{2,1,0:T(8,128)(2,1)S(1)}, bf16[8,48,768]{2,1,0:T(8,128)(2,1)S(1)}, u32[]{:S(2)}, u32[]{:S(2)}) collective-permute-start(bf16[8,48,768]{2,1,0:T(8,128)(2,1)S(1)} %get-tuple-element.188), channel_id=1, source_target_pairs={{0,2},{2,0},{4,6},{6,4},{8,10},{10,8},{12,14},{14,12},{16,18},{18,... | collective-permute-start | bytes 1769480 | tf_op jit(solution)/shard_map/ppermute | solution.py:414
  160.6 20.3 %collective-permute-start.32 = (bf16[8,48,768]{2,1,0:T(8,128)(2,1)S(1)}, bf16[8,48,768]{2,1,0:T(8,128)(2,1)S(1)}, u32[]{:S(2)}, u32[]{:S(2)}) collective-permute-start(bf16[8,48,768]{2,1,0:T(8,128)(2,1)S(1)} %get-tuple-element.189), channel_id=1, source_target_pairs={{0,4},{2,6},{4,0},{6,2},{8,12},{10,14},{12,8},{14,10},{16,20},{18,... | collective-permute-start | bytes 1769480 | tf_op jit(solution)/shard_map/ppermute | solution.py:414
  180.9 16.3 %collective-permute-start.35 = (bf16[8,48,768]{2,1,0:T(8,128)(2,1)S(1)}, bf16[8,48,768]{2,1,0:T(8,128)(2,1)S(1)}, u32[]{:S(2)}, u32[]{:S(2)}) collective-permute-start(bf16[8,48,768]{2,1,0:T(8,128)(2,1)S(1)} %get-tuple-element.195), channel_id=1, source_target_pairs={{0,4},{2,6},{4,0},{6,2},{8,12},{10,14},{12,8},{14,10},{16,20},{18,... | collective-permute-start | bytes 1769480 | tf_op jit(solution)/shard_map/ppermute | solution.py:414
  182.2 16.7 %collective-permute-start.36 = (bf16[4,2,48,768]{3,2,1,0:T(8,128)(2,1)S(1)}, bf16[4,2,48,768]{3,2,1,0:T(8,128)(2,1)S(1)}, u32[]{:S(2)}, u32[]{:S(2)}) collective-permute-start(bf16[4,2,48,768]{3,2,1,0:T(8,128)(2,1)S(1)} %slice.262), channel_id=1, source_target_pairs={{0,2},{2,0},{4,6},{6,4},{8,10},{10,8},{12,14},{14,12},{16,18},{18,... | collective-permute-start | bytes 1769480 | tf_op jit(solution)/shard_map/ppermute | solution.py:414
  183.8 27.4 %collective-permute-start.34 = (bf16[8,48,768]{2,1,0:T(8,128)(2,1)S(1)}, bf16[8,48,768]{2,1,0:T(8,128)(2,1)S(1)}, u32[]{:S(2)}, u32[]{:S(2)}) collective-permute-start(bf16[8,48,768]{2,1,0:T(8,128)(2,1)S(1)} %get-tuple-element.193), channel_id=1, source_target_pairs={{0,2},{2,0},{4,6},{6,4},{8,10},{10,8},{12,14},{14,12},{16,18},{18,... | collective-permute-start | bytes 1769480 | tf_op jit(solution)/shard_map/ppermute | solution.py:414
  184.7 26.8 %collective-permute-start.33 = (bf16[4,2,48,768]{3,2,1,0:T(8,128)(2,1)S(1)}, bf16[4,2,48,768]{3,2,1,0:T(8,128)(2,1)S(1)}, u32[]{:S(2)}, u32[]{:S(2)}) collective-permute-start(bf16[4,2,48,768]{3,2,1,0:T(8,128)(2,1)S(1)} %slice.260), channel_id=1, source_target_pairs={{0,4},{2,6},{4,0},{6,2},{8,12},{10,14},{12,8},{14,10},{16,20},{18,... | collective-permute-start | bytes 1769480 | tf_op jit(solution)/shard_map/ppermute | solution.py:414
  185.8 34.6 %collective-permute-start.28 = (bf16[544,768]{1,0:T(8,128)(2,1)S(1)}, bf16[544,768]{1,0:T(8,128)(2,1)S(1)}, u32[]{:S(2)}, u32[]{:S(2)}) collective-permute-start(bf16[544,768]{1,0:T(8,128)(2,1)S(1)} %get-tuple-element.172.own_ref), channel_id=1, source_target_pairs={{0,1},{1,0},{2,3},{3,2},{4,5},{5,4},{6,7},{7,6},{8,9},{9,8},{10,11... | collective-permute-start | bytes 2506760 | tf_op jit(solution)/shard_map/ppermute | solution.py:414
  197.4 23.8 %collective-permute-start.41 = (bf16[4,48,768]{2,1,0:T(8,128)(2,1)S(1)}, bf16[4,48,768]{2,1,0:T(8,128)(2,1)S(1)}, u32[]{:S(2)}, u32[]{:S(2)}) collective-permute-start(bf16[4,48,768]{2,1,0:T(8,128)(2,1)S(1)} %slice.278), channel_id=1, source_target_pairs={{0,2},{2,0},{4,6},{6,4},{8,10},{10,8},{12,14},{14,12},{16,18},{18,... | collective-permute-start | bytes 884744 | tf_op jit(solution)/shard_map/ppermute | solution.py:414
  211.5 9.7 %collective-permute-start.40 = (bf16[4,48,768]{2,1,0:T(8,128)(2,1)S(1)}, bf16[4,48,768]{2,1,0:T(8,128)(2,1)S(1)}, u32[]{:S(2)}, u32[]{:S(2)}) collective-permute-start(bf16[4,48,768]{2,1,0:T(8,128)(2,1)S(1)} %slice.276), channel_id=1, source_target_pairs={{0,4},{2,6},{4,0},{6,2},{8,12},{10,14},{12,8},{14,10},{16,20},{18,... | collective-permute-start | bytes 884744 | tf_op jit(solution)/shard_map/ppermute | solution.py:414
  212.9 12.4 %collective-permute-start.39 = (bf16[2,48,1536]{2,1,0:T(8,128)(2,1)S(1)}, bf16[2,48,1536]{2,1,0:T(8,128)(2,1)S(1)}, u32[]{:S(2)}, u32[]{:S(2)}) collective-permute-start(bf16[2,48,1536]{2,1,0:T(8,128)(2,1)S(1)} %get-tuple-element.241), channel_id=1, source_target_pairs={{0,24},{2,26},{4,28},{6,30},{8,16},{10,18},{12,20},{14,22},{16,8},... | collective-permute-start | bytes 884744 | tf_op jit(solution)/shard_map/ppermute | solution.py:414
  215.3 26.9 %collective-permute-start.37 = (bf16[2,48,1536]{2,1,0:T(8,128)(2,1)S(1)}, bf16[2,48,1536]{2,1,0:T(8,128)(2,1)S(1)}, u32[]{:S(2)}, u32[]{:S(2)}) collective-permute-start(bf16[2,48,1536]{2,1,0:T(8,128)(2,1)S(1)} %get-tuple-element.242), channel_id=1, source_target_pairs={{0,8},{2,10},{4,12},{6,14},{8,0},{10,2},{12,4},{14,6},{16,24},{18,... | collective-permute-start | bytes 884744 | tf_op jit(solution)/shard_map/ppermute | solution.py:414
  220.4 27.7 %collective-permute-start.38 = (bf16[2,48,1536]{2,1,0:T(8,128)(2,1)S(1)}, bf16[2,48,1536]{2,1,0:T(8,128)(2,1)S(1)}, u32[]{:S(2)}, u32[]{:S(2)}) collective-permute-start(bf16[2,48,1536]{2,1,0:T(8,128)(2,1)S(1)} %get-tuple-element.243), channel_id=1, source_target_pairs={{0,16},{2,18},{4,20},{6,22},{8,24},{10,26},{12,28},{14,30},{16,0},... | collective-permute-start | bytes 884744 | tf_op jit(solution)/shard_map/ppermute | solution.py:414
  221.4 26.8 %collective-permute-start.44 = (bf16[48,1536]{1,0:T(8,128)(2,1)S(1)}, bf16[48,1536]{1,0:T(8,128)(2,1)S(1)}, u32[]{:S(2)}, u32[]{:S(2)}) collective-permute-start(bf16[48,1536]{1,0:T(8,128)(2,1)S(1)} %get-tuple-element.244), channel_id=1, source_target_pairs={{0,24},{2,26},{4,28},{6,30},{8,16},{10,18},{12,20},{14,22},{16,8},... | collective-permute-start | bytes 442376 | tf_op jit(solution)/shard_map/ppermute | solution.py:414
  223.8 24.4 %collective-permute-start.42 = (bf16[48,1536]{1,0:T(8,128)(2,1)S(1)}, bf16[48,1536]{1,0:T(8,128)(2,1)S(1)}, u32[]{:S(2)}, u32[]{:S(2)}) collective-permute-start(bf16[48,1536]{1,0:T(8,128)(2,1)S(1)} %get-tuple-element.246), channel_id=1, source_target_pairs={{0,8},{2,10},{4,12},{6,14},{8,0},{10,2},{12,4},{14,6},{16,24},{18,... | collective-permute-start | bytes 442376 | tf_op jit(solution)/shard_map/ppermute | solution.py:414
  225.4 25.9 %collective-permute-start.43 = (bf16[48,1536]{1,0:T(8,128)(2,1)S(1)}, bf16[48,1536]{1,0:T(8,128)(2,1)S(1)}, u32[]{:S(2)}, u32[]{:S(2)}) collective-permute-start(bf16[48,1536]{1,0:T(8,128)(2,1)S(1)} %get-tuple-element.247), channel_id=1, source_target_pairs={{0,16},{2,18},{4,20},{6,22},{8,24},{10,26},{12,28},{14,30},{16,0},... | collective-permute-start | bytes 442376 | tf_op jit(solution)/shard_map/ppermute | solution.py:414
  251.8 5.3 %collective-permute-start.47 = (f32[24,768]{1,0:T(8,128)S(1)}, f32[24,768]{1,0:T(8,128)S(1)}, u32[]{:S(2)}, u32[]{:S(2)}) collective-permute-start(f32[24,768]{1,0:T(8,128)S(1)} %get-tuple-element.212), channel_id=1, source_target_pairs={{0,6},{2,4},{4,2},{6,0},{8,14},{10,12},{12,10},{14,8},{16,22},{18,... | collective-permute-start | bytes 221192 | tf_op jit(solution)/shard_map/ppermute | solution.py:414
  253.4 4.5 %collective-permute-start.46 = (f32[24,768]{1,0:T(8,128)S(1)}, f32[24,768]{1,0:T(8,128)S(1)}, u32[]{:S(2)}, u32[]{:S(2)}) collective-permute-start(f32[24,768]{1,0:T(8,128)S(1)} %get-tuple-element.212), channel_id=1, source_target_pairs={{0,4},{2,6},{4,0},{6,2},{8,12},{10,14},{12,8},{14,10},{16,20},{18,... | collective-permute-start | bytes 221192 | tf_op jit(solution)/shard_map/ppermute | solution.py:414
  254.5 4.4 %collective-permute-start.45 = (f32[24,768]{1,0:T(8,128)S(1)}, f32[24,768]{1,0:T(8,128)S(1)}, u32[]{:S(2)}, u32[]{:S(2)}) collective-permute-start(f32[24,768]{1,0:T(8,128)S(1)} %get-tuple-element.212), channel_id=1, source_target_pairs={{0,2},{2,0},{4,6},{6,4},{8,10},{10,8},{12,14},{14,12},{16,18},{18,... | collective-permute-start | bytes 221192 | tf_op jit(solution)/shard_map/ppermute | solution.py:414
  258.9 6.2 %collective-permute-start.50 = (f32[24,768]{1,0:T(8,128)S(1)}, f32[24,768]{1,0:T(8,128)S(1)}, u32[]{:S(2)}, u32[]{:S(2)}) collective-permute-start(f32[24,768]{1,0:T(8,128)S(1)} %add_add_fusion.1), channel_id=1, source_target_pairs={{0,24},{2,26},{4,28},{6,30},{8,16},{10,18},{12,20},{14,22},{16,8},... | collective-permute-start | bytes 221192 | tf_op jit(solution)/shard_map/ppermute | solution.py:414
  261.2 5.4 %collective-permute-start.49 = (f32[24,768]{1,0:T(8,128)S(1)}, f32[24,768]{1,0:T(8,128)S(1)}, u32[]{:S(2)}, u32[]{:S(2)}) collective-permute-start(f32[24,768]{1,0:T(8,128)S(1)} %add_add_fusion.1), channel_id=1, source_target_pairs={{0,16},{2,18},{4,20},{6,22},{8,24},{10,26},{12,28},{14,30},{16,0},... | collective-permute-start | bytes 221192 | tf_op jit(solution)/shard_map/ppermute | solution.py:414
  261.2 5.4 %collective-permute-start.48 = (f32[24,768]{1,0:T(8,128)S(1)}, f32[24,768]{1,0:T(8,128)S(1)}, u32[]{:S(2)}, u32[]{:S(2)}) collective-permute-start(f32[24,768]{1,0:T(8,128)S(1)} %add_add_fusion.1), channel_id=1, source_target_pairs={{0,8},{2,10},{4,12},{6,14},{8,0},{10,2},{12,4},{14,6},{16,24},{18,... | collective-permute-start | bytes 221192 | tf_op jit(solution)/shard_map/ppermute | solution.py:414
  (27 other events, 76.7 us)
where the time goes:
time: 278 us; the launch traced here: 274 us
  waiting for transfers between devices  94 us (34%)
  Pallas kernels  83.9 us (30%)
  starting transfers between devices  76.1 us (27%)
  other arithmetic  9.58 us (3%)
  local copies, waits for them, and re-layouts  6.62 us (2%)
  between operations  3.86 us (1%)
    ppermute x52, waiting for transfers between devices, exchange(): return lax.ppermute(values, axis, [(i, i ^ flip) for i in range(size)])  94 us
    pallas_call x17, Pallas kernels, call(): pl.pallas_call(kernel, out_shape=[jax.ShapeDtypeStruct(s, d) for s, d in...  83.9 us
    ppermute x52, starting transfers between devices, exchange(): return lax.ppermute(values, axis, [(i, i ^ flip) for i in range(size)])  76.1 us
  transfers between devices with their start and end apart: 52, of which 28 were waited for; matrix products, arithmetic and copies ran while one was open for 4% of the time, Pallas kernels for 13%

commit v1 on v0

--- a/solution.py
+++ b/solution.py
@@ -26,7 +26,7 @@
 SLOTS = 16
 PAD = 16
 USED = 10
-WIDE = 384
+WIDE = 256
 CHUNK = 256
 LOW, CTX, H_LOW, ACTIVE, DF_LOW, DU, DA, DQKV = range(8)
 
@@ -101,6 +101,19 @@
         begin += count
 
 
+def dead_rows(rows):
+    at = lax.broadcasted_iota(jnp.int32, (rows, 128), 0) - (rows - 2 * PAD)
+    return (at >= 0) & ((at & (PAD - 1)) >= USED)
+
+
+def masked_scores(q, k, mine, dead, lane, head, dot):
+    spare = lane == (127 if head == 0 else 0)
+    zero = jnp.zeros_like(q)
+    q_one = jnp.where(spare, jnp.ones_like(q), jnp.where(mine, q, zero))
+    k_one = jnp.where(spare, jnp.where(dead, jnp.full_like(k, NEG), zero), k)
+    return dot(q_one, k_one)
+
+
 def attn_rows(low_ref, qk_ref, vo_ref, bias_ref, part_ref, qkv_ref, lse_ref, ctx_ref):
     rows = low_ref.shape[0]
     width = vo_ref.shape[1] // 2
@@ -111,10 +124,9 @@
     qkv_ref[:, width : 2 * width] = qk[:, width:].astype(BF)
     v_all = dot_nn(low, vo_ref[:, :width])
     qkv_ref[:, 2 * width :] = (v_all + bias_ref[:, width : 2 * width]).astype(BF)
-    key_at = lax.broadcasted_iota(jnp.int32, (1, rows), 1)
-    dead = (key_at >= seg) & (((key_at - seg) & (PAD - 1)) >= USED)
     lane = lax.broadcasted_iota(jnp.int32, (rows, 128), 1)
     lse_ref[...] = jnp.zeros_like(lse_ref)
+    dead = dead_rows(rows)
 
     def heads(pair, carry):
         at = pl.multiple_of(pair * 128, 128)
@@ -124,13 +136,11 @@
         outs = []
         for head in range(2):
             mine = (lane < 64) if head == 0 else (lane >= 64)
-            s = dot_nt(jnp.where(mine, q, jnp.zeros_like(q)), k) * (HD**-0.5 * LOG2E)
-            s = jnp.where(dead, NEG, s)
+            s = masked_scores(q, k, mine, dead, lane, head, dot_nt) * (HD**-0.5 * LOG2E)
             top = jnp.max(s, axis=1, keepdims=True)
             e = jnp.exp2(s - top)
             total = jnp.sum(e, axis=1, keepdims=True)
-            p = (e * (1.0 / total)).astype(BF)
-            outs.append(dot_nn(p, v))
+            outs.append(dot_nn(e.astype(BF), v) * (1.0 / total))
             lse_ref[...] = jnp.where(lane == 2 * pair + head, top + jnp.log2(total), lse_ref[...])
         ctx_ref[:, pl.ds(at, 128)] = jnp.where(lane < 64, outs[0], outs[1]).astype(BF)
         return carry
@@ -173,7 +183,7 @@
 
 
 def ffn_forward_kernel(token_ref, mem_ref, own_ref, other_ref, up_ref, down_ref, bias_ref, shared_ref,
-                       part_ref, first_ref, low_ref, act_ref, slope_ref, total_ref):
+                       part_ref, first_ref, low_ref, act_ref, slope_ref):
     seg = token_ref.shape[0]
     hidden_units = up_ref.shape[1]
     begin = bias_ref.shape[1] - hidden_units
@@ -184,7 +194,6 @@
     unit, unused = norm_stats(first_ref[...])
     hidden = unit * shared_ref[USED + 2 : USED + 3, :] + shared_ref[USED + 3 : USED + 4, :]
     low_ref[...] = hidden.astype(BF)
-    total_ref[...] = jnp.zeros_like(total_ref)
 
     def units(step, carry):
         for piece in range(2):
@@ -195,15 +204,14 @@
             active = (u * cdf).astype(BF)
             act_ref[:, pl.ds(at, WIDE)] = active
             slope_ref[:, pl.ds(at, WIDE)] = (cdf + u * density).astype(BF)
-            total_ref[...] += dot_nt(active, down_ref[:, pl.ds(at, WIDE)])
         return carry
 
     lax.fori_loop(0, hidden_units // (2 * WIDE), units, 0)
-    part_ref[...] = total_ref[...].astype(BF)
+    part_ref[...] = dot_nt(act_ref[...], down_ref[...]).astype(BF)
 
 
 def ffn_backward_rows(second, dmem, cot_ref, alive_ref, shared_ref, up_ref, down_ref, slope_ref,
-                      part_ref, dsecond_ref, dlow_ref, du_ref, dbias_ref, dvec_ref, total_ref):
+                      part_ref, dsecond_ref, dlow_ref, du_ref, dbias_ref, dvec_ref):
     unit, scale = norm_stats(second)
     dy = jnp.concatenate(
         [cot_ref[...].astype(F32) * alive_ref[...], jnp.zeros((PAD, unit.shape[1]), F32), dmem * alive_ref[...]], axis=0
@@ -215,7 +223,6 @@
     dvec_ref[2:3, :] = row_sum(dy)
     dvec_ref[3:, :] = jnp.zeros((dvec_ref.shape[0] - 3, unit.shape[1]), F32)
     dlow_ref[...] = dsecond.astype(BF)
-    total_ref[...] = jnp.zeros_like(total_ref)
 
     def units(step, carry):
         for piece in range(2):
@@ -224,11 +231,10 @@
             dbias_ref[:, pl.ds(at, WIDE)] = row_sum(du)
             du_low = du.astype(BF)
             du_ref[:, pl.ds(at, WIDE)] = du_low
-            total_ref[...] += dot_nt(du_low, up_ref[:, pl.ds(at, WIDE)])
         return carry
 
     lax.fori_loop(0, up_ref.shape[1] // (2 * WIDE), units, 0)
-    part_ref[...] = total_ref[...].astype(BF)
+    part_ref[...] = dot_nt(du_ref[...], up_ref[...]).astype(BF)
 
 
 def ffn_last_kernel(first_ref, own_ref, other_ref, cot_ref, dmem_ref, alive_ref, shared_ref, up_ref, down_ref, slope_ref,
@@ -274,10 +280,8 @@
     da_ref[...] = dfirst.astype(BF)
     dctx_ref[...] = dot_nn(da_ref[...], vo_ref[:, width:]).astype(BF)
     lse_t_ref[...] = jnp.transpose(lse_ref[...])
-    key_at = lax.broadcasted_iota(jnp.int32, (rows, 1), 0)
-    dead = (key_at >= seg) & (((key_at - seg) & (PAD - 1)) >= USED)
+    dead = dead_rows(rows)
     lane = lax.broadcasted_iota(jnp.int32, (rows, 128), 1)
-    sub = lax.broadcasted_iota(jnp.int32, (128, rows), 0)
 
     def heads(pair, carry):
         at = pl.multiple_of(pair * 128, 128)
@@ -285,23 +289,24 @@
         k = qkv_ref[:, pl.ds(width + at, 128)]
         v = qkv_ref[:, pl.ds(2 * width + at, 128)]
         dc = dctx_ref[:, pl.ds(at, 128)]
-        dq_t, dk, dv = [], None, None
+        dq, dk, dv = None, None, None
         for head in range(2):
             mine = (lane < 64) if head == 0 else (lane >= 64)
             q_one = jnp.where(mine, q, jnp.zeros_like(q))
             dc_one = jnp.where(mine, dc, jnp.zeros_like(dc))
-            s_t = dot_nt(k, q_one) * (HD**-0.5 * LOG2E)
+            s_t = masked_scores(q, k, mine, dead, lane, head, lambda a, b: dot_nt(b, a)) * (HD**-0.5 * LOG2E)
             lse_row = lse_t_ref[pl.ds(2 * pair + head, 1), :]
-            p_t = jnp.where(dead, 0.0, jnp.exp2(s_t - lse_row))
+            p_t = jnp.exp2(s_t - lse_row)
             dp_t = dot_nt(v, dc_one)
             dv_one = dot_nn(p_t.astype(BF), dc_one)
             inner = row_sum(p_t * dp_t)
             ds_t = (p_t * (dp_t - inner)).astype(BF)
             dk_one = dot_nn(ds_t, q_one)
-            dq_t.append(dot_tn(k, ds_t))
+            dq_one = dot_tn(ds_t, jnp.where(mine, k, jnp.zeros_like(k)))
+            dq = dq_one if dq is None else dq + dq_one
             dv = dv_one if dv is None else dv + dv_one
             dk = dk_one if dk is None else dk + dk_one
-        dq = jnp.transpose(jnp.where(sub < 64, dq_t[0], dq_t[1])) * (HD**-0.5)
+        dq = dq * (HD**-0.5)
         dk = dk * (HD**-0.5)
         dhead_ref[:, pl.ds(at, 128)] = row_sum(dq)
         dhead_ref[:, pl.ds(width + at, 128)] = row_sum(dv)
@@ -532,7 +537,6 @@
         low_c = [jnp.concatenate([v[i] for v in line_three]) for i in range(2)]
         low_c = [after(v, *high_two) for v in low_c]
         high_c = [exchange(low_c[i], "dp", size, 2 - i) for i in range(2)]
-        high_one = [after(h, *low_two) for h in high_one]
         w_qk, w_vo = assembled(z_first, [[low_one[i], high_one[i]] for i in range(2)], False)
         (w_up,) = assembled(z_first, [[low_two[i], high_two[i]] for i in range(2)], True)
         (w_down,) = assembled(z_mid, [[low_c[i], high_c[i]] for i in range(2)], True)
@@ -567,7 +571,6 @@
             ffn_forward_kernel,
             [((rows, model), BF), ((rows, model), F32), ((rows, model), BF), ((rows, hidden), BF), ((rows, hidden), BF)],
             [tokens, memory, part, other, w_up, w_down, head_bias, shared_params],
-            scratch=[pltpu.VMEM((rows, model), F32)],
         )
         other = exchange(ffn_part, "head", pair, 1)
         saved.append((*attn, first_in, h_low, active, slope))
@@ -596,13 +599,11 @@
     for slot in reversed(range(segments)):
         low, qkv, lse, ctx, first_in, h_low, active, slope = saved[slot][:8]
         weights = [alive[slot], shared_params, w_up, w_down, slope]
-        scratch = [pltpu.VMEM((rows, model), F32)]
         if slot == segments - 1:
             out_rows, part, dsecond, df_low, du, dbias, dvec_two = call(
                 ffn_last_kernel,
                 [((seg, model), BF)] + ffn_outs,
                 [first_in, ffn_part, other, cotangent[0, slot], dmem, *weights],
-                scratch=scratch,
             )
             tokens_out.append(out_rows)
         else:
@@ -610,7 +611,6 @@
                 ffn_before_kernel,
                 [((seg, model), BF), ((pad, model), F32)] + ffn_outs,
                 [dfirst, part, other, alive[slot + 1], dmem, saved[slot][8], cotangent[0, slot], *weights],
-                scratch=scratch,
             )
         other = exchange(part, "head", pair, 1)
         stacks[slot] = (low, ctx, h_low, active, df_low, du)
@@ -652,27 +652,25 @@
     x_first, y_first = (1, 2), (2, 1)
     if size == SLOTS:
         got_down, got_up = hop([p[1] for p in dw_down], x_first), hop([p[1] for p in dw_up], x_first)
-        stacks[0] = stacks[0][:DQKV] + (after(stacks[0][DQKV], *got_down),)
+        down = add_halves([p[0] for p in dw_down], [after(g, stacks[0][DQKV]) for g in got_down])
+        stacks[0] = stacks[0][:DQKV] + (after(stacks[0][DQKV], *down),)
+        got_down = hop([v[4:] for v in down], y_first)
     dw_qkvo = weight_grad(
         (LOW, DQKV, DA, CTX),
         [[(LOW, DQKV, 0, 2 * width)], [(LOW, DQKV, 2 * width, width), (DA, CTX, 0, width)]],
         z_first,
     )
     if size == SLOTS:
-        dw_qkvo = [[after(v, *got_up) for v in part] for part in dw_qkvo]
+        dw_qkvo = [[after(v, *got_up, *got_down) for v in part] for part in dw_qkvo]
         got_qkvo = hop([p[1] for p in dw_qkvo], x_first)
-        keep = [jnp.stack([dw_down[i][0], dw_up[i][0]], axis=1) for i in range(2)]
-        got = [jnp.stack([after(got_down[i], dw_qkvo[0][0]), got_up[i]], axis=1) for i in range(2)]
-        both = add_halves(keep, got)
-        got = hop([v[4:] for v in both], y_first)
-        both = add_halves([v[:4] for v in both], [after(g, *got_qkvo) for g in got])
-        last = add_halves([p[0] for p in dw_qkvo], got_qkvo)
-        last = add_halves([v[:4] for v in last], hop([v[4:] for v in last], y_first))
-        both = jnp.concatenate(both, axis=3)
-        got = line_hop(both)
-        last = jnp.concatenate(last, axis=2)
-        sums = [[both[0, i], *[g[i] for g in got]] for i in range(2)]
-        sums.append([last[0], *line_hop(last)])
+        down = jnp.concatenate(add_halves([v[:4] for v in down], [after(g, dw_qkvo[0][0]) for g in got_down]), axis=2)
+        got_down = line_hop(down)
+        up = add_halves([p[0] for p in dw_up], [after(g, down) for g in got_up])
+        got_up = hop([v[4:] for v in up], y_first)
+        last = add_halves([p[0] for p in dw_qkvo], [after(g, *got_down) for g in got_qkvo])
+        up = jnp.concatenate(add_halves([v[:4] for v in up], [after(g, *got_qkvo) for g in got_up]), axis=2)
+        last = jnp.concatenate(add_halves([v[:4] for v in last], hop([v[4:] for v in last], y_first)), axis=2)
+        sums = [[down[0], *got_down], [up[0], *line_hop(up)], [last[0], *line_hop(last)]]
     else:
         sums = [[fallback(p, z_first)] for p in (dw_down, dw_up, dw_qkvo)]
     height, wide = sums[0][0].shape

time: 278 us -> 265 us (0.953)
  Pallas kernels: 83.9 us -> 77.7 us
  starting transfers between devices: 76.1 us -> 71.7 us
    pallas_call x17, Pallas kernels: 83.9 us -> 77.7 us  [call(): pl.pallas_call(kernel, out_shape=[jax.ShapeDtypeStruct(s, d) for s, d in...]
    ppermute x52 -> x57, starting transfers between devices: 76.1 us -> 71.7 us  [exchange(): return lax.ppermute(values, axis, [(i, i ^ flip) for i in range(size)])]
    ppermute x52 -> x57, waiting for transfers between devices: 94 us -> 91.9 us  [exchange(): return lax.ppermute(values, axis, [(i, i ^ flip) for i in range(size)])]
  transfers between devices with their start and end apart: 52 -> 57, of which waited for: 28 -> 35; matrix products, arithmetic and copies ran while one was open for 4% -> 4% of each run, Pallas kernels for 13% -> 13%
where the time goes in v1:
time: 265 us; the launch traced here: 261 us
  waiting for transfers between devices  91.9 us (35%)
  Pallas kernels  77.7 us (29%)
  starting transfers between devices  71.7 us (27%)
  other arithmetic  10.6 us (4%)
  local copies, waits for them, and re-layouts  5.66 us (2%)
  between operations  3.57 us (1%)
    ppermute x57, waiting for transfers between devices, exchange(): return lax.ppermute(values, axis, [(i, i ^ flip) for i in range(size)])  91.9 us
    pallas_call x17, Pallas kernels, call(): pl.pallas_call(kernel, out_shape=[jax.ShapeDtypeStruct(s, d) for s, d in...  77.7 us
    ppermute x57, starting transfers between devices, exchange(): return lax.ppermute(values, axis, [(i, i ^ flip) for i in range(size)])  71.7 us
  transfers between devices with their start and end apart: 57, of which 35 were waited for; matrix products, arithmetic and copies ran while one was open for 4% of the time, Pallas kernels for 13%

profile of v1, /device:TPU:0, one launch (start us, length us, event | category | flops | bytes accessed | tf_op | source)
XLA Modules:
  0.0 261.0 jit_solution(1398458783689219434)
XLA Ops:
  3.4 5.0 %collective-permute-start.2 = (bf16[2,48,768]{2,1,0:T(8,128)(2,1)}, bf16[2,48,768]{2,1,0:T(8,128)(2,1)S(1)}, u32[]{:S(2)}, u32[]{:S(2)}) collective-permute-start(bf16[2,48,768]{2,1,0:T(8,128)(2,1)} %pad_maximum_fusion.10), channel_id=1, source_target_pairs={{0,24},{2,26},{4,28},{6,30},{8,16},{10,18},{12,20},{14,22},{16,8},... | collective-permute-start | bytes 442376 | tf_op jit(solution)/shard_map/ppermute | solution.py:419
  10.7 1.7 collective-permute-start.16
  18.0 3.2 %collective-permute-done.1 = bf16[2,48,768]{2,1,0:T(8,128)(2,1)} collective-permute-done((bf16[2,48,768]{2,1,0:T(8,128)(2,1)}, bf16[2,48,768]{2,1,0:T(8,128)(2,1)}, u32[]{:S(2)}, u32[]{:S(2)}) %collective-permute-start.1) | collective-permute-done | bytes 147488 | tf_op jit(solution)/shard_map/ppermute | solution.py:419
  21.2 2.7 %collective-permute-start.10 = (bf16[2,48,768]{2,1,0:T(8,128)(2,1)S(1)}, bf16[2,48,768]{2,1,0:T(8,128)(2,1)S(1)}, u32[]{:S(2)}, u32[]{:S(2)}) collective-permute-start(bf16[2,48,768]{2,1,0:T(8,128)(2,1)S(1)} %pad_maximum_fusion.11), channel_id=1, source_target_pairs={{0,24},{2,26},{4,28},{6,30},{8,16},{10,18},{12,20},{14,22},{16,8},... | collective-permute-start | bytes 442376 | tf_op jit(solution)/shard_map/ppermute | solution.py:419
  23.9 1.7 collective-permute-start.8
  27.6 1.6 collective-permute-start.3
  30.8 4.3 %collective-permute-done.9 = bf16[2,48,768]{2,1,0:T(8,128)(2,1)S(1)} collective-permute-done((bf16[2,48,768]{2,1,0:T(8,128)(2,1)S(1)}, bf16[2,48,768]{2,1,0:T(8,128)(2,1)S(1)}, u32[]{:S(2)}, u32[]{:S(2)}) %collective-permute-start.9) | collective-permute-done | bytes 147488 | tf_op jit(solution)/shard_map/ppermute | solution.py:419
  38.5 2.5 collective-permute-start.19
  41.1 1.9 collective-permute-start.17
  43.1 6.8 %collective-permute-done.6.refs_3_ = bf16[8,48,768]{2,1,0:T(8,128)(2,1)S(1)} collective-permute-done((bf16[8,48,768]{2,1,0:T(8,128)(2,1)S(1)}, bf16[8,48,768]{2,1,0:T(8,128)(2,1)S(1)}, u32[]{:S(2)}, u32[]{:S(2)}) %collective-permute-start.6) | collective-permute-done | bytes 589856 | tf_op jit(solution)/shard_map/ppermute | solution.py:419
  53.4 4.9 %collective-permute-done.13 = bf16[4,48,768]{2,1,0:T(8,128)(2,1)S(1)} collective-permute-done((bf16[4,48,768]{2,1,0:T(8,128)(2,1)S(1)}, bf16[4,48,768]{2,1,0:T(8,128)(2,1)S(1)}, u32[]{:S(2)}, u32[]{:S(2)}) %collective-permute-start.13) | collective-permute-done | bytes 294944 | tf_op jit(solution)/shard_map/ppermute | solution.py:419
  58.8 2.1 collective-permute-done.11
  61.0 3.0 %collective-permute-done.18 = bf16[2,2,48,768]{3,2,1,0:T(8,128)(2,1)S(1)} collective-permute-done((bf16[2,2,48,768]{3,2,1,0:T(8,128)(2,1)S(1)}, bf16[2,2,48,768]{3,2,1,0:T(8,128)(2,1)S(1)}, u32[]{:S(2)}, u32[]{:S(2)}) %collective-permute-start.18) | collective-permute-done | bytes 294944 | tf_op jit(solution)/shard_map/ppermute | solution.py:419
  64.7 7.0 %shard_map.365 = (bf16[544,768]{1,0:T(8,128)(2,1)S(1)}, bf16[544,768]{1,0:T(8,128)(2,1)S(1)}, bf16[544,1152]{1,0:T(8,128)(2,1)S(1)}, f32[544,128]{1,0:T(8,128)S(1)}, bf16[544,384]{1,0:T(8,128)(2,1)S(1)}) custom-call(bf16[512,768]{1,0:T(8,128)(2,1)S(1)} %get-tuple-element.245.token_ref, f32[16,768]{1,0:T(8,128)S(1)} %broadcast_select_fusion.mem_ref.keep_ref, ...), custom_call_target="tpu_custom_call" | custom-call | tf_op jit(solution)/shard_map/pallas_call | solution.py:66
  74.3 13.4 %collective-permute-done.20.refs_1_ = bf16[8,48,768]{2,1,0:T(8,128)(2,1)S(1)} collective-permute-done((bf16[8,48,768]{2,1,0:T(8,128)(2,1)S(1)}, bf16[8,48,768]{2,1,0:T(8,128)(2,1)S(1)}, u32[]{:S(2)}, u32[]{:S(2)}) %collective-permute-start.20) | collective-permute-done | bytes 589856 | tf_op jit(solution)/shard_map/ppermute | solution.py:419
  88.2 5.2 %shard_map.368 = (bf16[544,768]{1,0:T(8,128)(2,1)S(1)}, f32[544,768]{1,0:T(8,128)S(1)}, bf16[544,768]{1,0:T(8,128)(2,1)S(1)}, bf16[544,1536]{1,0:T(8,128)(2,1)S(1)}, bf16[544,1536]{1,0:T(8,128)(2,1)S(1)}) custom-call(bf16[512,768]{1,0:T(8,128)(2,1)S(1)} %get-tuple-element.245.token_ref, f32[16,768]{1,0:T(8,128)S(1)} %broadcast_select_fusion.mem_ref.keep_ref, ...), custom_call_target="tpu_custom_call" | custom-call | tf_op jit(solution)/shard_map/pallas_call | solution.py:66
  94.1 1.7 collective-permute-done.22.other_ref
  95.8 8.0 %shard_map.369 = (bf16[512,768]{1,0:T(8,128)(2,1)S(1)}, f32[16,768]{1,0:T(8,128)S(1)}, f32[544,768]{1,0:T(8,128)S(1)}, bf16[544,768]{1,0:T(8,128)(2,1)S(1)}, bf1...) custom-call(f32[544,768]{1,0:T(8,128)S(1)} %get-tuple-element.141.fi, ...), custom_call_target="tpu_custom_call" | custom-call | tf_op jit(solution)/shard_map/pallas_call | solution.py:66
  104.0 2.2 collective-permute-done.23.other_ref
  106.2 5.5 %shard_map.370 = (bf16[544,768]{1,0:T(8,128)(2,1)S(1)}, f32[544,768]{1,0:T(8,128)S(1)}, bf16[544,768]{1,0:T(8,128)(2,1)S(1)}, bf16[544,1536]{1,0:T(8,128)(2,1)S(1)}, bf16[544,1536]{1,0:T(8,128)(2,1)S(1)}) custom-call(bf16[512,768]{1,0:T(8,128)(2,1)S(1)} %get-tuple-element.246.token_ref, f32[16,768]{1,0:T(8,128)S(1)} %get-tuple-element.144.mem_ref, ...), custom_call_target="tpu_custom_call" | custom-call | tf_op jit(solution)/shard_map/pallas_call | solution.py:66
  112.0 2.1 collective-permute-done.24.other_ref
  114.1 5.6 %shard_map.371 = (bf16[512,768]{1,0:T(8,128)(2,1)S(1)}, bf16[544,768]{1,0:T(8,128)(2,1)S(1)}, f32[544,768]{1,0:T(8,128)S(1)}, bf16[544,768]{1,0:T(8,128)(2,1)S(1...) custom-call(f32[544,768]{1,0:T(8,128)S(1)} %get-tuple-element.146.first_ref, ...), custom_call_target="tpu_custom_call" | custom-call | tf_op jit(solution)/shard_map/pallas_call | solution.py:66
  120.0 2.2 collective-permute-done.25.other_ref
  122.2 9.9 %shard_map.372 = (bf16[544,768]{1,0:T(8,128)(2,1)S(1)}, f32[544,768]{1,0:T(8,128)S(1)}, bf16[544,768]{1,0:T(8,128)(2,1)S(1)}, bf16[544,1152]{1,0:T(8,128)(2,1)S(...) custom-call(f32[544,768]{1,0:T(8,128)S(1)} %get-tuple-element.150.dsecond_ref, ...), custom_call_target="tpu_custom_call" | custom-call | tf_op jit(solution)/shard_map/pallas_call | solution.py:66
  132.3 2.2 collective-permute-done.26.other_ref
  134.5 5.9 %shard_map.373 = (bf16[512,768]{1,0:T(8,128)(2,1)S(1)}, f32[16,768]{1,0:T(8,128)S(1)}, bf16[544,768]{1,0:T(8,128)(2,1)S(1)}, f32[544,768]{1,0:T(8,128)S(1)}, bf1...) custom-call(f32[544,768]{1,0:T(8,128)S(1)} %get-tuple-element.154.dfirs, ...), custom_call_target="tpu_custom_call" | custom-call | tf_op jit(solution)/shard_map/pallas_call | solution.py:66
  140.7 5.1 %shard_map.374 = (bf16[8,48,768]{2,1,0:T(8,128)(2,1)S(1)}, bf16[8,48,768]{2,1,0:T(8,128)(2,1)S(1)}, bf16[8,48,768]{2,1,0:T(8,128)(2,1)S(1)}, bf16[8,48,768]{2,1,0:T(8,128)(2,1)S(1)}) custom-call(s32[1]{0:T(128)} %bitcast.1.me_ref, bf16[544,768]{1,0:T(8,128)(2,1)S(1)} %get-tuple-element.159.refs_0_, bf16[544,768]{1,0:T(8,128)(2,1)S(1)} %get-tuple-element.160.refs_1_, ...), custom_call_target="tpu_custom_call" | custom-call | tf_op jit(solution)/shard_map/pallas_call | solution.py:66
  147.9 5.1 %shard_map.375 = (bf16[8,48,768]{2,1,0:T(8,128)(2,1)S(1)}, bf16[8,48,768]{2,1,0:T(8,128)(2,1)S(1)}, bf16[8,48,768]{2,1,0:T(8,128)(2,1)S(1)}, bf16[8,48,768]{2,1,0:T(8,128)(2,1)S(1)}) custom-call(s32[1]{0:T(128)} %bitcast.1.me_ref, bf16[544,768]{1,0:T(8,128)(2,1)S(1)} %get-tuple-element.164.refs_0_, bf16[544,768]{1,0:T(8,128)(2,1)S(1)} %get-tuple-element.165.refs_1_, ...), custom_call_target="tpu_custom_call" | custom-call | tf_op jit(solution)/shard_map/pallas_call | solution.py:66
  155.1 9.9 %shard_map.376 = (bf16[544,768]{1,0:T(8,128)(2,1)S(1)}, f32[544,768]{1,0:T(8,128)S(1)}, bf16[544,768]{1,0:T(8,128)(2,1)S(1)}, bf16[544,1152]{1,0:T(8,128)(2,1)S(...) custom-call(f32[544,768]{1,0:T(8,128)S(1)} %get-tuple-element.169.dsecond_ref, ...), custom_call_target="tpu_custom_call" | custom-call | tf_op jit(solution)/shard_map/pallas_call | solution.py:66
  167.6 6.4 %shard_map.378 = (bf16[8,48,768]{2,1,0:T(8,128)(2,1)S(1)}, bf16[8,48,768]{2,1,0:T(8,128)(2,1)S(1)}, bf16[8,48,768]{2,1,0:T(8,128)(2,1)S(1)}, bf16[8,48,768]{2,1,0:T(8,128)(2,1)S(1)}) custom-call(s32[1]{0:T(128)} %bitcast.1.me_ref, bf16[544,768]{1,0:T(8,128)(2,1)S(1)} %get-tuple-element.181.refs_0_, bf16[544,768]{1,0:T(8,128)(2,1)S(1)} %get-tuple-element.182.refs_1_, ...), custom_call_target="tpu_custom_call" | custom-call | tf_op jit(solution)/shard_map/pallas_call | solution.py:66
  175.2 5.2 %collective-permute-done.34 = bf16[4,48,768]{2,1,0:T(8,128)(2,1)S(1)} collective-permute-done((bf16[4,48,768]{2,1,0:T(8,128)(2,1)S(1)}, bf16[4,48,768]{2,1,0:T(8,128)(2,1)S(1)}, u32[]{:S(2)}, u32[]{:S(2)}) %collective-permute-start.34) | collective-permute-done | bytes 294944 | tf_op jit(solution)/shard_map/ppermute | solution.py:419
  182.4 2.1 collective-permute-start.37
  184.5 3.9 %collective-permute-start.35 = (bf16[48,1536]{1,0:T(8,128)(2,1)S(1)}, bf16[48,1536]{1,0:T(8,128)(2,1)S(1)}, u32[]{:S(2)}, u32[]{:S(2)}) collective-permute-start(bf16[48,1536]{1,0:T(8,128)(2,1)S(1)} %get-tuple-element.257), channel_id=1, source_target_pairs={{0,8},{2,10},{4,12},{6,14},{8,0},{10,2},{12,4},{14,6},{16,24},{18,... | collective-permute-start | bytes 442376 | tf_op jit(solution)/shard_map/ppermute | solution.py:419
  190.5 1.6 collective-permute-start.41
  192.6 6.3 %collective-permute-done.36.refs_2_ = bf16[48,1536]{1,0:T(8,128)(2,1)S(1)} collective-permute-done((bf16[48,1536]{1,0:T(8,128)(2,1)S(1)}, bf16[48,1536]{1,0:T(8,128)(2,1)S(1)}, u32[]{:S(2)}, u32[]{:S(2)}) %collective-permute-start.36) | collective-permute-done | bytes 147488 | tf_op jit(solution)/shard_map/ppermute | solution.py:419
  201.2 3.1 %collective-permute-done.40 = bf16[8,48,768]{2,1,0:T(8,128)(2,1)S(1)} collective-permute-done((bf16[8,48,768]{2,1,0:T(8,128)(2,1)S(1)}, bf16[8,48,768]{2,1,0:T(8,128)(2,1)S(1)}, u32[]{:S(2)}, u32[]{:S(2)}) %collective-permute-start.40) | collective-permute-done | bytes 589856 | tf_op jit(solution)/shard_map/ppermute | solution.py:419
  204.3 6.2 %collective-permute-done.38 = bf16[4,48,768]{2,1,0:T(8,128)(2,1)S(1)} collective-permute-done((bf16[4,48,768]{2,1,0:T(8,128)(2,1)S(1)}, bf16[4,48,768]{2,1,0:T(8,128)(2,1)S(1)}, u32[]{:S(2)}, u32[]{:S(2)}) %collective-permute-start.38) | collective-permute-done | bytes 294944 | tf_op jit(solution)/shard_map/ppermute | solution.py:419
  210.8 2.3 collective-permute-start.46
  213.2 2.1 collective-permute-start.44
  218.0 2.1 collective-permute-start.49
  222.0 5.4 %collective-permute-start.48 = (bf16[48,1536]{1,0:T(8,128)(2,1)S(1)}, bf16[48,1536]{1,0:T(8,128)(2,1)S(1)}, u32[]{:S(2)}, u32[]{:S(2)}) collective-permute-start(bf16[48,1536]{1,0:T(8,128)(2,1)S(1)} %get-tuple-element.250), channel_id=1, source_target_pairs={{0,16},{2,18},{4,20},{6,22},{8,24},{10,26},{12,28},{14,30},{16,0},... | collective-permute-start | bytes 442376 | tf_op jit(solution)/shard_map/ppermute | solution.py:419
  228.2 5.6 %collective-permute-done.43.refs_6_ = bf16[48,1536]{1,0:T(8,128)(2,1)S(1)} collective-permute-done((bf16[48,1536]{1,0:T(8,128)(2,1)S(1)}, bf16[48,1536]{1,0:T(8,128)(2,1)S(1)}, u32[]{:S(2)}, u32[]{:S(2)}) %collective-permute-start.43) | collective-permute-done | bytes 147488 | tf_op jit(solution)/shard_map/ppermute | solution.py:419
  233.8 5.3 %collective-permute-done.48.refs_10_ = bf16[48,1536]{1,0:T(8,128)(2,1)S(1)} collective-permute-done((bf16[48,1536]{1,0:T(8,128)(2,1)S(1)}, bf16[48,1536]{1,0:T(8,128)(2,1)S(1)}, u32[]{:S(2)}, u32[]{:S(2)}) %collective-permute-start.48) | collective-permute-done | bytes 147488 | tf_op jit(solution)/shard_map/ppermute | solution.py:419
  243.2 1.8 collective-permute-done.52
  246.0 2.1 collective-permute-start.55
  248.1 2.4 collective-permute-start.53
  252.3 1.6 collective-permute-done.54
  258.6 2.3 shard_map.380
  (194 shorter events, 57.0 us)
Async XLA Ops:
  3.4 14.6 %collective-permute-start.2 = (bf16[2,48,768]{2,1,0:T(8,128)(2,1)}, bf16[2,48,768]{2,1,0:T(8,128)(2,1)S(1)}, u32[]{:S(2)}, u32[]{:S(2)}) collective-permute-start(bf16[2,48,768]{2,1,0:T(8,128)(2,1)} %pad_maximum_fusion.10), channel_id=1, source_target_pairs={{0,24},{2,26},{4,28},{6,30},{8,16},{10,18},{12,20},{14,22},{16,8},... | collective-permute-start | bytes 442376 | tf_op jit(solution)/shard_map/ppermute | solution.py:419
  8.4 12.8 %collective-permute-start.1 = (bf16[2,48,768]{2,1,0:T(8,128)(2,1)}, bf16[2,48,768]{2,1,0:T(8,128)(2,1)}, u32[]{:S(2)}, u32[]{:S(2)}) collective-permute-start(bf16[2,48,768]{2,1,0:T(8,128)(2,1)} %pad_maximum_fusion.10), channel_id=1, source_target_pairs={{0,16},{2,18},{4,20},{6,22},{8,24},{10,26},{12,28},{14,30},{16,0},... | collective-permute-start | bytes 442376 | tf_op jit(solution)/shard_map/ppermute | solution.py:419
  8.4 12.8 %collective-permute-start = (bf16[2,48,768]{2,1,0:T(8,128)(2,1)}, bf16[2,48,768]{2,1,0:T(8,128)(2,1)}, u32[]{:S(2)}, u32[]{:S(2)}) collective-permute-start(bf16[2,48,768]{2,1,0:T(8,128)(2,1)} %pad_maximum_fusion.10), channel_id=1, source_target_pairs={{0,8},{2,10},{4,12},{6,14},{8,0},{10,2},{12,4},{14,6},{16,24},{18,... | collective-permute-start | bytes 442376 | tf_op jit(solution)/shard_map/ppermute | solution.py:419
  10.7 4.7 %collective-permute-start.16 = (bf16[48,768]{1,0:T(8,128)(2,1)}, bf16[48,768]{1,0:T(8,128)(2,1)}, u32[]{:S(2)}, u32[]{:S(2)}) collective-permute-start(bf16[48,768]{1,0:T(8,128)(2,1)} %get-tuple-element.269), channel_id=1, source_target_pairs={{0,4},{2,6},{4,0},{6,2},{8,12},{10,14},{12,8},{14,10},{16,20},{18,... | collective-permute-start | bytes 221192 | tf_op jit(solution)/shard_map/ppermute | solution.py:419
  21.2 9.6 %collective-permute-start.10 = (bf16[2,48,768]{2,1,0:T(8,128)(2,1)S(1)}, bf16[2,48,768]{2,1,0:T(8,128)(2,1)S(1)}, u32[]{:S(2)}, u32[]{:S(2)}) collective-permute-start(bf16[2,48,768]{2,1,0:T(8,128)(2,1)S(1)} %pad_maximum_fusion.11), channel_id=1, source_target_pairs={{0,24},{2,26},{4,28},{6,30},{8,16},{10,18},{12,20},{14,22},{16,8},... | collective-permute-start | bytes 442376 | tf_op jit(solution)/shard_map/ppermute | solution.py:419
  23.9 11.2 %collective-permute-start.9 = (bf16[2,48,768]{2,1,0:T(8,128)(2,1)S(1)}, bf16[2,48,768]{2,1,0:T(8,128)(2,1)S(1)}, u32[]{:S(2)}, u32[]{:S(2)}) collective-permute-start(bf16[2,48,768]{2,1,0:T(8,128)(2,1)S(1)} %pad_maximum_fusion.11), channel_id=1, source_target_pairs={{0,16},{2,18},{4,20},{6,22},{8,24},{10,26},{12,28},{14,30},{16,0},... | collective-permute-start | bytes 442376 | tf_op jit(solution)/shard_map/ppermute | solution.py:419
  23.9 14.5 %collective-permute-start.8 = (bf16[2,48,768]{2,1,0:T(8,128)(2,1)S(1)}, bf16[2,48,768]{2,1,0:T(8,128)(2,1)S(1)}, u32[]{:S(2)}, u32[]{:S(2)}) collective-permute-start(bf16[2,48,768]{2,1,0:T(8,128)(2,1)S(1)} %pad_maximum_fusion.11), channel_id=1, source_target_pairs={{0,8},{2,10},{4,12},{6,14},{8,0},{10,2},{12,4},{14,6},{16,24},{18,... | collective-permute-start | bytes 442376 | tf_op jit(solution)/shard_map/ppermute | solution.py:419
  27.6 9.2 %collective-permute-start.3 = (bf16[4,48,768]{2,1,0:T(8,128)(2,1)S(1)}, bf16[4,48,768]{2,1,0:T(8,128)(2,1)S(1)}, u32[]{:S(2)}, u32[]{:S(2)}) collective-permute-start(bf16[4,48,768]{2,1,0:T(8,128)(2,1)S(1)} %pad_maximum_fusion.3), channel_id=1, source_target_pairs={{0,4},{2,6},{4,0},{6,2},{8,12},{10,14},{12,8},{14,10},{16,20},{18,... | collective-permute-start | bytes 884744 | tf_op jit(solution)/shard_map/ppermute | solution.py:419
  29.2 7.0 %collective-permute-start.5 = (bf16[4,48,768]{2,1,0:T(8,128)(2,1)S(1)}, bf16[4,48,768]{2,1,0:T(8,128)(2,1)S(1)}, u32[]{:S(2)}, u32[]{:S(2)}) collective-permute-start(bf16[4,48,768]{2,1,0:T(8,128)(2,1)S(1)} %pad_maximum_fusion.4), channel_id=1, source_target_pairs={{0,2},{2,0},{4,6},{6,4},{8,10},{10,8},{12,14},{14,12},{16,18},{18,... | collective-permute-start | bytes 884744 | tf_op jit(solution)/shard_map/ppermute | solution.py:419
  36.2 13.6 %collective-permute-start.6 = (bf16[8,48,768]{2,1,0:T(8,128)(2,1)S(1)}, bf16[8,48,768]{2,1,0:T(8,128)(2,1)S(1)}, u32[]{:S(2)}, u32[]{:S(2)}) collective-permute-start(bf16[8,48,768]{2,1,0:T(8,128)(2,1)S(1)} %constant_dynamic-update-slice_fusion.5.refs_2_), channel_id=1, source_target_pairs={{0,4},{2,6},{4,0},{6,2},{8,12},{10,14},{12,8},{14,10},{16,20},{18,... | collective-permute-start | bytes 1769480 | tf_op jit(solution)/shard_map/ppermute | solution.py:419
  36.8 14.4 %collective-permute-start.4 = (bf16[8,48,768]{2,1,0:T(8,128)(2,1)S(1)}, bf16[8,48,768]{2,1,0:T(8,128)(2,1)S(1)}, u32[]{:S(2)}, u32[]{:S(2)}) collective-permute-start(bf16[8,48,768]{2,1,0:T(8,128)(2,1)S(1)} %constant_dynamic-update-slice_fusion.refs_0_), channel_id=1, source_target_pairs={{0,2},{2,0},{4,6},{6,4},{8,10},{10,8},{12,14},{14,12},{16,18},{18,... | collective-permute-start | bytes 1769480 | tf_op jit(solution)/shard_map/ppermute | solution.py:419
  38.5 14.2 %collective-permute-start.19 = (bf16[2,2,48,768]{3,2,1,0:T(8,128)(2,1)S(1)}, bf16[2,2,48,768]{3,2,1,0:T(8,128)(2,1)S(1)}, u32[]{:S(2)}, u32[]{:S(2)}) collective-permute-start(bf16[2,2,48,768]{3,2,1,0:T(8,128)(2,1)S(1)} %pad_maximum_fusion.7), channel_id=1, source_target_pairs={{0,24},{2,26},{4,28},{6,30},{8,16},{10,18},{12,20},{14,22},{16,8},... | collective-permute-start | bytes 884744 | tf_op jit(solution)/shard_map/ppermute | solution.py:419
  41.0 23.0 %collective-permute-start.18 = (bf16[2,2,48,768]{3,2,1,0:T(8,128)(2,1)S(1)}, bf16[2,2,48,768]{3,2,1,0:T(8,128)(2,1)S(1)}, u32[]{:S(2)}, u32[]{:S(2)}) collective-permute-start(bf16[2,2,48,768]{3,2,1,0:T(8,128)(2,1)S(1)} %pad_maximum_fusion.7), channel_id=1, source_target_pairs={{0,16},{2,18},{4,20},{6,22},{8,24},{10,26},{12,28},{14,30},{16,0},... | collective-permute-start | bytes 884744 | tf_op jit(solution)/shard_map/ppermute | solution.py:419
  41.1 22.9 %collective-permute-start.17 = (bf16[2,2,48,768]{3,2,1,0:T(8,128)(2,1)S(1)}, bf16[2,2,48,768]{3,2,1,0:T(8,128)(2,1)S(1)}, u32[]{:S(2)}, u32[]{:S(2)}) collective-permute-start(bf16[2,2,48,768]{3,2,1,0:T(8,128)(2,1)S(1)} %pad_maximum_fusion.7), channel_id=1, source_target_pairs={{0,8},{2,10},{4,12},{6,14},{8,0},{10,2},{12,4},{14,6},{16,24},{18,... | collective-permute-start | bytes 884744 | tf_op jit(solution)/shard_map/ppermute | solution.py:419
  51.2 7.1 %collective-permute-start.13 = (bf16[4,48,768]{2,1,0:T(8,128)(2,1)S(1)}, bf16[4,48,768]{2,1,0:T(8,128)(2,1)S(1)}, u32[]{:S(2)}, u32[]{:S(2)}) collective-permute-start(bf16[4,48,768]{2,1,0:T(8,128)(2,1)S(1)} %pad_maximum_fusion.6), channel_id=1, source_target_pairs={{0,2},{2,0},{4,6},{6,4},{8,10},{10,8},{12,14},{14,12},{16,18},{18,... | collective-permute-start | bytes 884744 | tf_op jit(solution)/shard_map/ppermute | solution.py:419
  52.7 8.2 %collective-permute-start.11 = (bf16[4,48,768]{2,1,0:T(8,128)(2,1)S(1)}, bf16[4,48,768]{2,1,0:T(8,128)(2,1)S(1)}, u32[]{:S(2)}, u32[]{:S(2)}) collective-permute-start(bf16[4,48,768]{2,1,0:T(8,128)(2,1)S(1)} %pad_maximum_fusion.5), channel_id=1, source_target_pairs={{0,4},{2,6},{4,0},{6,2},{8,12},{10,14},{12,8},{14,10},{16,20},{18,... | collective-permute-start | bytes 884744 | tf_op jit(solution)/shard_map/ppermute | solution.py:419
  58.3 13.9 %collective-permute-start.14 = (bf16[8,48,768]{2,1,0:T(8,128)(2,1)S(1)}, bf16[8,48,768]{2,1,0:T(8,128)(2,1)S(1)}, u32[]{:S(2)}, u32[]{:S(2)}) collective-permute-start(bf16[8,48,768]{2,1,0:T(8,128)(2,1)S(1)} %constant_dynamic-update-slice_fusion.12.refs_2_), channel_id=1, source_target_pairs={{0,4},{2,6},{4,0},{6,2},{8,12},{10,14},{12,8},{14,10},{16,20},{18,... | collective-permute-start | bytes 1769480 | tf_op jit(solution)/shard_map/ppermute | solution.py:419
  60.9 11.3 %collective-permute-start.12 = (bf16[8,48,768]{2,1,0:T(8,128)(2,1)S(1)}, bf16[8,48,768]{2,1,0:T(8,128)(2,1)S(1)}, u32[]{:S(2)}, u32[]{:S(2)}) collective-permute-start(bf16[8,48,768]{2,1,0:T(8,128)(2,1)S(1)} %constant_dynamic-update-slice_fusion.10.refs_0_), channel_id=1, source_target_pairs={{0,2},{2,0},{4,6},{6,4},{8,10},{10,8},{12,14},{14,12},{16,18},{18,... | collective-permute-start | bytes 1769480 | tf_op jit(solution)/shard_map/ppermute | solution.py:419
  71.7 16.5 %collective-permute-start.7 = (bf16[544,768]{1,0:T(8,128)(2,1)S(1)}, bf16[544,768]{1,0:T(8,128)(2,1)S(1)}, u32[]{:S(2)}, u32[]{:S(2)}) collective-permute-start(bf16[544,768]{1,0:T(8,128)(2,1)S(1)} %get-tuple-element.134.own_ref), channel_id=1, source_target_pairs={{0,1},{1,0},{2,3},{3,2},{4,5},{5,4},{6,7},{7,6},{8,9},{9,8},{10,11... | collective-permute-start | bytes 2506760 | tf_op jit(solution)/shard_map/ppermute | solution.py:419
  72.2 15.6 %collective-permute-start.20 = (bf16[8,48,768]{2,1,0:T(8,128)(2,1)S(1)}, bf16[8,48,768]{2,1,0:T(8,128)(2,1)S(1)}, u32[]{:S(2)}, u32[]{:S(2)}) collective-permute-start(bf16[8,48,768]{2,1,0:T(8,128)(2,1)S(1)} %pad_maximum_fusion.1.refs_0_), channel_id=1, source_target_pairs={{0,4},{2,6},{4,0},{6,2},{8,12},{10,14},{12,8},{14,10},{16,20},{18,... | collective-permute-start | bytes 1769480 | tf_op jit(solution)/shard_map/ppermute | solution.py:419
  72.7 15.3 %collective-permute-start.21 = (bf16[8,48,768]{2,1,0:T(8,128)(2,1)S(1)}, bf16[8,48,768]{2,1,0:T(8,128)(2,1)S(1)}, u32[]{:S(2)}, u32[]{:S(2)}) collective-permute-start(bf16[8,48,768]{2,1,0:T(8,128)(2,1)S(1)} %pad_maximum_fusion.2.refs_2_), channel_id=1, source_target_pairs={{0,2},{2,0},{4,6},{6,4},{8,10},{10,8},{12,14},{14,12},{16,18},{18,... | collective-permute-start | bytes 1769480 | tf_op jit(solution)/shard_map/ppermute | solution.py:419
  140.4 14.7 %collective-permute-start.27 = (bf16[544,768]{1,0:T(8,128)(2,1)S(1)}, bf16[544,768]{1,0:T(8,128)(2,1)S(1)}, u32[]{:S(2)}, u32[]{:S(2)}) collective-permute-start(bf16[544,768]{1,0:T(8,128)(2,1)S(1)} %get-tuple-element.170.own_ref), channel_id=1, source_target_pairs={{0,1},{1,0},{2,3},{3,2},{4,5},{5,4},{6,7},{7,6},{8,9},{9,8},{10,11... | collective-permute-start | bytes 2506760 | tf_op jit(solution)/shard_map/ppermute | solution.py:419
  145.8 19.3 %collective-permute-start.29 = (bf16[8,48,768]{2,1,0:T(8,128)(2,1)S(1)}, bf16[8,48,768]{2,1,0:T(8,128)(2,1)S(1)}, u32[]{:S(2)}, u32[]{:S(2)}) collective-permute-start(bf16[8,48,768]{2,1,0:T(8,128)(2,1)S(1)} %get-tuple-element.178), channel_id=1, source_target_pairs={{0,2},{2,0},{4,6},{6,4},{8,10},{10,8},{12,14},{14,12},{16,18},{18,... | collective-permute-start | bytes 1769480 | tf_op jit(solution)/shard_map/ppermute | solution.py:419
  146.4 18.8 %collective-permute-start.31 = (bf16[8,48,768]{2,1,0:T(8,128)(2,1)S(1)}, bf16[8,48,768]{2,1,0:T(8,128)(2,1)S(1)}, u32[]{:S(2)}, u32[]{:S(2)}) collective-permute-start(bf16[8,48,768]{2,1,0:T(8,128)(2,1)S(1)} %get-tuple-element.184), channel_id=1, source_target_pairs={{0,4},{2,6},{4,0},{6,2},{8,12},{10,14},{12,8},{14,10},{16,20},{18,... | collective-permute-start | bytes 1769480 | tf_op jit(solution)/shard_map/ppermute | solution.py:419
  153.0 21.6 %collective-permute-start.32 = (bf16[8,48,768]{2,1,0:T(8,128)(2,1)S(1)}, bf16[8,48,768]{2,1,0:T(8,128)(2,1)S(1)}, u32[]{:S(2)}, u32[]{:S(2)}) collective-permute-start(bf16[8,48,768]{2,1,0:T(8,128)(2,1)S(1)} %get-tuple-element.193), channel_id=1, source_target_pairs={{0,2},{2,0},{4,6},{6,4},{8,10},{10,8},{12,14},{14,12},{16,18},{18,... | collective-permute-start | bytes 1769480 | tf_op jit(solution)/shard_map/ppermute | solution.py:419
  154.6 20.6 %collective-permute-start.33 = (bf16[8,48,768]{2,1,0:T(8,128)(2,1)S(1)}, bf16[8,48,768]{2,1,0:T(8,128)(2,1)S(1)}, u32[]{:S(2)}, u32[]{:S(2)}) collective-permute-start(bf16[8,48,768]{2,1,0:T(8,128)(2,1)S(1)} %get-tuple-element.194), channel_id=1, source_target_pairs={{0,4},{2,6},{4,0},{6,2},{8,12},{10,14},{12,8},{14,10},{16,20},{18,... | collective-permute-start | bytes 1769480 | tf_op jit(solution)/shard_map/ppermute | solution.py:419
  165.4 15.0 %collective-permute-start.34 = (bf16[4,48,768]{2,1,0:T(8,128)(2,1)S(1)}, bf16[4,48,768]{2,1,0:T(8,128)(2,1)S(1)}, u32[]{:S(2)}, u32[]{:S(2)}) collective-permute-start(bf16[4,48,768]{2,1,0:T(8,128)(2,1)S(1)} %slice.265), channel_id=1, source_target_pairs={{0,2},{2,0},{4,6},{6,4},{8,10},{10,8},{12,14},{14,12},{16,18},{18,... | collective-permute-start | bytes 884744 | tf_op jit(solution)/shard_map/ppermute | solution.py:419
  166.0 14.6 %collective-permute-start.30 = (bf16[4,48,768]{2,1,0:T(8,128)(2,1)S(1)}, bf16[4,48,768]{2,1,0:T(8,128)(2,1)S(1)}, u32[]{:S(2)}, u32[]{:S(2)}) collective-permute-start(bf16[4,48,768]{2,1,0:T(8,128)(2,1)S(1)} %slice.264), channel_id=1, source_target_pairs={{0,4},{2,6},{4,0},{6,2},{8,12},{10,14},{12,8},{14,10},{16,20},{18,... | collective-permute-start | bytes 884744 | tf_op jit(solution)/shard_map/ppermute | solution.py:419
  180.8 19.6 %collective-permute-start.39 = (bf16[8,48,768]{2,1,0:T(8,128)(2,1)S(1)}, bf16[8,48,768]{2,1,0:T(8,128)(2,1)S(1)}, u32[]{:S(2)}, u32[]{:S(2)}) collective-permute-start(bf16[8,48,768]{2,1,0:T(8,128)(2,1)S(1)} %get-tuple-element.200), channel_id=1, source_target_pairs={{0,2},{2,0},{4,6},{6,4},{8,10},{10,8},{12,14},{14,12},{16,18},{18,... | collective-permute-start | bytes 1769480 | tf_op jit(solution)/shard_map/ppermute | solution.py:419
  182.4 8.1 %collective-permute-start.37 = (bf16[48,1536]{1,0:T(8,128)(2,1)S(1)}, bf16[48,1536]{1,0:T(8,128)(2,1)S(1)}, u32[]{:S(2)}, u32[]{:S(2)}) collective-permute-start(bf16[48,1536]{1,0:T(8,128)(2,1)S(1)} %get-tuple-element.255), channel_id=1, source_target_pairs={{0,24},{2,26},{4,28},{6,30},{8,16},{10,18},{12,20},{14,22},{16,8},... | collective-permute-start | bytes 442376 | tf_op jit(solution)/shard_map/ppermute | solution.py:419
  184.5 8.1 %collective-permute-start.35 = (bf16[48,1536]{1,0:T(8,128)(2,1)S(1)}, bf16[48,1536]{1,0:T(8,128)(2,1)S(1)}, u32[]{:S(2)}, u32[]{:S(2)}) collective-permute-start(bf16[48,1536]{1,0:T(8,128)(2,1)S(1)} %get-tuple-element.257), channel_id=1, source_target_pairs={{0,8},{2,10},{4,12},{6,14},{8,0},{10,2},{12,4},{14,6},{16,24},{18,... | collective-permute-start | bytes 442376 | tf_op jit(solution)/shard_map/ppermute | solution.py:419
  188.5 10.4 %collective-permute-start.36 = (bf16[48,1536]{1,0:T(8,128)(2,1)S(1)}, bf16[48,1536]{1,0:T(8,128)(2,1)S(1)}, u32[]{:S(2)}, u32[]{:S(2)}) collective-permute-start(bf16[48,1536]{1,0:T(8,128)(2,1)S(1)} %get-tuple-element.258), channel_id=1, source_target_pairs={{0,16},{2,18},{4,20},{6,22},{8,24},{10,26},{12,28},{14,30},{16,0},... | collective-permute-start | bytes 442376 | tf_op jit(solution)/shard_map/ppermute | solution.py:419
  188.8 15.5 %collective-permute-start.40 = (bf16[8,48,768]{2,1,0:T(8,128)(2,1)S(1)}, bf16[8,48,768]{2,1,0:T(8,128)(2,1)S(1)}, u32[]{:S(2)}, u32[]{:S(2)}) collective-permute-start(bf16[8,48,768]{2,1,0:T(8,128)(2,1)S(1)} %get-tuple-element.202), channel_id=1, source_target_pairs={{0,4},{2,6},{4,0},{6,2},{8,12},{10,14},{12,8},{14,10},{16,20},{18,... | collective-permute-start | bytes 1769480 | tf_op jit(solution)/shard_map/ppermute | solution.py:419
  190.5 13.8 %collective-permute-start.41 = (bf16[4,48,768]{2,1,0:T(8,128)(2,1)S(1)}, bf16[4,48,768]{2,1,0:T(8,128)(2,1)S(1)}, u32[]{:S(2)}, u32[]{:S(2)}) collective-permute-start(bf16[4,48,768]{2,1,0:T(8,128)(2,1)S(1)} %slice.278), channel_id=1, source_target_pairs={{0,2},{2,0},{4,6},{6,4},{8,10},{10,8},{12,14},{14,12},{16,18},{18,... | collective-permute-start | bytes 884744 | tf_op jit(solution)/shard_map/ppermute | solution.py:419
  192.6 27.5 %collective-permute-start.28 = (bf16[544,768]{1,0:T(8,128)(2,1)S(1)}, bf16[544,768]{1,0:T(8,128)(2,1)S(1)}, u32[]{:S(2)}, u32[]{:S(2)}) collective-permute-start(bf16[544,768]{1,0:T(8,128)(2,1)S(1)} %get-tuple-element.174.own_ref), channel_id=1, source_target_pairs={{0,1},{1,0},{2,3},{3,2},{4,5},{5,4},{6,7},{7,6},{8,9},{9,8},{10,11... | collective-permute-start | bytes 2506760 | tf_op jit(solution)/shard_map/ppermute | solution.py:419
  198.9 11.7 %collective-permute-start.38 = (bf16[4,48,768]{2,1,0:T(8,128)(2,1)S(1)}, bf16[4,48,768]{2,1,0:T(8,128)(2,1)S(1)}, u32[]{:S(2)}, u32[]{:S(2)}) collective-permute-start(bf16[4,48,768]{2,1,0:T(8,128)(2,1)S(1)} %slice.276), channel_id=1, source_target_pairs={{0,4},{2,6},{4,0},{6,2},{8,12},{10,14},{12,8},{14,10},{16,20},{18,... | collective-permute-start | bytes 884744 | tf_op jit(solution)/shard_map/ppermute | solution.py:419
  200.6 15.8 %collective-permute-start.45 = (bf16[4,48,768]{2,1,0:T(8,128)(2,1)S(1)}, bf16[4,48,768]{2,1,0:T(8,128)(2,1)S(1)}, u32[]{:S(2)}, u32[]{:S(2)}) collective-permute-start(bf16[4,48,768]{2,1,0:T(8,128)(2,1)S(1)} %slice.286), channel_id=1, source_target_pairs={{0,4},{2,6},{4,0},{6,2},{8,12},{10,14},{12,8},{14,10},{16,20},{18,... | collective-permute-start | bytes 884744 | tf_op jit(solution)/shard_map/ppermute | solution.py:419
  210.8 7.0 %collective-permute-start.46 = (bf16[4,48,768]{2,1,0:T(8,128)(2,1)S(1)}, bf16[4,48,768]{2,1,0:T(8,128)(2,1)S(1)}, u32[]{:S(2)}, u32[]{:S(2)}) collective-permute-start(bf16[4,48,768]{2,1,0:T(8,128)(2,1)S(1)} %slice.288), channel_id=1, source_target_pairs={{0,2},{2,0},{4,6},{6,4},{8,10},{10,8},{12,14},{14,12},{16,18},{18,... | collective-permute-start | bytes 884744 | tf_op jit(solution)/shard_map/ppermute | solution.py:419
  213.2 8.8 %collective-permute-start.44 = (bf16[48,1536]{1,0:T(8,128)(2,1)S(1)}, bf16[48,1536]{1,0:T(8,128)(2,1)S(1)}, u32[]{:S(2)}, u32[]{:S(2)}) collective-permute-start(bf16[48,1536]{1,0:T(8,128)(2,1)S(1)} %get-tuple-element.251), channel_id=1, source_target_pairs={{0,24},{2,26},{4,28},{6,30},{8,16},{10,18},{12,20},{14,22},{16,8},... | collective-permute-start | bytes 442376 | tf_op jit(solution)/shard_map/ppermute | solution.py:419
  215.3 12.8 %collective-permute-start.42 = (bf16[48,1536]{1,0:T(8,128)(2,1)S(1)}, bf16[48,1536]{1,0:T(8,128)(2,1)S(1)}, u32[]{:S(2)}, u32[]{:S(2)}) collective-permute-start(bf16[48,1536]{1,0:T(8,128)(2,1)S(1)} %get-tuple-element.253), channel_id=1, source_target_pairs={{0,8},{2,10},{4,12},{6,14},{8,0},{10,2},{12,4},{14,6},{16,24},{18,... | collective-permute-start | bytes 442376 | tf_op jit(solution)/shard_map/ppermute | solution.py:419
  216.5 17.3 %collective-permute-start.43 = (bf16[48,1536]{1,0:T(8,128)(2,1)S(1)}, bf16[48,1536]{1,0:T(8,128)(2,1)S(1)}, u32[]{:S(2)}, u32[]{:S(2)}) collective-permute-start(bf16[48,1536]{1,0:T(8,128)(2,1)S(1)} %get-tuple-element.254), channel_id=1, source_target_pairs={{0,16},{2,18},{4,20},{6,22},{8,24},{10,26},{12,28},{14,30},{16,0},... | collective-permute-start | bytes 442376 | tf_op jit(solution)/shard_map/ppermute | solution.py:419
  218.0 15.8 %collective-permute-start.49 = (bf16[48,1536]{1,0:T(8,128)(2,1)S(1)}, bf16[48,1536]{1,0:T(8,128)(2,1)S(1)}, u32[]{:S(2)}, u32[]{:S(2)}) collective-permute-start(bf16[48,1536]{1,0:T(8,128)(2,1)S(1)} %get-tuple-element.247), channel_id=1, source_target_pairs={{0,24},{2,26},{4,28},{6,30},{8,16},{10,18},{12,20},{14,22},{16,8},... | collective-permute-start | bytes 442376 | tf_op jit(solution)/shard_map/ppermute | solution.py:419
  220.1 13.7 %collective-permute-start.47 = (bf16[48,1536]{1,0:T(8,128)(2,1)S(1)}, bf16[48,1536]{1,0:T(8,128)(2,1)S(1)}, u32[]{:S(2)}, u32[]{:S(2)}) collective-permute-start(bf16[48,1536]{1,0:T(8,128)(2,1)S(1)} %get-tuple-element.249), channel_id=1, source_target_pairs={{0,8},{2,10},{4,12},{6,14},{8,0},{10,2},{12,4},{14,6},{16,24},{18,... | collective-permute-start | bytes 442376 | tf_op jit(solution)/shard_map/ppermute | solution.py:419
  222.0 17.1 %collective-permute-start.48 = (bf16[48,1536]{1,0:T(8,128)(2,1)S(1)}, bf16[48,1536]{1,0:T(8,128)(2,1)S(1)}, u32[]{:S(2)}, u32[]{:S(2)}) collective-permute-start(bf16[48,1536]{1,0:T(8,128)(2,1)S(1)} %get-tuple-element.250), channel_id=1, source_target_pairs={{0,16},{2,18},{4,20},{6,22},{8,24},{10,26},{12,28},{14,30},{16,0},... | collective-permute-start | bytes 442376 | tf_op jit(solution)/shard_map/ppermute | solution.py:419
  239.6 5.3 %collective-permute-start.52 = (f32[24,768]{1,0:T(8,128)S(1)}, f32[24,768]{1,0:T(8,128)S(1)}, u32[]{:S(2)}, u32[]{:S(2)}) collective-permute-start(f32[24,768]{1,0:T(8,128)S(1)} %get-tuple-element.220), channel_id=1, source_target_pairs={{0,6},{2,4},{4,2},{6,0},{8,14},{10,12},{12,10},{14,8},{16,22},{18,... | collective-permute-start | bytes 221192 | tf_op jit(solution)/shard_map/ppermute | solution.py:419
  246.0 6.2 %collective-permute-start.55 = (f32[24,768]{1,0:T(8,128)S(1)}, f32[24,768]{1,0:T(8,128)S(1)}, u32[]{:S(2)}, u32[]{:S(2)}) collective-permute-start(f32[24,768]{1,0:T(8,128)S(1)} %add_add_fusion.1), channel_id=1, source_target_pairs={{0,24},{2,26},{4,28},{6,30},{8,16},{10,18},{12,20},{14,22},{16,8},... | collective-permute-start | bytes 221192 | tf_op jit(solution)/shard_map/ppermute | solution.py:419
  248.1 5.7 %collective-permute-start.54 = (f32[24,768]{1,0:T(8,128)S(1)}, f32[24,768]{1,0:T(8,128)S(1)}, u32[]{:S(2)}, u32[]{:S(2)}) collective-permute-start(f32[24,768]{1,0:T(8,128)S(1)} %add_add_fusion.1), channel_id=1, source_target_pairs={{0,16},{2,18},{4,20},{6,22},{8,24},{10,26},{12,28},{14,30},{16,0},... | collective-permute-start | bytes 221192 | tf_op jit(solution)/shard_map/ppermute | solution.py:419
  248.1 5.7 %collective-permute-start.53 = (f32[24,768]{1,0:T(8,128)S(1)}, f32[24,768]{1,0:T(8,128)S(1)}, u32[]{:S(2)}, u32[]{:S(2)}) collective-permute-start(f32[24,768]{1,0:T(8,128)S(1)} %add_add_fusion.1), channel_id=1, source_target_pairs={{0,8},{2,10},{4,12},{6,14},{8,0},{10,2},{12,4},{14,6},{16,24},{18,... | collective-permute-start | bytes 221192 | tf_op jit(solution)/shard_map/ppermute | solution.py:419
  (30 other events, 89.6 us)

commit v2 on v1

--- a/solution.py
+++ b/solution.py
@@ -237,31 +237,36 @@
     part_ref[...] = dot_nt(du_ref[...], up_ref[...]).astype(BF)
 
 
-def ffn_last_kernel(first_ref, own_ref, other_ref, cot_ref, dmem_ref, alive_ref, shared_ref, up_ref, down_ref, slope_ref,
-                    out_ref, *outs):
+def ffn_last_kernel(before, *refs):
+    first_ref, own_ref, other_ref, cot_ref, dmem_ref, alive_ref, shared_ref, up_ref, down_ref, slope_ref, out_ref, *outs = refs[before:]
+    for slot in range(before):
+        out_ref[slot] = refs[slot][...]
     second = close_rows(first_ref, own_ref, other_ref, shared_ref)
     unit, unused = norm_stats(second)
     result = unit * shared_ref[USED + 4 : USED + 5, :] + shared_ref[USED + 5 : USED + 6, :]
-    out_ref[...] = (result[: out_ref.shape[0]] * alive_ref[...]).astype(BF)
+    out_ref[before] = (result[: out_ref.shape[1]] * alive_ref[...]).astype(BF)
     ffn_backward_rows(second, dmem_ref[...], cot_ref, alive_ref, shared_ref, up_ref, down_ref, slope_ref, *outs)
 
 
-def input_rows(dfirst_ref, own_ref, other_ref, grad_ref, live, keep):
-    seg = grad_ref.shape[0]
+def input_rows(dfirst_ref, own_ref, other_ref, grad_ref, here, live, keep):
+    seg = grad_ref.shape[-2]
     dx = dfirst_ref[...] + (own_ref[...].astype(F32) + other_ref[...].astype(F32))
-    grad_ref[...] = (dx[:seg] * live).astype(BF)
+    grad_ref[here] = (dx[:seg] * live).astype(BF)
     return jnp.where(live > 0.0, dx[seg : seg + PAD] + dx[seg + PAD :], keep)
 
 
 def ffn_before_kernel(dfirst_ref, own_ref, other_ref, live_ref, keep_ref, second_ref, cot_ref, alive_ref, shared_ref, up_ref, down_ref,
                       slope_ref, grad_ref, dmem_ref, *outs):
-    dmem = input_rows(dfirst_ref, own_ref, other_ref, grad_ref, live_ref[...], keep_ref[...])
+    dmem = input_rows(dfirst_ref, own_ref, other_ref, grad_ref, ..., live_ref[...], keep_ref[...])
     dmem_ref[...] = dmem
     ffn_backward_rows(second_ref[...], dmem, cot_ref, alive_ref, shared_ref, up_ref, down_ref, slope_ref, *outs)
 
 
-def input_grad_kernel(dfirst_ref, own_ref, other_ref, live_ref, keep_ref, grad_ref, dmem_ref):
-    dmem_ref[...] = input_rows(dfirst_ref, own_ref, other_ref, grad_ref, live_ref[...], keep_ref[...])
+def input_grad_kernel(dfirst_ref, own_ref, other_ref, live_ref, keep_ref, *refs):
+    *later, grad_ref, dmem_ref = refs
+    for slot, ref in enumerate(later):
+        grad_ref[slot + 1] = ref[...]
+    dmem_ref[...] = input_rows(dfirst_ref, own_ref, other_ref, grad_ref, 0, live_ref[...], keep_ref[...])
 
 
 def attn_backward_kernel(dsecond_ref, own_ref, other_ref, first_ref, shared_ref, qk_ref, vo_ref, qkv_ref, lse_ref,
@@ -354,13 +359,17 @@
     small[at:, :] = jnp.broadcast_to(squares, (small.shape[0] - at, model))
 
 
-def adam_kernel(plan, small_ref, own_ref, other_ref, *refs):
+def adam_kernel(plan, small_ref, other_ref, *refs):
     count = len(plan)
     grads = refs[:3]
     olds, news = refs[3 : 3 + 3 * count], refs[4 + 3 * count :]
     norm_ref = refs[3 + 3 * count]
     shared = small_ref[: USED + 6, :]
-    norm = jnp.sqrt((own_ref[:1, :1] + other_ref[:1, :1]) + jnp.sum(shared * shared, keepdims=True))
+    halves = []
+    for ref in (small_ref, other_ref):
+        biases = ref[USED + 6 : USED + 9, :]
+        halves.append(ref[USED + 9 : USED + 10, :1] + jnp.sum(biases * biases, keepdims=True))
+    norm = jnp.sqrt((halves[0] + halves[1]) + jnp.sum(shared * shared, keepdims=True))
     norm_ref[...] = norm
     factor = CLIP_NORM / jnp.maximum(norm, CLIP_NORM)
     for number, (source, row, column, rate, decay) in enumerate(plan):
@@ -386,7 +395,16 @@
             news[3 * number + 2][here + (...,)] = second
 
 
-def weight_grad_kernel(plan, kinds, sizes, me_ref, *refs):
+def weight_start_kernel(left_ref, right_ref, total_ref):
+    def rows_of(step, carry):
+        begin = pl.multiple_of(step * CHUNK, CHUNK)
+        total_ref[pl.ds(begin, CHUNK), :] = dot_tn(left_ref[:, pl.ds(begin, CHUNK)], right_ref[...])
+        return carry
+
+    lax.fori_loop(0, total_ref.shape[0] // CHUNK, rows_of, 0)
+
+
+def weight_grad_kernel(plan, kinds, sizes, base, me_ref, *refs):
     count = len(kinds) * len(sizes)
     outs = refs[-count - 1 : -1]
     total_ref = refs[-1]
@@ -397,7 +415,7 @@
 
             def rows_of(step, carry, left=left, right=right, start=start, size=size, at=at):
                 begin = pl.multiple_of(step * CHUNK, CHUNK)
-                total = None
+                total = None if base is None else refs[base][pl.ds(begin, CHUNK), start : start + size]
                 for one, two in zip(left, right):
                     add = dot_tn(refs[one][:, pl.ds(begin, CHUNK)], refs[two][:, start : start + size])
                     total = add if total is None else total + add
@@ -577,15 +595,16 @@
 
     count = segments
 
-    def weight_grad(names, plan, kinds):
+    def weight_grad(names, plan, kinds, base=None):
         sizes = (8, 8)
-        operands = [stacks[s][n] for n in names for s in range(count)]
-        at = {n: [i * count + s for s in range(count)] for i, n in enumerate(names)}
+        slots = range(count) if base is None else (0,)
+        operands = [stacks[s][n] for n in names for s in slots]
+        at = {n: [i * len(slots) + j for j in range(len(slots))] for i, n in enumerate(names)}
         steps = [[(at[a], at[b], start, length) for a, b, start, length in pieces] for pieces in plan]
         result = call(
-            functools.partial(weight_grad_kernel, steps, kinds, sizes),
+            functools.partial(weight_grad_kernel, steps, kinds, sizes, None if base is None else len(operands)),
             [((length, model // SLOTS, model), BF) for kind in kinds for length in sizes],
-            [me, *operands],
+            [me, *operands] + ([] if base is None else [base]),
             scalars=1,
             scratch=[pltpu.VMEM((model, model), F32)],
         )
@@ -594,18 +613,17 @@
     dmem = jnp.zeros((pad, model), F32)
     grads = [None] * segments
     stacks = [None] * segments
-    smalls = []
+    smalls, base = [], None
     ffn_outs = [((rows, model), BF), ((rows, model), F32), ((rows, model), BF), ((rows, hidden), BF), ((1, hidden), F32), ((8, model), F32)]
     for slot in reversed(range(segments)):
         low, qkv, lse, ctx, first_in, h_low, active, slope = saved[slot][:8]
         weights = [alive[slot], shared_params, w_up, w_down, slope]
         if slot == segments - 1:
-            out_rows, part, dsecond, df_low, du, dbias, dvec_two = call(
-                ffn_last_kernel,
-                [((seg, model), BF)] + ffn_outs,
-                [first_in, ffn_part, other, cotangent[0, slot], dmem, *weights],
+            outputs, part, dsecond, df_low, du, dbias, dvec_two = call(
+                functools.partial(ffn_last_kernel, slot),
+                [((segments, seg, model), BF)] + ffn_outs,
+                [*tokens_out, first_in, ffn_part, other, cotangent[0, slot], dmem, *weights],
             )
-            tokens_out.append(out_rows)
         else:
             grads[slot + 1], dmem, part, dsecond, df_low, du, dbias, dvec_two = call(
                 ffn_before_kernel,
@@ -615,9 +633,12 @@
         other = exchange(part, "head", pair, 1)
         stacks[slot] = (low, ctx, h_low, active, df_low, du)
         if slot == 0:
-            dw_down = weight_grad((DF_LOW, ACTIVE), [[(DF_LOW, ACTIVE, 0, half)], [(DF_LOW, ACTIVE, half, half)]], z_first)
+            dw_down = weight_grad((DF_LOW, ACTIVE), [[(DF_LOW, ACTIVE, 0, half)], [(DF_LOW, ACTIVE, half, half)]], z_first, base)
             dw_up = weight_grad((H_LOW, DU), [[(H_LOW, DU, 0, half)], [(H_LOW, DU, half, half)]], z_first)
             dsecond = after(dsecond, dw_down[0][0], dw_up[0][0])
+        elif segments == 2:
+            (base,) = call(weight_start_kernel, [((model, hidden), F32)], [df_low, active])
+            dsecond = after(dsecond, base)
         part, dfirst, da, dqkv, dhead, dvec_one = call(
             attn_backward_kernel,
             [((rows, model), BF), ((rows, model), F32), ((rows, model), BF), ((rows, 3 * width), BF), ((1, 2 * width), F32), ((8, model), F32)],
@@ -627,13 +648,11 @@
         other = exchange(part, "head", pair, 1)
         stacks[slot] += (da, dqkv)
         smalls += [dvec_one, dvec_two, dhead, dbias]
-    grads[0], dmem = call(
+    input_grad, dmem = call(
         input_grad_kernel,
-        [((seg, model), BF), ((pad, model), F32)],
-        [dfirst, part, other, alive[0], dmem],
+        [((segments, seg, model), BF), ((pad, model), F32)],
+        [dfirst, part, other, alive[0], dmem, *grads[1:]],
     )
-    outputs = jnp.stack(tokens_out)[None]
-    input_grad = jnp.stack(grads)[None]
 
     def fallback(parts, kinds):
         full = [canonical_join(p, kind) for p, kind in zip(parts, kinds)]
@@ -653,24 +672,27 @@
     if size == SLOTS:
         got_down, got_up = hop([p[1] for p in dw_down], x_first), hop([p[1] for p in dw_up], x_first)
         down = add_halves([p[0] for p in dw_down], [after(g, stacks[0][DQKV]) for g in got_down])
-        stacks[0] = stacks[0][:DQKV] + (after(stacks[0][DQKV], *down),)
         got_down = hop([v[4:] for v in down], y_first)
+        up = add_halves([p[0] for p in dw_up], [after(g, *down) for g in got_up])
+        stacks[0] = stacks[0][:DQKV] + (after(stacks[0][DQKV], *up),)
+        got_up = hop([v[4:] for v in up], y_first)
     dw_qkvo = weight_grad(
         (LOW, DQKV, DA, CTX),
         [[(LOW, DQKV, 0, 2 * width)], [(LOW, DQKV, 2 * width, width), (DA, CTX, 0, width)]],
         z_first,
     )
     if size == SLOTS:
-        dw_qkvo = [[after(v, *got_up, *got_down) for v in part] for part in dw_qkvo]
+        got_down = [after(g, dw_qkvo[0][0]) for g in got_down]
+        down = jnp.concatenate(add_halves([v[:4] for v in down], got_down), axis=2)
+        got_down = line_hop(down)
+        dw_qkvo = [[after(v, *got_up) for v in part] for part in dw_qkvo]
         got_qkvo = hop([p[1] for p in dw_qkvo], x_first)
-        down = jnp.concatenate(add_halves([v[:4] for v in down], [after(g, dw_qkvo[0][0]) for g in got_down]), axis=2)
-        got_down = line_hop(down)
-        up = add_halves([p[0] for p in dw_up], [after(g, down) for g in got_up])
-        got_up = hop([v[4:] for v in up], y_first)
-        last = add_halves([p[0] for p in dw_qkvo], [after(g, *got_down) for g in got_qkvo])
-        up = jnp.concatenate(add_halves([v[:4] for v in up], [after(g, *got_qkvo) for g in got_up]), axis=2)
-        last = jnp.concatenate(add_halves([v[:4] for v in last], hop([v[4:] for v in last], y_first)), axis=2)
-        sums = [[down[0], *got_down], [up[0], *line_hop(up)], [last[0], *line_hop(last)]]
+        up = jnp.concatenate(add_halves([v[:4] for v in up], got_up), axis=2)
+        got_up = line_hop(up)
+        last = add_halves([p[0] for p in dw_qkvo], [after(g, *got_down, *got_up) for g in got_qkvo])
+        got_qkvo = hop([v[4:] for v in last], y_first)
+        last = jnp.concatenate(add_halves([v[:4] for v in last], got_qkvo), axis=2)
+        sums = [[down[0], *got_down], [up[0], *got_up], [last[0], *line_hop(last)]]
     else:
         sums = [[fallback(p, z_first)] for p in (dw_down, dw_up, dw_qkvo)]
     height, wide = sums[0][0].shape
@@ -680,9 +702,7 @@
         [*sums[0], *sums[1], *sums[2], dmem, *smalls],
     )
     small = sum_all(small, "dp", size)
-    bias_grad = small[used + 6 : used + 9]
-    squares = jnp.full((8, 128), small[used + 9, 0] + jnp.sum(bias_grad * bias_grad))
-    other = exchange(squares, "head", pair, 1)
+    other = exchange(small, "head", pair, 1)
     plan = (
         (2, 0, 0, LEARN_RATE, DECAY_RATE),
         (2, 0, 3 * width, LEARN_RATE, DECAY_RATE),
@@ -702,12 +722,12 @@
     grad_norm, *news = call(
         functools.partial(adam_kernel, plan),
         [((1, 1), F32)] + [(o.shape, F32) for old in olds for o in old],
-        [small, squares, other, *matrices, *[o for old in olds for o in old]],
+        [small, other, *matrices, *[o for old in olds for o in old]],
     )
     results = [news[3 * i : 3 * i + 3] for i in range(6)]
     for number in (1, 3):
         results[number] = [r.T for r in results[number]]
-    return (outputs, input_grad, grad_norm[0, 0]) + tuple(r[i] for i in range(3) for r in results)
+    return (outputs[None], input_grad[None], grad_norm[0, 0]) + tuple(r[i] for i in range(3) for r in results)
 
 
 def solution(mesh):

time: 265 us -> 258 us (0.974)
  other arithmetic: 10.6 us -> 6.38 us
  waiting for transfers between devices: 91.9 us -> 87.9 us
    ppermute x57, waiting for transfers between devices: 91.9 us -> 87.9 us  [exchange(): return lax.ppermute(values, axis, [(i, i ^ flip) for i in range(size)])]
    pallas_call x17 -> x18, Pallas kernels: 77.7 us -> 79.7 us  [call(): pl.pallas_call(kernel, out_shape=[jax.ShapeDtypeStruct(s, d) for s, d in...]
  transfers between devices with their start and end apart: 57 -> 57, of which waited for: 35 -> 31; matrix products, arithmetic and copies ran while one was open for 4% -> 3% of each run, Pallas kernels for 13% -> 15%
where the time goes in v2:
time: 258 us; the launch traced here: 254 us
  waiting for transfers between devices  87.9 us (34%)
  Pallas kernels  79.7 us (31%)
  starting transfers between devices  72.5 us (28%)
  other arithmetic  6.38 us (2%)
  local copies, waits for them, and re-layouts  5.42 us (2%)
    ppermute x57, waiting for transfers between devices, exchange(): return lax.ppermute(values, axis, [(i, i ^ flip) for i in range(size)])  87.9 us
    pallas_call x18, Pallas kernels, call(): pl.pallas_call(kernel, out_shape=[jax.ShapeDtypeStruct(s, d) for s, d in...  79.7 us
    ppermute x57, starting transfers between devices, exchange(): return lax.ppermute(values, axis, [(i, i ^ flip) for i in range(size)])  72.5 us
  transfers between devices with their start and end apart: 57, of which 31 were waited for; matrix products, arithmetic and copies ran while one was open for 3% of the time, Pallas kernels for 15%

profile of v2, /device:TPU:0, one launch (start us, length us, event | category | flops | bytes accessed | tf_op | source)
XLA Modules:
  0.0 254.3 jit_solution(5863437392463782961)
XLA Ops:
  3.3 5.0 %collective-permute-start.2 = (bf16[2,48,768]{2,1,0:T(8,128)(2,1)}, bf16[2,48,768]{2,1,0:T(8,128)(2,1)}, u32[]{:S(2)}, u32[]{:S(2)}) collective-permute-start(bf16[2,48,768]{2,1,0:T(8,128)(2,1)} %pad_maximum_fusion.10), channel_id=1, source_target_pairs={{0,24},{2,26},{4,28},{6,30},{8,16},{10,18},{12,20},{14,22},{16,8},... | collective-permute-start | bytes 442376 | tf_op jit(solution)/shard_map/ppermute | solution.py:437
  9.7 1.7 collective-permute-start.16
  17.0 4.1 %collective-permute-done.1 = bf16[2,48,768]{2,1,0:T(8,128)(2,1)} collective-permute-done((bf16[2,48,768]{2,1,0:T(8,128)(2,1)}, bf16[2,48,768]{2,1,0:T(8,128)(2,1)}, u32[]{:S(2)}, u32[]{:S(2)}) %collective-permute-start.1) | collective-permute-done | bytes 147488 | tf_op jit(solution)/shard_map/ppermute | solution.py:437
  21.2 2.7 %collective-permute-start.10 = (bf16[2,48,768]{2,1,0:T(8,128)(2,1)S(1)}, bf16[2,48,768]{2,1,0:T(8,128)(2,1)S(1)}, u32[]{:S(2)}, u32[]{:S(2)}) collective-permute-start(bf16[2,48,768]{2,1,0:T(8,128)(2,1)S(1)} %pad_maximum_fusion.11), channel_id=1, source_target_pairs={{0,24},{2,26},{4,28},{6,30},{8,16},{10,18},{12,20},{14,22},{16,8},... | collective-permute-start | bytes 442376 | tf_op jit(solution)/shard_map/ppermute | solution.py:437
  23.8 1.7 collective-permute-start.8
  31.7 3.4 %collective-permute-done.9 = bf16[2,48,768]{2,1,0:T(8,128)(2,1)S(1)} collective-permute-done((bf16[2,48,768]{2,1,0:T(8,128)(2,1)S(1)}, bf16[2,48,768]{2,1,0:T(8,128)(2,1)S(1)}, u32[]{:S(2)}, u32[]{:S(2)}) %collective-permute-start.9) | collective-permute-done | bytes 147488 | tf_op jit(solution)/shard_map/ppermute | solution.py:437
  35.1 2.0 collective-permute-done.5
  39.3 2.5 collective-permute-start.19
  41.9 1.9 collective-permute-start.17
  43.9 5.9 %collective-permute-done.6.refs_3_ = bf16[8,48,768]{2,1,0:T(8,128)(2,1)S(1)} collective-permute-done((bf16[8,48,768]{2,1,0:T(8,128)(2,1)S(1)}, bf16[8,48,768]{2,1,0:T(8,128)(2,1)S(1)}, u32[]{:S(2)}, u32[]{:S(2)}) %collective-permute-start.6) | collective-permute-done | bytes 589856 | tf_op jit(solution)/shard_map/ppermute | solution.py:437
  53.4 4.5 %collective-permute-done.13 = bf16[4,48,768]{2,1,0:T(8,128)(2,1)S(1)} collective-permute-done((bf16[4,48,768]{2,1,0:T(8,128)(2,1)S(1)}, bf16[4,48,768]{2,1,0:T(8,128)(2,1)S(1)}, u32[]{:S(2)}, u32[]{:S(2)}) %collective-permute-start.13) | collective-permute-done | bytes 294944 | tf_op jit(solution)/shard_map/ppermute | solution.py:437
  58.6 3.5 %collective-permute-done.11 = bf16[4,48,768]{2,1,0:T(8,128)(2,1)S(1)} collective-permute-done((bf16[4,48,768]{2,1,0:T(8,128)(2,1)S(1)}, bf16[4,48,768]{2,1,0:T(8,128)(2,1)S(1)}, u32[]{:S(2)}, u32[]{:S(2)}) %collective-permute-start.11) | collective-permute-done | bytes 294944 | tf_op jit(solution)/shard_map/ppermute | solution.py:437
  62.2 1.7 collective-permute-done.18
  64.7 7.4 %shard_map.365 = (bf16[544,768]{1,0:T(8,128)(2,1)S(1)}, bf16[544,768]{1,0:T(8,128)(2,1)S(1)}, bf16[544,1152]{1,0:T(8,128)(2,1)S(1)}, f32[544,128]{1,0:T(8,128)S(1)}, bf16[544,384]{1,0:T(8,128)(2,1)S(1)}) custom-call(bf16[512,768]{1,0:T(8,128)(2,1)S(1)} %get-tuple-element.244.token_ref, f32[16,768]{1,0:T(8,128)S(1)} %broadcast_select_fusion.mem_ref.keep_ref, ...), custom_call_target="tpu_custom_call" | custom-call | tf_op jit(solution)/shard_map/pallas_call | solution.py:66
  74.2 13.9 %collective-permute-done.20.refs_1_ = bf16[8,48,768]{2,1,0:T(8,128)(2,1)S(1)} collective-permute-done((bf16[8,48,768]{2,1,0:T(8,128)(2,1)S(1)}, bf16[8,48,768]{2,1,0:T(8,128)(2,1)S(1)}, u32[]{:S(2)}, u32[]{:S(2)}) %collective-permute-start.20) | collective-permute-done | bytes 589856 | tf_op jit(solution)/shard_map/ppermute | solution.py:437
  89.1 5.2 %shard_map.368 = (bf16[544,768]{1,0:T(8,128)(2,1)S(1)}, f32[544,768]{1,0:T(8,128)S(1)}, bf16[544,768]{1,0:T(8,128)(2,1)S(1)}, bf16[544,1536]{1,0:T(8,128)(2,1)S(1)}, bf16[544,1536]{1,0:T(8,128)(2,1)S(1)}) custom-call(bf16[512,768]{1,0:T(8,128)(2,1)S(1)} %get-tuple-element.244.token_ref, f32[16,768]{1,0:T(8,128)S(1)} %broadcast_select_fusion.mem_ref.keep_ref, ...), custom_call_target="tpu_custom_call" | custom-call | tf_op jit(solution)/shard_map/pallas_call | solution.py:66
  96.8 7.9 %shard_map.369 = (bf16[512,768]{1,0:T(8,128)(2,1)S(1)}, f32[16,768]{1,0:T(8,128)S(1)}, f32[544,768]{1,0:T(8,128)S(1)}, bf16[544,768]{1,0:T(8,128)(2,1)S(1)}, bf1...) custom-call(f32[544,768]{1,0:T(8,128)S(1)} %get-tuple-element.140.fi, ...), custom_call_target="tpu_custom_call" | custom-call | tf_op jit(solution)/shard_map/pallas_call | solution.py:66
  104.9 2.2 collective-permute-done.23.other_ref
  107.1 5.4 %shard_map.370 = (bf16[544,768]{1,0:T(8,128)(2,1)S(1)}, f32[544,768]{1,0:T(8,128)S(1)}, bf16[544,768]{1,0:T(8,128)(2,1)S(1)}, bf16[544,1536]{1,0:T(8,128)(2,1)S(1)}, bf16[544,1536]{1,0:T(8,128)(2,1)S(1)}) custom-call(bf16[512,768]{1,0:T(8,128)(2,1)S(1)} %get-tuple-element.243.token_ref, f32[16,768]{1,0:T(8,128)S(1)} %get-tuple-element.143.mem_ref, ...), custom_call_target="tpu_custom_call" | custom-call | tf_op jit(solution)/shard_map/pallas_call | solution.py:66
  112.9 2.1 collective-permute-done.24.refs_3_
  115.0 5.7 %shard_map.371 = (bf16[2,512,768]{2,1,0:T(8,128)(2,1)}, bf16[544,768]{1,0:T(8,128)(2,1)S(1)}, f32[544,768]{1,0:T(8,128)S(1)}, bf16[544,768]{1,0:T(8,128)(2,1)S(1...) custom-call(bf16[512,768]{1,0:T(8,128)(2,1)S(1)} %get-tuple-element.142.refs_0_, ...), custom_call_target="tpu_custom_call" | custom-call | tf_op jit(solution)/shard_map/pallas_call | solution.py:66
  120.9 2.4 shard_map.372.refs_2_
  123.3 10.1 %shard_map.373 = (bf16[544,768]{1,0:T(8,128)(2,1)S(1)}, f32[544,768]{1,0:T(8,128)S(1)}, bf16[544,768]{1,0:T(8,128)(2,1)S(1)}, bf16[544,1152]{1,0:T(8,128)(2,1)S(...) custom-call(f32[544,768]{1,0:T(8,128)S(1)} %get-tuple-element.152.dsecond_ref, ...), custom_call_target="tpu_custom_call" | custom-call | tf_op jit(solution)/shard_map/pallas_call | solution.py:66
  133.9 2.0 collective-permute-done.26.other_ref
  135.9 5.4 %shard_map.374 = (bf16[512,768]{1,0:T(8,128)(2,1)S(1)}, f32[16,768]{1,0:T(8,128)S(1)}, bf16[544,768]{1,0:T(8,128)(2,1)S(1)}, f32[544,768]{1,0:T(8,128)S(1)}, bf1...) custom-call(f32[544,768]{1,0:T(8,128)S(1)} %get-tuple-element.156.dfirs, ...), custom_call_target="tpu_custom_call" | custom-call | tf_op jit(solution)/shard_map/pallas_call | solution.py:66
  141.7 3.4 %shard_map.375 = (bf16[8,48,768]{2,1,0:T(8,128)(2,1)S(1)}, bf16[8,48,768]{2,1,0:T(8,128)(2,1)S(1)}, bf16[8,48,768]{2,1,0:T(8,128)(2,1)S(1)}, bf16[8,48,768]{2,1,0:T(8,128)(2,1)S(1)}) custom-call(s32[1]{0:T(128)} %bitcast.1.me_ref, bf16[544,768]{1,0:T(8,128)(2,1)S(1)} %get-tuple-element.161.refs_0_, bf16[544,1536]{1,0:T(8,128)(2,1)S(1)} %get-tuple-element.162.refs_1_, ...), custom_call_target="tpu_custom_call" | custom-call | tf_op jit(solution)/shard_map/pallas_call | solution.py:66
  146.6 5.1 %shard_map.376 = (bf16[8,48,768]{2,1,0:T(8,128)(2,1)S(1)}, bf16[8,48,768]{2,1,0:T(8,128)(2,1)S(1)}, bf16[8,48,768]{2,1,0:T(8,128)(2,1)S(1)}, bf16[8,48,768]{2,1,0:T(8,128)(2,1)S(1)}) custom-call(s32[1]{0:T(128)} %bitcast.1.me_ref, bf16[544,768]{1,0:T(8,128)(2,1)S(1)} %get-tuple-element.164.refs_0_, bf16[544,768]{1,0:T(8,128)(2,1)S(1)} %get-tuple-element.165.refs_1_, ...), custom_call_target="tpu_custom_call" | custom-call | tf_op jit(solution)/shard_map/pallas_call | solution.py:66
  154.4 10.2 %shard_map.377 = (bf16[544,768]{1,0:T(8,128)(2,1)S(1)}, f32[544,768]{1,0:T(8,128)S(1)}, bf16[544,768]{1,0:T(8,128)(2,1)S(1)}, bf16[544,1152]{1,0:T(8,128)(2,1)S(...) custom-call(f32[544,768]{1,0:T(8,128)S(1)} %get-tuple-element.169.dsecond_ref, ...), custom_call_target="tpu_custom_call" | custom-call | tf_op jit(solution)/shard_map/pallas_call | solution.py:66
  165.0 8.8 %collective-permute-done.31 = bf16[8,48,768]{2,1,0:T(8,128)(2,1)S(1)} collective-permute-done((bf16[8,48,768]{2,1,0:T(8,128)(2,1)S(1)}, bf16[8,48,768]{2,1,0:T(8,128)(2,1)S(1)}, u32[]{:S(2)}, u32[]{:S(2)}) %collective-permute-start.31) | collective-permute-done | bytes 589856 | tf_op jit(solution)/shard_map/ppermute | solution.py:437
  178.4 6.2 %shard_map.379 = (bf16[8,48,768]{2,1,0:T(8,128)(2,1)S(1)}, bf16[8,48,768]{2,1,0:T(8,128)(2,1)S(1)}, bf16[8,48,768]{2,1,0:T(8,128)(2,1)S(1)}, bf16[8,48,768]{2,1,0:T(8,128)(2,1)S(1)}) custom-call(s32[1]{0:T(128)} %bitcast.1.me_ref, bf16[544,768]{1,0:T(8,128)(2,1)S(1)} %get-tuple-element.181.refs_0_, bf16[544,768]{1,0:T(8,128)(2,1)S(1)} %get-tuple-element.182.refs_1_, ...), custom_call_target="tpu_custom_call" | custom-call | tf_op jit(solution)/shard_map/pallas_call | solution.py:66
  184.8 2.5 collective-permute-start.37
  187.3 4.3 %collective-permute-start.35 = (bf16[48,1536]{1,0:T(8,128)(2,1)S(1)}, bf16[48,1536]{1,0:T(8,128)(2,1)S(1)}, u32[]{:S(2)}, u32[]{:S(2)}) collective-permute-start(bf16[48,1536]{1,0:T(8,128)(2,1)S(1)} %get-tuple-element.255), channel_id=1, source_target_pairs={{0,8},{2,10},{4,12},{6,14},{8,0},{10,2},{12,4},{14,6},{16,24},{18,... | collective-permute-start | bytes 442376 | tf_op jit(solution)/shard_map/ppermute | solution.py:437
  194.2 2.4 collective-permute-start.42
  196.5 8.6 %collective-permute-start.40 = (bf16[48,1536]{1,0:T(8,128)(2,1)S(1)}, bf16[48,1536]{1,0:T(8,128)(2,1)S(1)}, u32[]{:S(2)}, u32[]{:S(2)}) collective-permute-start(bf16[48,1536]{1,0:T(8,128)(2,1)S(1)} %get-tuple-element.251), channel_id=1, source_target_pairs={{0,8},{2,10},{4,12},{6,14},{8,0},{10,2},{12,4},{14,6},{16,24},{18,... | collective-permute-start | bytes 442376 | tf_op jit(solution)/shard_map/ppermute | solution.py:437
  205.2 2.7 %collective-permute-done.36.refs_2_ = bf16[48,1536]{1,0:T(8,128)(2,1)S(1)} collective-permute-done((bf16[48,1536]{1,0:T(8,128)(2,1)S(1)}, bf16[48,1536]{1,0:T(8,128)(2,1)S(1)}, u32[]{:S(2)}, u32[]{:S(2)}) %collective-permute-start.36) | collective-permute-done | bytes 147488 | tf_op jit(solution)/shard_map/ppermute | solution.py:437
  207.8 2.3 collective-permute-done.40.refs_5_
  210.1 4.5 %collective-permute-done.41.refs_6_ = bf16[48,1536]{1,0:T(8,128)(2,1)S(1)} collective-permute-done((bf16[48,1536]{1,0:T(8,128)(2,1)S(1)}, bf16[48,1536]{1,0:T(8,128)(2,1)S(1)}, u32[]{:S(2)}, u32[]{:S(2)}) %collective-permute-start.41) | collective-permute-done | bytes 147488 | tf_op jit(solution)/shard_map/ppermute | solution.py:437
  217.3 4.3 %collective-permute-done.44 = bf16[4,48,768]{2,1,0:T(8,128)(2,1)S(1)} collective-permute-done((bf16[4,48,768]{2,1,0:T(8,128)(2,1)S(1)}, bf16[4,48,768]{2,1,0:T(8,128)(2,1)S(1)}, u32[]{:S(2)}, u32[]{:S(2)}) %collective-permute-start.44) | collective-permute-done | bytes 294944 | tf_op jit(solution)/shard_map/ppermute | solution.py:437
  223.3 1.9 collective-permute-start.49
  225.2 2.5 collective-permute-start.48
  227.7 1.9 shard_map.378
  230.5 2.7 %collective-permute-done.47.refs_9_ = bf16[48,1536]{1,0:T(8,128)(2,1)S(1)} collective-permute-done((bf16[48,1536]{1,0:T(8,128)(2,1)S(1)}, bf16[48,1536]{1,0:T(8,128)(2,1)S(1)}, u32[]{:S(2)}, u32[]{:S(2)}) %collective-permute-start.47) | collective-permute-done | bytes 147488 | tf_op jit(solution)/shard_map/ppermute | solution.py:437
  234.5 1.8 collective-permute-start.52
  238.0 1.8 collective-permute-done.52
  242.2 2.8 %collective-permute-start.55 = (f32[24,768]{1,0:T(8,128)S(1)}, f32[24,768]{1,0:T(8,128)S(1)}, u32[]{:S(2)}, u32[]{:S(2)}) collective-permute-start(f32[24,768]{1,0:T(8,128)S(1)} %add_add_fusion.1), channel_id=1, source_target_pairs={{0,24},{2,26},{4,28},{6,30},{8,16},{10,18},{12,20},{14,22},{16,8},... | collective-permute-start | bytes 221192 | tf_op jit(solution)/shard_map/ppermute | solution.py:437
  246.7 1.8 collective-permute-done.55
  248.4 1.9 collective-permute-done.54
  251.8 2.3 shard_map.381
  (194 shorter events, 54.7 us)
Async XLA Ops:
  3.3 13.7 %collective-permute-start.2 = (bf16[2,48,768]{2,1,0:T(8,128)(2,1)}, bf16[2,48,768]{2,1,0:T(8,128)(2,1)}, u32[]{:S(2)}, u32[]{:S(2)}) collective-permute-start(bf16[2,48,768]{2,1,0:T(8,128)(2,1)} %pad_maximum_fusion.10), channel_id=1, source_target_pairs={{0,24},{2,26},{4,28},{6,30},{8,16},{10,18},{12,20},{14,22},{16,8},... | collective-permute-start | bytes 442376 | tf_op jit(solution)/shard_map/ppermute | solution.py:437
  8.4 12.8 %collective-permute-start.1 = (bf16[2,48,768]{2,1,0:T(8,128)(2,1)}, bf16[2,48,768]{2,1,0:T(8,128)(2,1)}, u32[]{:S(2)}, u32[]{:S(2)}) collective-permute-start(bf16[2,48,768]{2,1,0:T(8,128)(2,1)} %pad_maximum_fusion.10), channel_id=1, source_target_pairs={{0,16},{2,18},{4,20},{6,22},{8,24},{10,26},{12,28},{14,30},{16,0},... | collective-permute-start | bytes 442376 | tf_op jit(solution)/shard_map/ppermute | solution.py:437
  8.4 12.8 %collective-permute-start = (bf16[2,48,768]{2,1,0:T(8,128)(2,1)}, bf16[2,48,768]{2,1,0:T(8,128)(2,1)}, u32[]{:S(2)}, u32[]{:S(2)}) collective-permute-start(bf16[2,48,768]{2,1,0:T(8,128)(2,1)} %pad_maximum_fusion.10), channel_id=1, source_target_pairs={{0,8},{2,10},{4,12},{6,14},{8,0},{10,2},{12,4},{14,6},{16,24},{18,... | collective-permute-start | bytes 442376 | tf_op jit(solution)/shard_map/ppermute | solution.py:437
  9.7 4.7 %collective-permute-start.16 = (bf16[48,768]{1,0:T(8,128)(2,1)}, bf16[48,768]{1,0:T(8,128)(2,1)}, u32[]{:S(2)}, u32[]{:S(2)}) collective-permute-start(bf16[48,768]{1,0:T(8,128)(2,1)} %get-tuple-element.267), channel_id=1, source_target_pairs={{0,4},{2,6},{4,0},{6,2},{8,12},{10,14},{12,8},{14,10},{16,20},{18,... | collective-permute-start | bytes 221192 | tf_op jit(solution)/shard_map/ppermute | solution.py:437
  21.2 10.5 %collective-permute-start.10 = (bf16[2,48,768]{2,1,0:T(8,128)(2,1)S(1)}, bf16[2,48,768]{2,1,0:T(8,128)(2,1)S(1)}, u32[]{:S(2)}, u32[]{:S(2)}) collective-permute-start(bf16[2,48,768]{2,1,0:T(8,128)(2,1)S(1)} %pad_maximum_fusion.11), channel_id=1, source_target_pairs={{0,24},{2,26},{4,28},{6,30},{8,16},{10,18},{12,20},{14,22},{16,8},... | collective-permute-start | bytes 442376 | tf_op jit(solution)/shard_map/ppermute | solution.py:437
  23.8 11.2 %collective-permute-start.9 = (bf16[2,48,768]{2,1,0:T(8,128)(2,1)S(1)}, bf16[2,48,768]{2,1,0:T(8,128)(2,1)S(1)}, u32[]{:S(2)}, u32[]{:S(2)}) collective-permute-start(bf16[2,48,768]{2,1,0:T(8,128)(2,1)S(1)} %pad_maximum_fusion.11), channel_id=1, source_target_pairs={{0,16},{2,18},{4,20},{6,22},{8,24},{10,26},{12,28},{14,30},{16,0},... | collective-permute-start | bytes 442376 | tf_op jit(solution)/shard_map/ppermute | solution.py:437
  23.8 15.4 %collective-permute-start.8 = (bf16[2,48,768]{2,1,0:T(8,128)(2,1)S(1)}, bf16[2,48,768]{2,1,0:T(8,128)(2,1)S(1)}, u32[]{:S(2)}, u32[]{:S(2)}) collective-permute-start(bf16[2,48,768]{2,1,0:T(8,128)(2,1)S(1)} %pad_maximum_fusion.11), channel_id=1, source_target_pairs={{0,8},{2,10},{4,12},{6,14},{8,0},{10,2},{12,4},{14,6},{16,24},{18,... | collective-permute-start | bytes 442376 | tf_op jit(solution)/shard_map/ppermute | solution.py:437
  28.4 9.2 %collective-permute-start.3 = (bf16[4,48,768]{2,1,0:T(8,128)(2,1)S(1)}, bf16[4,48,768]{2,1,0:T(8,128)(2,1)S(1)}, u32[]{:S(2)}, u32[]{:S(2)}) collective-permute-start(bf16[4,48,768]{2,1,0:T(8,128)(2,1)S(1)} %pad_maximum_fusion.2), channel_id=1, source_target_pairs={{0,4},{2,6},{4,0},{6,2},{8,12},{10,14},{12,8},{14,10},{16,20},{18,... | collective-permute-start | bytes 884744 | tf_op jit(solution)/shard_map/ppermute | solution.py:437
  30.1 7.0 %collective-permute-start.5 = (bf16[4,48,768]{2,1,0:T(8,128)(2,1)S(1)}, bf16[4,48,768]{2,1,0:T(8,128)(2,1)S(1)}, u32[]{:S(2)}, u32[]{:S(2)}) collective-permute-start(bf16[4,48,768]{2,1,0:T(8,128)(2,1)S(1)} %pad_maximum_fusion.3), channel_id=1, source_target_pairs={{0,2},{2,0},{4,6},{6,4},{8,10},{10,8},{12,14},{14,12},{16,18},{18,... | collective-permute-start | bytes 884744 | tf_op jit(solution)/shard_map/ppermute | solution.py:437
  37.1 12.7 %collective-permute-start.6 = (bf16[8,48,768]{2,1,0:T(8,128)(2,1)S(1)}, bf16[8,48,768]{2,1,0:T(8,128)(2,1)S(1)}, u32[]{:S(2)}, u32[]{:S(2)}) collective-permute-start(bf16[8,48,768]{2,1,0:T(8,128)(2,1)S(1)} %constant_dynamic-update-slice_fusion.5.refs_2_), channel_id=1, source_target_pairs={{0,4},{2,6},{4,0},{6,2},{8,12},{10,14},{12,8},{14,10},{16,20},{18,... | collective-permute-start | bytes 1769480 | tf_op jit(solution)/shard_map/ppermute | solution.py:437
  37.7 13.6 %collective-permute-start.4 = (bf16[8,48,768]{2,1,0:T(8,128)(2,1)S(1)}, bf16[8,48,768]{2,1,0:T(8,128)(2,1)S(1)}, u32[]{:S(2)}, u32[]{:S(2)}) collective-permute-start(bf16[8,48,768]{2,1,0:T(8,128)(2,1)S(1)} %constant_dynamic-update-slice_fusion.refs_0_), channel_id=1, source_target_pairs={{0,2},{2,0},{4,6},{6,4},{8,10},{10,8},{12,14},{14,12},{16,18},{18,... | collective-permute-start | bytes 1769480 | tf_op jit(solution)/shard_map/ppermute | solution.py:437
  39.3 13.4 %collective-permute-start.19 = (bf16[2,2,48,768]{3,2,1,0:T(8,128)(2,1)S(1)}, bf16[2,2,48,768]{3,2,1,0:T(8,128)(2,1)S(1)}, u32[]{:S(2)}, u32[]{:S(2)}) collective-permute-start(bf16[2,2,48,768]{3,2,1,0:T(8,128)(2,1)S(1)} %pad_maximum_fusion.6), channel_id=1, source_target_pairs={{0,24},{2,26},{4,28},{6,30},{8,16},{10,18},{12,20},{14,22},{16,8},... | collective-permute-start | bytes 884744 | tf_op jit(solution)/shard_map/ppermute | solution.py:437
  41.9 22.0 %collective-permute-start.18 = (bf16[2,2,48,768]{3,2,1,0:T(8,128)(2,1)S(1)}, bf16[2,2,48,768]{3,2,1,0:T(8,128)(2,1)S(1)}, u32[]{:S(2)}, u32[]{:S(2)}) collective-permute-start(bf16[2,2,48,768]{3,2,1,0:T(8,128)(2,1)S(1)} %pad_maximum_fusion.6), channel_id=1, source_target_pairs={{0,16},{2,18},{4,20},{6,22},{8,24},{10,26},{12,28},{14,30},{16,0},... | collective-permute-start | bytes 884744 | tf_op jit(solution)/shard_map/ppermute | solution.py:437
  41.9 22.0 %collective-permute-start.17 = (bf16[2,2,48,768]{3,2,1,0:T(8,128)(2,1)S(1)}, bf16[2,2,48,768]{3,2,1,0:T(8,128)(2,1)S(1)}, u32[]{:S(2)}, u32[]{:S(2)}) collective-permute-start(bf16[2,2,48,768]{3,2,1,0:T(8,128)(2,1)S(1)} %pad_maximum_fusion.6), channel_id=1, source_target_pairs={{0,8},{2,10},{4,12},{6,14},{8,0},{10,2},{12,4},{14,6},{16,24},{18,... | collective-permute-start | bytes 884744 | tf_op jit(solution)/shard_map/ppermute | solution.py:437
  51.3 6.7 %collective-permute-start.13 = (bf16[4,48,768]{2,1,0:T(8,128)(2,1)S(1)}, bf16[4,48,768]{2,1,0:T(8,128)(2,1)S(1)}, u32[]{:S(2)}, u32[]{:S(2)}) collective-permute-start(bf16[4,48,768]{2,1,0:T(8,128)(2,1)S(1)} %pad_maximum_fusion.5), channel_id=1, source_target_pairs={{0,2},{2,0},{4,6},{6,4},{8,10},{10,8},{12,14},{14,12},{16,18},{18,... | collective-permute-start | bytes 884744 | tf_op jit(solution)/shard_map/ppermute | solution.py:437
  52.8 9.3 %collective-permute-start.11 = (bf16[4,48,768]{2,1,0:T(8,128)(2,1)S(1)}, bf16[4,48,768]{2,1,0:T(8,128)(2,1)S(1)}, u32[]{:S(2)}, u32[]{:S(2)}) collective-permute-start(bf16[4,48,768]{2,1,0:T(8,128)(2,1)S(1)} %pad_maximum_fusion.4), channel_id=1, source_target_pairs={{0,4},{2,6},{4,0},{6,2},{8,12},{10,14},{12,8},{14,10},{16,20},{18,... | collective-permute-start | bytes 884744 | tf_op jit(solution)/shard_map/ppermute | solution.py:437
  58.0 14.3 %collective-permute-start.14 = (bf16[8,48,768]{2,1,0:T(8,128)(2,1)S(1)}, bf16[8,48,768]{2,1,0:T(8,128)(2,1)S(1)}, u32[]{:S(2)}, u32[]{:S(2)}) collective-permute-start(bf16[8,48,768]{2,1,0:T(8,128)(2,1)S(1)} %constant_dynamic-update-slice_fusion.12.refs_2_), channel_id=1, source_target_pairs={{0,4},{2,6},{4,0},{6,2},{8,12},{10,14},{12,8},{14,10},{16,20},{18,... | collective-permute-start | bytes 1769480 | tf_op jit(solution)/shard_map/ppermute | solution.py:437
  62.1 10.2 %collective-permute-start.12 = (bf16[8,48,768]{2,1,0:T(8,128)(2,1)S(1)}, bf16[8,48,768]{2,1,0:T(8,128)(2,1)S(1)}, u32[]{:S(2)}, u32[]{:S(2)}) collective-permute-start(bf16[8,48,768]{2,1,0:T(8,128)(2,1)S(1)} %constant_dynamic-update-slice_fusion.10.refs_0_), channel_id=1, source_target_pairs={{0,2},{2,0},{4,6},{6,4},{8,10},{10,8},{12,14},{14,12},{16,18},{18,... | collective-permute-start | bytes 1769480 | tf_op jit(solution)/shard_map/ppermute | solution.py:437
  72.0 17.1 %collective-permute-start.7 = (bf16[544,768]{1,0:T(8,128)(2,1)S(1)}, bf16[544,768]{1,0:T(8,128)(2,1)S(1)}, u32[]{:S(2)}, u32[]{:S(2)}) collective-permute-start(bf16[544,768]{1,0:T(8,128)(2,1)S(1)} %get-tuple-element.133.own_ref), channel_id=1, source_target_pairs={{0,1},{1,0},{2,3},{3,2},{4,5},{5,4},{6,7},{7,6},{8,9},{9,8},{10,11... | collective-permute-start | bytes 2506760 | tf_op jit(solution)/shard_map/ppermute | solution.py:437
  72.3 15.8 %collective-permute-start.20 = (bf16[8,48,768]{2,1,0:T(8,128)(2,1)S(1)}, bf16[8,48,768]{2,1,0:T(8,128)(2,1)S(1)}, u32[]{:S(2)}, u32[]{:S(2)}) collective-permute-start(bf16[8,48,768]{2,1,0:T(8,128)(2,1)S(1)} %pad_maximum_fusion.refs_0_), channel_id=1, source_target_pairs={{0,4},{2,6},{4,0},{6,2},{8,12},{10,14},{12,8},{14,10},{16,20},{18,... | collective-permute-start | bytes 1769480 | tf_op jit(solution)/shard_map/ppermute | solution.py:437
  73.5 15.4 %collective-permute-start.21 = (bf16[8,48,768]{2,1,0:T(8,128)(2,1)S(1)}, bf16[8,48,768]{2,1,0:T(8,128)(2,1)S(1)}, u32[]{:S(2)}, u32[]{:S(2)}) collective-permute-start(bf16[8,48,768]{2,1,0:T(8,128)(2,1)S(1)} %pad_maximum_fusion.1.refs_2_), channel_id=1, source_target_pairs={{0,2},{2,0},{4,6},{6,4},{8,10},{10,8},{12,14},{14,12},{16,18},{18,... | collective-permute-start | bytes 1769480 | tf_op jit(solution)/shard_map/ppermute | solution.py:437
  141.3 13.1 %collective-permute-start.27 = (bf16[544,768]{1,0:T(8,128)(2,1)S(1)}, bf16[544,768]{1,0:T(8,128)(2,1)S(1)}, u32[]{:S(2)}, u32[]{:S(2)}) collective-permute-start(bf16[544,768]{1,0:T(8,128)(2,1)S(1)} %get-tuple-element.170.own_ref), channel_id=1, source_target_pairs={{0,1},{1,0},{2,3},{3,2},{4,5},{5,4},{6,7},{7,6},{8,9},{9,8},{10,11... | collective-permute-start | bytes 2506760 | tf_op jit(solution)/shard_map/ppermute | solution.py:437
  145.1 19.5 %collective-permute-start.32 = (bf16[8,48,768]{2,1,0:T(8,128)(2,1)S(1)}, bf16[8,48,768]{2,1,0:T(8,128)(2,1)S(1)}, u32[]{:S(2)}, u32[]{:S(2)}) collective-permute-start(bf16[8,48,768]{2,1,0:T(8,128)(2,1)S(1)} %get-tuple-element.185), channel_id=1, source_target_pairs={{0,4},{2,6},{4,0},{6,2},{8,12},{10,14},{12,8},{14,10},{16,20},{18,... | collective-permute-start | bytes 1769480 | tf_op jit(solution)/shard_map/ppermute | solution.py:437
  146.1 18.7 %collective-permute-start.29 = (bf16[8,48,768]{2,1,0:T(8,128)(2,1)S(1)}, bf16[8,48,768]{2,1,0:T(8,128)(2,1)S(1)}, u32[]{:S(2)}, u32[]{:S(2)}) collective-permute-start(bf16[8,48,768]{2,1,0:T(8,128)(2,1)S(1)} %get-tuple-element.178), channel_id=1, source_target_pairs={{0,2},{2,0},{4,6},{6,4},{8,10},{10,8},{12,14},{14,12},{16,18},{18,... | collective-permute-start | bytes 1769480 | tf_op jit(solution)/shard_map/ppermute | solution.py:437
  151.7 22.1 %collective-permute-start.31 = (bf16[8,48,768]{2,1,0:T(8,128)(2,1)S(1)}, bf16[8,48,768]{2,1,0:T(8,128)(2,1)S(1)}, u32[]{:S(2)}, u32[]{:S(2)}) collective-permute-start(bf16[8,48,768]{2,1,0:T(8,128)(2,1)S(1)} %get-tuple-element.183), channel_id=1, source_target_pairs={{0,2},{2,0},{4,6},{6,4},{8,10},{10,8},{12,14},{14,12},{16,18},{18,... | collective-permute-start | bytes 1769480 | tf_op jit(solution)/shard_map/ppermute | solution.py:437
  153.3 21.2 %collective-permute-start.33 = (bf16[8,48,768]{2,1,0:T(8,128)(2,1)S(1)}, bf16[8,48,768]{2,1,0:T(8,128)(2,1)S(1)}, u32[]{:S(2)}, u32[]{:S(2)}) collective-permute-start(bf16[8,48,768]{2,1,0:T(8,128)(2,1)S(1)} %get-tuple-element.189), channel_id=1, source_target_pairs={{0,4},{2,6},{4,0},{6,2},{8,12},{10,14},{12,8},{14,10},{16,20},{18,... | collective-permute-start | bytes 1769480 | tf_op jit(solution)/shard_map/ppermute | solution.py:437
  173.8 10.8 %collective-permute-start.34 = (bf16[4,48,768]{2,1,0:T(8,128)(2,1)S(1)}, bf16[4,48,768]{2,1,0:T(8,128)(2,1)S(1)}, u32[]{:S(2)}, u32[]{:S(2)}) collective-permute-start(bf16[4,48,768]{2,1,0:T(8,128)(2,1)S(1)} %slice.258), channel_id=1, source_target_pairs={{0,2},{2,0},{4,6},{6,4},{8,10},{10,8},{12,14},{14,12},{16,18},{18,... | collective-permute-start | bytes 884744 | tf_op jit(solution)/shard_map/ppermute | solution.py:437
  174.5 10.1 %collective-permute-start.30 = (bf16[4,48,768]{2,1,0:T(8,128)(2,1)S(1)}, bf16[4,48,768]{2,1,0:T(8,128)(2,1)S(1)}, u32[]{:S(2)}, u32[]{:S(2)}) collective-permute-start(bf16[4,48,768]{2,1,0:T(8,128)(2,1)S(1)} %slice.256), channel_id=1, source_target_pairs={{0,4},{2,6},{4,0},{6,2},{8,12},{10,14},{12,8},{14,10},{16,20},{18,... | collective-permute-start | bytes 884744 | tf_op jit(solution)/shard_map/ppermute | solution.py:437
  175.9 16.1 %collective-permute-start.39 = (bf16[4,48,768]{2,1,0:T(8,128)(2,1)S(1)}, bf16[4,48,768]{2,1,0:T(8,128)(2,1)S(1)}, u32[]{:S(2)}, u32[]{:S(2)}) collective-permute-start(bf16[4,48,768]{2,1,0:T(8,128)(2,1)S(1)} %slice.268), channel_id=1, source_target_pairs={{0,2},{2,0},{4,6},{6,4},{8,10},{10,8},{12,14},{14,12},{16,18},{18,... | collective-permute-start | bytes 884744 | tf_op jit(solution)/shard_map/ppermute | solution.py:437
  177.5 14.5 %collective-permute-start.38 = (bf16[4,48,768]{2,1,0:T(8,128)(2,1)S(1)}, bf16[4,48,768]{2,1,0:T(8,128)(2,1)S(1)}, u32[]{:S(2)}, u32[]{:S(2)}) collective-permute-start(bf16[4,48,768]{2,1,0:T(8,128)(2,1)S(1)} %slice.266), channel_id=1, source_target_pairs={{0,4},{2,6},{4,0},{6,2},{8,12},{10,14},{12,8},{14,10},{16,20},{18,... | collective-permute-start | bytes 884744 | tf_op jit(solution)/shard_map/ppermute | solution.py:437
  184.8 9.4 %collective-permute-start.37 = (bf16[48,1536]{1,0:T(8,128)(2,1)S(1)}, bf16[48,1536]{1,0:T(8,128)(2,1)S(1)}, u32[]{:S(2)}, u32[]{:S(2)}) collective-permute-start(bf16[48,1536]{1,0:T(8,128)(2,1)S(1)} %get-tuple-element.253), channel_id=1, source_target_pairs={{0,24},{2,26},{4,28},{6,30},{8,16},{10,18},{12,20},{14,22},{16,8},... | collective-permute-start | bytes 442376 | tf_op jit(solution)/shard_map/ppermute | solution.py:437
  187.3 9.3 %collective-permute-start.35 = (bf16[48,1536]{1,0:T(8,128)(2,1)S(1)}, bf16[48,1536]{1,0:T(8,128)(2,1)S(1)}, u32[]{:S(2)}, u32[]{:S(2)}) collective-permute-start(bf16[48,1536]{1,0:T(8,128)(2,1)S(1)} %get-tuple-element.255), channel_id=1, source_target_pairs={{0,8},{2,10},{4,12},{6,14},{8,0},{10,2},{12,4},{14,6},{16,24},{18,... | collective-permute-start | bytes 442376 | tf_op jit(solution)/shard_map/ppermute | solution.py:437
  191.6 16.2 %collective-permute-start.36 = (bf16[48,1536]{1,0:T(8,128)(2,1)S(1)}, bf16[48,1536]{1,0:T(8,128)(2,1)S(1)}, u32[]{:S(2)}, u32[]{:S(2)}) collective-permute-start(bf16[48,1536]{1,0:T(8,128)(2,1)S(1)} %get-tuple-element.256), channel_id=1, source_target_pairs={{0,16},{2,18},{4,20},{6,22},{8,24},{10,26},{12,28},{14,30},{16,0},... | collective-permute-start | bytes 442376 | tf_op jit(solution)/shard_map/ppermute | solution.py:437
  192.0 22.6 %collective-permute-start.43 = (bf16[8,48,768]{2,1,0:T(8,128)(2,1)S(1)}, bf16[8,48,768]{2,1,0:T(8,128)(2,1)S(1)}, u32[]{:S(2)}, u32[]{:S(2)}) collective-permute-start(bf16[8,48,768]{2,1,0:T(8,128)(2,1)S(1)} %get-tuple-element.202), channel_id=1, source_target_pairs={{0,2},{2,0},{4,6},{6,4},{8,10},{10,8},{12,14},{14,12},{16,18},{18,... | collective-permute-start | bytes 1769480 | tf_op jit(solution)/shard_map/ppermute | solution.py:437
  192.7 23.5 %collective-permute-start.45 = (bf16[8,48,768]{2,1,0:T(8,128)(2,1)S(1)}, bf16[8,48,768]{2,1,0:T(8,128)(2,1)S(1)}, u32[]{:S(2)}, u32[]{:S(2)}) collective-permute-start(bf16[8,48,768]{2,1,0:T(8,128)(2,1)S(1)} %get-tuple-element.207), channel_id=1, source_target_pairs={{0,4},{2,6},{4,0},{6,2},{8,12},{10,14},{12,8},{14,10},{16,20},{18,... | collective-permute-start | bytes 1769480 | tf_op jit(solution)/shard_map/ppermute | solution.py:437
  194.2 13.7 %collective-permute-start.42 = (bf16[48,1536]{1,0:T(8,128)(2,1)S(1)}, bf16[48,1536]{1,0:T(8,128)(2,1)S(1)}, u32[]{:S(2)}, u32[]{:S(2)}) collective-permute-start(bf16[48,1536]{1,0:T(8,128)(2,1)S(1)} %get-tuple-element.249), channel_id=1, source_target_pairs={{0,24},{2,26},{4,28},{6,30},{8,16},{10,18},{12,20},{14,22},{16,8},... | collective-permute-start | bytes 442376 | tf_op jit(solution)/shard_map/ppermute | solution.py:437
  196.5 13.6 %collective-permute-start.40 = (bf16[48,1536]{1,0:T(8,128)(2,1)S(1)}, bf16[48,1536]{1,0:T(8,128)(2,1)S(1)}, u32[]{:S(2)}, u32[]{:S(2)}) collective-permute-start(bf16[48,1536]{1,0:T(8,128)(2,1)S(1)} %get-tuple-element.251), channel_id=1, source_target_pairs={{0,8},{2,10},{4,12},{6,14},{8,0},{10,2},{12,4},{14,6},{16,24},{18,... | collective-permute-start | bytes 442376 | tf_op jit(solution)/shard_map/ppermute | solution.py:437
  207.8 6.8 %collective-permute-start.41 = (bf16[48,1536]{1,0:T(8,128)(2,1)S(1)}, bf16[48,1536]{1,0:T(8,128)(2,1)S(1)}, u32[]{:S(2)}, u32[]{:S(2)}) collective-permute-start(bf16[48,1536]{1,0:T(8,128)(2,1)S(1)} %get-tuple-element.252), channel_id=1, source_target_pairs={{0,16},{2,18},{4,20},{6,22},{8,24},{10,26},{12,28},{14,30},{16,0},... | collective-permute-start | bytes 442376 | tf_op jit(solution)/shard_map/ppermute | solution.py:437
  214.8 6.8 %collective-permute-start.44 = (bf16[4,48,768]{2,1,0:T(8,128)(2,1)S(1)}, bf16[4,48,768]{2,1,0:T(8,128)(2,1)S(1)}, u32[]{:S(2)}, u32[]{:S(2)}) collective-permute-start(bf16[4,48,768]{2,1,0:T(8,128)(2,1)S(1)} %slice.276), channel_id=1, source_target_pairs={{0,4},{2,6},{4,0},{6,2},{8,12},{10,14},{12,8},{14,10},{16,20},{18,... | collective-permute-start | bytes 884744 | tf_op jit(solution)/shard_map/ppermute | solution.py:437
  216.3 6.8 %collective-permute-start.46 = (bf16[4,48,768]{2,1,0:T(8,128)(2,1)S(1)}, bf16[4,48,768]{2,1,0:T(8,128)(2,1)S(1)}, u32[]{:S(2)}, u32[]{:S(2)}) collective-permute-start(bf16[4,48,768]{2,1,0:T(8,128)(2,1)S(1)} %slice.278), channel_id=1, source_target_pairs={{0,2},{2,0},{4,6},{6,4},{8,10},{10,8},{12,14},{14,12},{16,18},{18,... | collective-permute-start | bytes 884744 | tf_op jit(solution)/shard_map/ppermute | solution.py:437
  217.3 10.4 %collective-permute-start.28 = (bf16[544,768]{1,0:T(8,128)(2,1)S(1)}, bf16[544,768]{1,0:T(8,128)(2,1)S(1)}, u32[]{:S(2)}, u32[]{:S(2)}) collective-permute-start(bf16[544,768]{1,0:T(8,128)(2,1)S(1)} %get-tuple-element.174.own_ref), channel_id=1, source_target_pairs={{0,1},{1,0},{2,3},{3,2},{4,5},{5,4},{6,7},{7,6},{8,9},{9,8},{10,11... | collective-permute-start | bytes 2506760 | tf_op jit(solution)/shard_map/ppermute | solution.py:437
  223.3 7.2 %collective-permute-start.49 = (bf16[48,1536]{1,0:T(8,128)(2,1)S(1)}, bf16[48,1536]{1,0:T(8,128)(2,1)S(1)}, u32[]{:S(2)}, u32[]{:S(2)}) collective-permute-start(bf16[48,1536]{1,0:T(8,128)(2,1)S(1)} %get-tuple-element.245), channel_id=1, source_target_pairs={{0,24},{2,26},{4,28},{6,30},{8,16},{10,18},{12,20},{14,22},{16,8},... | collective-permute-start | bytes 442376 | tf_op jit(solution)/shard_map/ppermute | solution.py:437
  225.2 8.0 %collective-permute-start.47 = (bf16[48,1536]{1,0:T(8,128)(2,1)S(1)}, bf16[48,1536]{1,0:T(8,128)(2,1)S(1)}, u32[]{:S(2)}, u32[]{:S(2)}) collective-permute-start(bf16[48,1536]{1,0:T(8,128)(2,1)S(1)} %get-tuple-element.247), channel_id=1, source_target_pairs={{0,8},{2,10},{4,12},{6,14},{8,0},{10,2},{12,4},{14,6},{16,24},{18,... | collective-permute-start | bytes 442376 | tf_op jit(solution)/shard_map/ppermute | solution.py:437
  225.2 8.7 %collective-permute-start.48 = (bf16[48,1536]{1,0:T(8,128)(2,1)S(1)}, bf16[48,1536]{1,0:T(8,128)(2,1)S(1)}, u32[]{:S(2)}, u32[]{:S(2)}) collective-permute-start(bf16[48,1536]{1,0:T(8,128)(2,1)S(1)} %get-tuple-element.248), channel_id=1, source_target_pairs={{0,16},{2,18},{4,20},{6,22},{8,24},{10,26},{12,28},{14,30},{16,0},... | collective-permute-start | bytes 442376 | tf_op jit(solution)/shard_map/ppermute | solution.py:437
  234.5 5.3 %collective-permute-start.52 = (f32[24,768]{1,0:T(8,128)S(1)}, f32[24,768]{1,0:T(8,128)S(1)}, u32[]{:S(2)}, u32[]{:S(2)}) collective-permute-start(f32[24,768]{1,0:T(8,128)S(1)} %get-tuple-element.218), channel_id=1, source_target_pairs={{0,6},{2,4},{4,2},{6,0},{8,14},{10,12},{12,10},{14,8},{16,22},{18,... | collective-permute-start | bytes 221192 | tf_op jit(solution)/shard_map/ppermute | solution.py:437
  242.2 6.2 %collective-permute-start.55 = (f32[24,768]{1,0:T(8,128)S(1)}, f32[24,768]{1,0:T(8,128)S(1)}, u32[]{:S(2)}, u32[]{:S(2)}) collective-permute-start(f32[24,768]{1,0:T(8,128)S(1)} %add_add_fusion.1), channel_id=1, source_target_pairs={{0,24},{2,26},{4,28},{6,30},{8,16},{10,18},{12,20},{14,22},{16,8},... | collective-permute-start | bytes 221192 | tf_op jit(solution)/shard_map/ppermute | solution.py:437
  245.0 5.3 %collective-permute-start.54 = (f32[24,768]{1,0:T(8,128)S(1)}, f32[24,768]{1,0:T(8,128)S(1)}, u32[]{:S(2)}, u32[]{:S(2)}) collective-permute-start(f32[24,768]{1,0:T(8,128)S(1)} %add_add_fusion.1), channel_id=1, source_target_pairs={{0,16},{2,18},{4,20},{6,22},{8,24},{10,26},{12,28},{14,30},{16,0},... | collective-permute-start | bytes 221192 | tf_op jit(solution)/shard_map/ppermute | solution.py:437
  245.0 5.3 %collective-permute-start.53 = (f32[24,768]{1,0:T(8,128)S(1)}, f32[24,768]{1,0:T(8,128)S(1)}, u32[]{:S(2)}, u32[]{:S(2)}) collective-permute-start(f32[24,768]{1,0:T(8,128)S(1)} %add_add_fusion.1), channel_id=1, source_target_pairs={{0,8},{2,10},{4,12},{6,14},{8,0},{10,2},{12,4},{14,6},{16,24},{18,... | collective-permute-start | bytes 221192 | tf_op jit(solution)/shard_map/ppermute | solution.py:437
  (32 other events, 319.1 us)

commit v3 on v2

--- a/solution.py
+++ b/solution.py
@@ -81,6 +81,27 @@
         return (outer + 2 * mid if kind[1] == "a" else 2 * outer + mid) + 4 * z
     outer, z, inner = number // 8, number // 2 % 4, number % 2
     return (2 * outer + inner if kind[1] == "a" else outer + 2 * inner) + 4 * z
+
+
+def own_first_kernel(qkv_ref, out_ref, own_ref):
+    width = out_ref.shape[1]
+    for part in range(2):
+        own_ref[part, :, :width] = qkv_ref[2 * part].astype(BF)
+    own_ref[0, :, width:] = qkv_ref[1].astype(BF)
+    own_ref[1, :, width:] = out_ref[...].astype(BF)
+
+
+def own_next_kernel(up_ref, down_ref, up_own_ref, *down_own_refs):
+    half = up_ref.shape[1] // 2
+    for part in range(2):
+        up_own_ref[part] = up_ref[:, part * half : (part + 1) * half].astype(BF)
+        down_own_refs[part][...] = down_ref[:, part * half : (part + 1) * half].astype(BF)
+
+
+def line_kernel(*refs):
+    for part, target in enumerate(refs[4:]):
+        for place, source in enumerate(refs[:4]):
+            target[place] = source[part]
 
 
 def assemble_kernel(kinds, counts, joined, me_ref, *refs):
@@ -515,15 +536,14 @@
     half = hidden // 2
 
     me = (lax.axis_index("dp") if size == SLOTS else jnp.int32(0)).astype(jnp.int32).reshape(1)
-    qkv_low = qkv_weight.astype(BF)
-    out_low = out_weight.T.astype(BF)
-    up_low = up_weight.astype(BF)
-    down_low = down_weight.T.astype(BF)
-    own = [
-        jnp.stack([jnp.concatenate([qkv_low[0], qkv_low[1]], axis=1), jnp.concatenate([qkv_low[2], out_low], axis=1)]),
-        jnp.stack([up_low[:, :half], up_low[:, half:]]),
-        jnp.stack([down_low[:, :half], down_low[:, half:]]),
-    ]
+    block = qkv_weight.shape[1]
+    (own_qkvo,) = call(own_first_kernel, [((2, block, 2 * width), BF)], [qkv_weight, out_weight.T])
+    own_up, *own_down = call(
+        own_next_kernel,
+        [((2, block, half), BF), ((block, half), BF), ((block, half), BF)],
+        [up_weight, down_weight.T],
+    )
+    own = [own_qkvo, own_up, own_down]
 
     def assembled(kinds, pieces, joined):
         return call(
@@ -547,7 +567,7 @@
         pair_c = [jnp.stack([own[2][i], exchange(own[2][i], "dp", size, 1 + i)]) for i in range(2)]
         line_one = line_stage(own[0], size)
         line_two = line_stage(after(own[1], *line_one), size)
-        low_one = spread([jnp.stack([v[i] for v in line_one]) for i in range(2)])
+        low_one = spread(call(line_kernel, [((4, *line_one[0].shape[1:]), BF)] * 2, line_one))
         line_three = line_stage(after(jnp.stack(pair_c), *line_two, *low_one), size)
         high_one = finish(*low_one)
         low_two = spread([after(jnp.stack([v[i] for v in line_two]), *high_one) for i in range(2)])

time: 258 us -> 256 us (level)
  waiting for transfers between devices: 87.9 us -> 92.7 us
  other arithmetic: 6.38 us -> 1.86 us
  starting transfers between devices: 72.5 us -> 69.5 us
    ppermute x57, waiting for transfers between devices: 87.9 us -> 92.7 us  [exchange(): return lax.ppermute(values, axis, [(i, i ^ flip) for i in range(size)])]
    unnamed x48 -> x52, local copies, waits for them, and re-layouts: 1.31 us -> 4.42 us
    ppermute x57, starting transfers between devices: 72.5 us -> 69.5 us  [exchange(): return lax.ppermute(values, axis, [(i, i ^ flip) for i in range(size)])]
    slice x3 -> x0, local copies, waits for them, and re-layouts: 2.83 us -> none  [shards(): low_one = spread([jnp.stack([v[i] for v in line_one]) for i in range(2)])]
    pallas_call x18 -> x21, Pallas kernels: 79.7 us -> 79.8 us  [call(): pl.pallas_call(kernel, out_shape=[jax.ShapeDtypeStruct(s, d) for s, d in...]
  transfers between devices with their start and end apart: 57 -> 57, of which waited for: 31 -> 31; matrix products, arithmetic and copies ran while one was open for 3% -> 2% of each run, Pallas kernels for 15% -> 15%
where the time goes in v3:
time: 256 us; the launch traced here: 253 us
  waiting for transfers between devices  92.7 us (36%)
  Pallas kernels  79.8 us (31%)
  starting transfers between devices  69.5 us (27%)
  local copies, waits for them, and re-layouts  6.33 us (2%)
    ppermute x57, waiting for transfers between devices, exchange(): return lax.ppermute(values, axis, [(i, i ^ flip) for i in range(size)])  92.7 us
    pallas_call x21, Pallas kernels, call(): pl.pallas_call(kernel, out_shape=[jax.ShapeDtypeStruct(s, d) for s, d in...  79.8 us
    ppermute x57, starting transfers between devices, exchange(): return lax.ppermute(values, axis, [(i, i ^ flip) for i in range(size)])  69.5 us
  transfers between devices with their start and end apart: 57, of which 31 were waited for; matrix products, arithmetic and copies ran while one was open for 2% of the time, Pallas kernels for 15%

profile of v3, /device:TPU:0, one launch (start us, length us, event | category | flops | bytes accessed | tf_op | source)
XLA Modules:
  0.0 252.6 jit_solution(16552578081112510208)
XLA Ops:
  2.5 5.1 %collective-permute-start.2 = (bf16[2,48,768]{2,1,0:T(8,128)(2,1)S(1)}, bf16[2,48,768]{2,1,0:T(8,128)(2,1)S(1)}, u32[]{:S(2)}, u32[]{:S(2)}) collective-permute-start(bf16[2,48,768]{2,1,0:T(8,128)(2,1)S(1)} %shard_map.364.refs_0_), channel_id=1, source_target_pairs={{0,24},{2,26},{4,28},{6,30},{8,16},{10,18},{12,20},{14,22},{16,8},... | collective-permute-start | bytes 442376 | tf_op jit(solution)/shard_map/ppermute | solution.py:458
  10.2 1.7 collective-permute-start.15
  16.3 3.8 %collective-permute-done.1.refs_2_ = bf16[2,48,768]{2,1,0:T(8,128)(2,1)S(1)} collective-permute-done((bf16[2,48,768]{2,1,0:T(8,128)(2,1)S(1)}, bf16[2,48,768]{2,1,0:T(8,128)(2,1)S(1)}, u32[]{:S(2)}, u32[]{:S(2)}) %collective-permute-start.1) | collective-permute-done | bytes 147488 | tf_op jit(solution)/shard_map/ppermute | solution.py:458
  20.1 2.8 %collective-permute-start.10 = (bf16[2,48,768]{2,1,0:T(8,128)(2,1)S(1)}, bf16[2,48,768]{2,1,0:T(8,128)(2,1)S(1)}, u32[]{:S(2)}, u32[]{:S(2)}) collective-permute-start(bf16[2,48,768]{2,1,0:T(8,128)(2,1)S(1)} %get-tuple-element.142), channel_id=1, source_target_pairs={{0,24},{2,26},{4,28},{6,30},{8,16},{10,18},{12,20},{14,22},{16,8},... | collective-permute-start | bytes 442376 | tf_op jit(solution)/shard_map/ppermute | solution.py:458
  22.9 1.7 collective-permute-start.8
  28.8 5.3 %collective-permute-done.9 = bf16[2,48,768]{2,1,0:T(8,128)(2,1)S(1)} collective-permute-done((bf16[2,48,768]{2,1,0:T(8,128)(2,1)S(1)}, bf16[2,48,768]{2,1,0:T(8,128)(2,1)S(1)}, u32[]{:S(2)}, u32[]{:S(2)}) %collective-permute-start.9) | collective-permute-done | bytes 147488 | tf_op jit(solution)/shard_map/ppermute | solution.py:458
  39.0 2.9 %collective-permute-start.17 = (bf16[2,2,48,768]{3,2,1,0:T(8,128)(2,1)S(1)}, bf16[2,2,48,768]{3,2,1,0:T(8,128)(2,1)S(1)}, u32[]{:S(2)}, u32[]{:S(2)}) collective-permute-start(bf16[2,2,48,768]{3,2,1,0:T(8,128)(2,1)S(1)} %pad_maximum_fusion.4), channel_id=1, source_target_pairs={{0,8},{2,10},{4,12},{6,14},{8,0},{10,2},{12,4},{14,6},{16,24},{18,... | collective-permute-start | bytes 884744 | tf_op jit(solution)/shard_map/ppermute | solution.py:458
  42.0 6.9 %collective-permute-done.6.refs_3_ = bf16[8,48,768]{2,1,0:T(8,128)(2,1)S(1)} collective-permute-done((bf16[8,48,768]{2,1,0:T(8,128)(2,1)S(1)}, bf16[8,48,768]{2,1,0:T(8,128)(2,1)S(1)}, u32[]{:S(2)}, u32[]{:S(2)}) %collective-permute-start.6) | collective-permute-done | bytes 589856 | tf_op jit(solution)/shard_map/ppermute | solution.py:458
  52.3 4.9 %collective-permute-done.13 = bf16[4,48,768]{2,1,0:T(8,128)(2,1)S(1)} collective-permute-done((bf16[4,48,768]{2,1,0:T(8,128)(2,1)S(1)}, bf16[4,48,768]{2,1,0:T(8,128)(2,1)S(1)}, u32[]{:S(2)}, u32[]{:S(2)}) %collective-permute-start.13) | collective-permute-done | bytes 294944 | tf_op jit(solution)/shard_map/ppermute | solution.py:458
  57.8 2.0 collective-permute-done.11
  60.0 2.9 %collective-permute-done.18 = bf16[2,2,48,768]{3,2,1,0:T(8,128)(2,1)S(1)} collective-permute-done((bf16[2,2,48,768]{3,2,1,0:T(8,128)(2,1)S(1)}, bf16[2,2,48,768]{3,2,1,0:T(8,128)(2,1)S(1)}, u32[]{:S(2)}, u32[]{:S(2)}) %collective-permute-start.18) | collective-permute-done | bytes 294944 | tf_op jit(solution)/shard_map/ppermute | solution.py:458
  63.6 7.3 %shard_map.367 = (bf16[544,768]{1,0:T(8,128)(2,1)S(1)}, bf16[544,768]{1,0:T(8,128)(2,1)S(1)}, bf16[544,1152]{1,0:T(8,128)(2,1)S(1)}, f32[544,128]{1,0:T(8,128)S(1)}, bf16[544,384]{1,0:T(8,128)(2,1)S(1)}) custom-call(bf16[512,768]{1,0:T(8,128)(2,1)S(1)} %get-tuple-element.254.token_ref, f32[16,768]{1,0:T(8,128)S(1)} %broadcast_select_fusion.mem_ref.keep_ref, ...), custom_call_target="tpu_custom_call" | custom-call | tf_op jit(solution)/shard_map/pallas_call | solution.py:66
  73.3 13.6 %collective-permute-done.20.refs_1_ = bf16[8,48,768]{2,1,0:T(8,128)(2,1)S(1)} collective-permute-done((bf16[8,48,768]{2,1,0:T(8,128)(2,1)S(1)}, bf16[8,48,768]{2,1,0:T(8,128)(2,1)S(1)}, u32[]{:S(2)}, u32[]{:S(2)}) %collective-permute-start.20) | collective-permute-done | bytes 589856 | tf_op jit(solution)/shard_map/ppermute | solution.py:458
  87.4 5.3 %shard_map.371 = (bf16[544,768]{1,0:T(8,128)(2,1)S(1)}, f32[544,768]{1,0:T(8,128)S(1)}, bf16[544,768]{1,0:T(8,128)(2,1)S(1)}, bf16[544,1536]{1,0:T(8,128)(2,1)S(1)}, bf16[544,1536]{1,0:T(8,128)(2,1)S(1)}) custom-call(bf16[512,768]{1,0:T(8,128)(2,1)S(1)} %get-tuple-element.254.token_ref, f32[16,768]{1,0:T(8,128)S(1)} %broadcast_select_fusion.mem_ref.keep_ref, ...), custom_call_target="tpu_custom_call" | custom-call | tf_op jit(solution)/shard_map/pallas_call | solution.py:66
  93.3 1.7 collective-permute-done.22.other_ref
  95.0 7.9 %shard_map.372 = (bf16[512,768]{1,0:T(8,128)(2,1)S(1)}, f32[16,768]{1,0:T(8,128)S(1)}, f32[544,768]{1,0:T(8,128)S(1)}, bf16[544,768]{1,0:T(8,128)(2,1)S(1)}, bf1...) custom-call(f32[544,768]{1,0:T(8,128)S(1)} %get-tuple-element.150.fi, ...), custom_call_target="tpu_custom_call" | custom-call | tf_op jit(solution)/shard_map/pallas_call | solution.py:66
  103.2 2.2 collective-permute-done.23.other_ref
  105.4 5.4 %shard_map.373 = (bf16[544,768]{1,0:T(8,128)(2,1)S(1)}, f32[544,768]{1,0:T(8,128)S(1)}, bf16[544,768]{1,0:T(8,128)(2,1)S(1)}, bf16[544,1536]{1,0:T(8,128)(2,1)S(1)}, bf16[544,1536]{1,0:T(8,128)(2,1)S(1)}) custom-call(bf16[512,768]{1,0:T(8,128)(2,1)S(1)} %get-tuple-element.253.token_ref, f32[16,768]{1,0:T(8,128)S(1)} %get-tuple-element.153.mem_ref, ...), custom_call_target="tpu_custom_call" | custom-call | tf_op jit(solution)/shard_map/pallas_call | solution.py:66
  111.2 2.1 collective-permute-done.24.refs_3_
  113.3 5.7 %shard_map.374 = (bf16[2,512,768]{2,1,0:T(8,128)(2,1)}, bf16[544,768]{1,0:T(8,128)(2,1)S(1)}, f32[544,768]{1,0:T(8,128)S(1)}, bf16[544,768]{1,0:T(8,128)(2,1)S(1...) custom-call(bf16[512,768]{1,0:T(8,128)(2,1)S(1)} %get-tuple-element.152.refs_0_, ...), custom_call_target="tpu_custom_call" | custom-call | tf_op jit(solution)/shard_map/pallas_call | solution.py:66
  119.2 2.4 shard_map.375.refs_2_
  121.6 10.1 %shard_map.376 = (bf16[544,768]{1,0:T(8,128)(2,1)S(1)}, f32[544,768]{1,0:T(8,128)S(1)}, bf16[544,768]{1,0:T(8,128)(2,1)S(1)}, bf16[544,1152]{1,0:T(8,128)(2,1)S(...) custom-call(f32[544,768]{1,0:T(8,128)S(1)} %get-tuple-element.162.dsecond_ref, ...), custom_call_target="tpu_custom_call" | custom-call | tf_op jit(solution)/shard_map/pallas_call | solution.py:66
  132.2 2.0 collective-permute-done.26.other_ref
  134.2 5.4 %shard_map.377 = (bf16[512,768]{1,0:T(8,128)(2,1)S(1)}, f32[16,768]{1,0:T(8,128)S(1)}, bf16[544,768]{1,0:T(8,128)(2,1)S(1)}, f32[544,768]{1,0:T(8,128)S(1)}, bf1...) custom-call(f32[544,768]{1,0:T(8,128)S(1)} %get-tuple-element.166.dfirs, ...), custom_call_target="tpu_custom_call" | custom-call | tf_op jit(solution)/shard_map/pallas_call | solution.py:66
  140.0 3.4 %shard_map.378 = (bf16[8,48,768]{2,1,0:T(8,128)(2,1)S(1)}, bf16[8,48,768]{2,1,0:T(8,128)(2,1)S(1)}, bf16[8,48,768]{2,1,0:T(8,128)(2,1)S(1)}, bf16[8,48,768]{2,1,0:T(8,128)(2,1)S(1)}) custom-call(s32[1]{0:T(128)} %bitcast.1.me_ref, bf16[544,768]{1,0:T(8,128)(2,1)S(1)} %get-tuple-element.171.refs_0_, bf16[544,1536]{1,0:T(8,128)(2,1)S(1)} %get-tuple-element.172.refs_1_, ...), custom_call_target="tpu_custom_call" | custom-call | tf_op jit(solution)/shard_map/pallas_call | solution.py:66
  145.5 5.1 %shard_map.379 = (bf16[8,48,768]{2,1,0:T(8,128)(2,1)S(1)}, bf16[8,48,768]{2,1,0:T(8,128)(2,1)S(1)}, bf16[8,48,768]{2,1,0:T(8,128)(2,1)S(1)}, bf16[8,48,768]{2,1,0:T(8,128)(2,1)S(1)}) custom-call(s32[1]{0:T(128)} %bitcast.1.me_ref, bf16[544,768]{1,0:T(8,128)(2,1)S(1)} %get-tuple-element.174.refs_0_, bf16[544,768]{1,0:T(8,128)(2,1)S(1)} %get-tuple-element.175.refs_1_, ...), custom_call_target="tpu_custom_call" | custom-call | tf_op jit(solution)/shard_map/pallas_call | solution.py:66
  152.7 10.2 %shard_map.380 = (bf16[544,768]{1,0:T(8,128)(2,1)S(1)}, f32[544,768]{1,0:T(8,128)S(1)}, bf16[544,768]{1,0:T(8,128)(2,1)S(1)}, bf16[544,1152]{1,0:T(8,128)(2,1)S(...) custom-call(f32[544,768]{1,0:T(8,128)S(1)} %get-tuple-element.179.dsecond_ref, ...), custom_call_target="tpu_custom_call" | custom-call | tf_op jit(solution)/shard_map/pallas_call | solution.py:66
  163.2 9.5 %collective-permute-done.31 = bf16[8,48,768]{2,1,0:T(8,128)(2,1)S(1)} collective-permute-done((bf16[8,48,768]{2,1,0:T(8,128)(2,1)S(1)}, bf16[8,48,768]{2,1,0:T(8,128)(2,1)S(1)}, u32[]{:S(2)}, u32[]{:S(2)}) %collective-permute-start.31) | collective-permute-done | bytes 589856 | tf_op jit(solution)/shard_map/ppermute | solution.py:458
  177.3 6.2 %shard_map.382 = (bf16[8,48,768]{2,1,0:T(8,128)(2,1)S(1)}, bf16[8,48,768]{2,1,0:T(8,128)(2,1)S(1)}, bf16[8,48,768]{2,1,0:T(8,128)(2,1)S(1)}, bf16[8,48,768]{2,1,0:T(8,128)(2,1)S(1)}) custom-call(s32[1]{0:T(128)} %bitcast.1.me_ref, bf16[544,768]{1,0:T(8,128)(2,1)S(1)} %get-tuple-element.191.refs_0_, bf16[544,768]{1,0:T(8,128)(2,1)S(1)} %get-tuple-element.192.refs_1_, ...), custom_call_target="tpu_custom_call" | custom-call | tf_op jit(solution)/shard_map/pallas_call | solution.py:66
  183.7 1.8 collective-permute-start.37
  185.5 7.0 %collective-permute-start.35 = (bf16[48,1536]{1,0:T(8,128)(2,1)S(1)}, bf16[48,1536]{1,0:T(8,128)(2,1)S(1)}, u32[]{:S(2)}, u32[]{:S(2)}) collective-permute-start(bf16[48,1536]{1,0:T(8,128)(2,1)S(1)} %get-tuple-element.265), channel_id=1, source_target_pairs={{0,8},{2,10},{4,12},{6,14},{8,0},{10,2},{12,4},{14,6},{16,24},{18,... | collective-permute-start | bytes 442376 | tf_op jit(solution)/shard_map/ppermute | solution.py:458
  194.6 1.6 collective-permute-start.42
  196.2 2.3 collective-permute-done.35.refs_1_
  198.6 3.4 %collective-permute-start.40 = (bf16[48,1536]{1,0:T(8,128)(2,1)S(1)}, bf16[48,1536]{1,0:T(8,128)(2,1)S(1)}, u32[]{:S(2)}, u32[]{:S(2)}) collective-permute-start(bf16[48,1536]{1,0:T(8,128)(2,1)S(1)} %get-tuple-element.261), channel_id=1, source_target_pairs={{0,8},{2,10},{4,12},{6,14},{8,0},{10,2},{12,4},{14,6},{16,24},{18,... | collective-permute-start | bytes 442376 | tf_op jit(solution)/shard_map/ppermute | solution.py:458
  202.0 5.4 %collective-permute-done.36.refs_2_ = bf16[48,1536]{1,0:T(8,128)(2,1)S(1)} collective-permute-done((bf16[48,1536]{1,0:T(8,128)(2,1)S(1)}, bf16[48,1536]{1,0:T(8,128)(2,1)S(1)}, u32[]{:S(2)}, u32[]{:S(2)}) %collective-permute-start.36) | collective-permute-done | bytes 147488 | tf_op jit(solution)/shard_map/ppermute | solution.py:458
  207.6 6.8 %collective-permute-done.41.refs_6_ = bf16[48,1536]{1,0:T(8,128)(2,1)S(1)} collective-permute-done((bf16[48,1536]{1,0:T(8,128)(2,1)S(1)}, bf16[48,1536]{1,0:T(8,128)(2,1)S(1)}, u32[]{:S(2)}, u32[]{:S(2)}) %collective-permute-start.41) | collective-permute-done | bytes 147488 | tf_op jit(solution)/shard_map/ppermute | solution.py:458
  215.1 2.0 collective-permute-start.46
  217.1 4.2 %collective-permute-done.44 = bf16[4,48,768]{2,1,0:T(8,128)(2,1)S(1)} collective-permute-done((bf16[4,48,768]{2,1,0:T(8,128)(2,1)S(1)}, bf16[4,48,768]{2,1,0:T(8,128)(2,1)S(1)}, u32[]{:S(2)}, u32[]{:S(2)}) %collective-permute-start.44) | collective-permute-done | bytes 294944 | tf_op jit(solution)/shard_map/ppermute | solution.py:458
  222.0 2.0 collective-permute-start.49
  224.0 2.5 collective-permute-start.48
  226.5 1.9 shard_map.381
  229.1 2.4 collective-permute-done.47.refs_9_
  231.5 1.9 collective-permute-done.48.refs_10_
  237.6 1.8 collective-permute-done.52
  240.6 2.1 collective-permute-start.55
  242.8 2.3 collective-permute-start.53
  245.1 1.8 collective-permute-done.55
  249.9 2.3 shard_map.384
  (183 shorter events, 49.3 us)
Async XLA Ops:
  2.5 13.8 %collective-permute-start.2 = (bf16[2,48,768]{2,1,0:T(8,128)(2,1)S(1)}, bf16[2,48,768]{2,1,0:T(8,128)(2,1)S(1)}, u32[]{:S(2)}, u32[]{:S(2)}) collective-permute-start(bf16[2,48,768]{2,1,0:T(8,128)(2,1)S(1)} %shard_map.364.refs_0_), channel_id=1, source_target_pairs={{0,24},{2,26},{4,28},{6,30},{8,16},{10,18},{12,20},{14,22},{16,8},... | collective-permute-start | bytes 442376 | tf_op jit(solution)/shard_map/ppermute | solution.py:458
  7.6 12.5 %collective-permute-start.1 = (bf16[2,48,768]{2,1,0:T(8,128)(2,1)S(1)}, bf16[2,48,768]{2,1,0:T(8,128)(2,1)S(1)}, u32[]{:S(2)}, u32[]{:S(2)}) collective-permute-start(bf16[2,48,768]{2,1,0:T(8,128)(2,1)S(1)} %shard_map.364.refs_0_), channel_id=1, source_target_pairs={{0,16},{2,18},{4,20},{6,22},{8,24},{10,26},{12,28},{14,30},{16,0},... | collective-permute-start | bytes 442376 | tf_op jit(solution)/shard_map/ppermute | solution.py:458
  7.6 12.5 %collective-permute-start = (bf16[2,48,768]{2,1,0:T(8,128)(2,1)S(1)}, bf16[2,48,768]{2,1,0:T(8,128)(2,1)S(1)}, u32[]{:S(2)}, u32[]{:S(2)}) collective-permute-start(bf16[2,48,768]{2,1,0:T(8,128)(2,1)S(1)} %shard_map.364.refs_0_), channel_id=1, source_target_pairs={{0,8},{2,10},{4,12},{6,14},{8,0},{10,2},{12,4},{14,6},{16,24},{18,... | collective-permute-start | bytes 442376 | tf_op jit(solution)/shard_map/ppermute | solution.py:458
  10.2 4.8 %collective-permute-start.15 = (bf16[48,768]{1,0:T(8,128)(2,1)S(1)}, bf16[48,768]{1,0:T(8,128)(2,1)S(1)}, u32[]{:S(2)}, u32[]{:S(2)}) collective-permute-start(bf16[48,768]{1,0:T(8,128)(2,1)S(1)} %get-tuple-element.145), channel_id=1, source_target_pairs={{0,2},{2,0},{4,6},{6,4},{8,10},{10,8},{12,14},{14,12},{16,18},{18,... | collective-permute-start | bytes 221192 | tf_op jit(solution)/shard_map/ppermute | solution.py:458
  20.1 8.6 %collective-permute-start.10 = (bf16[2,48,768]{2,1,0:T(8,128)(2,1)S(1)}, bf16[2,48,768]{2,1,0:T(8,128)(2,1)S(1)}, u32[]{:S(2)}, u32[]{:S(2)}) collective-permute-start(bf16[2,48,768]{2,1,0:T(8,128)(2,1)S(1)} %get-tuple-element.142), channel_id=1, source_target_pairs={{0,24},{2,26},{4,28},{6,30},{8,16},{10,18},{12,20},{14,22},{16,8},... | collective-permute-start | bytes 442376 | tf_op jit(solution)/shard_map/ppermute | solution.py:458
  22.9 11.2 %collective-permute-start.9 = (bf16[2,48,768]{2,1,0:T(8,128)(2,1)S(1)}, bf16[2,48,768]{2,1,0:T(8,128)(2,1)S(1)}, u32[]{:S(2)}, u32[]{:S(2)}) collective-permute-start(bf16[2,48,768]{2,1,0:T(8,128)(2,1)S(1)} %get-tuple-element.142), channel_id=1, source_target_pairs={{0,16},{2,18},{4,20},{6,22},{8,24},{10,26},{12,28},{14,30},{16,0},... | collective-permute-start | bytes 442376 | tf_op jit(solution)/shard_map/ppermute | solution.py:458
  22.9 14.5 %collective-permute-start.8 = (bf16[2,48,768]{2,1,0:T(8,128)(2,1)S(1)}, bf16[2,48,768]{2,1,0:T(8,128)(2,1)S(1)}, u32[]{:S(2)}, u32[]{:S(2)}) collective-permute-start(bf16[2,48,768]{2,1,0:T(8,128)(2,1)S(1)} %get-tuple-element.142), channel_id=1, source_target_pairs={{0,8},{2,10},{4,12},{6,14},{8,0},{10,2},{12,4},{14,6},{16,24},{18,... | collective-permute-start | bytes 442376 | tf_op jit(solution)/shard_map/ppermute | solution.py:458
  24.6 11.1 %collective-permute-start.3 = (bf16[4,48,768]{2,1,0:T(8,128)(2,1)S(1)}, bf16[4,48,768]{2,1,0:T(8,128)(2,1)S(1)}, u32[]{:S(2)}, u32[]{:S(2)}) collective-permute-start(bf16[4,48,768]{2,1,0:T(8,128)(2,1)S(1)} %get-tuple-element.136), channel_id=1, source_target_pairs={{0,4},{2,6},{4,0},{6,2},{8,12},{10,14},{12,8},{14,10},{16,20},{18,... | collective-permute-start | bytes 884744 | tf_op jit(solution)/shard_map/ppermute | solution.py:458
  26.2 7.9 %collective-permute-start.5 = (bf16[4,48,768]{2,1,0:T(8,128)(2,1)S(1)}, bf16[4,48,768]{2,1,0:T(8,128)(2,1)S(1)}, u32[]{:S(2)}, u32[]{:S(2)}) collective-permute-start(bf16[4,48,768]{2,1,0:T(8,128)(2,1)S(1)} %get-tuple-element.137), channel_id=1, source_target_pairs={{0,2},{2,0},{4,6},{6,4},{8,10},{10,8},{12,14},{14,12},{16,18},{18,... | collective-permute-start | bytes 884744 | tf_op jit(solution)/shard_map/ppermute | solution.py:458
  34.2 14.7 %collective-permute-start.6 = (bf16[8,48,768]{2,1,0:T(8,128)(2,1)S(1)}, bf16[8,48,768]{2,1,0:T(8,128)(2,1)S(1)}, u32[]{:S(2)}, u32[]{:S(2)}) collective-permute-start(bf16[8,48,768]{2,1,0:T(8,128)(2,1)S(1)} %constant_dynamic-update-slice_fusion.2.refs_2_), channel_id=1, source_target_pairs={{0,4},{2,6},{4,0},{6,2},{8,12},{10,14},{12,8},{14,10},{16,20},{18,... | collective-permute-start | bytes 1769480 | tf_op jit(solution)/shard_map/ppermute | solution.py:458
  35.8 14.4 %collective-permute-start.4 = (bf16[8,48,768]{2,1,0:T(8,128)(2,1)S(1)}, bf16[8,48,768]{2,1,0:T(8,128)(2,1)S(1)}, u32[]{:S(2)}, u32[]{:S(2)}) collective-permute-start(bf16[8,48,768]{2,1,0:T(8,128)(2,1)S(1)} %constant_dynamic-update-slice_fusion.refs_0_), channel_id=1, source_target_pairs={{0,2},{2,0},{4,6},{6,4},{8,10},{10,8},{12,14},{14,12},{16,18},{18,... | collective-permute-start | bytes 1769480 | tf_op jit(solution)/shard_map/ppermute | solution.py:458
  37.4 14.3 %collective-permute-start.19 = (bf16[2,2,48,768]{3,2,1,0:T(8,128)(2,1)S(1)}, bf16[2,2,48,768]{3,2,1,0:T(8,128)(2,1)S(1)}, u32[]{:S(2)}, u32[]{:S(2)}) collective-permute-start(bf16[2,2,48,768]{3,2,1,0:T(8,128)(2,1)S(1)} %pad_maximum_fusion.4), channel_id=1, source_target_pairs={{0,24},{2,26},{4,28},{6,30},{8,16},{10,18},{12,20},{14,22},{16,8},... | collective-permute-start | bytes 884744 | tf_op jit(solution)/shard_map/ppermute | solution.py:458
  39.0 23.9 %collective-permute-start.18 = (bf16[2,2,48,768]{3,2,1,0:T(8,128)(2,1)S(1)}, bf16[2,2,48,768]{3,2,1,0:T(8,128)(2,1)S(1)}, u32[]{:S(2)}, u32[]{:S(2)}) collective-permute-start(bf16[2,2,48,768]{3,2,1,0:T(8,128)(2,1)S(1)} %pad_maximum_fusion.4), channel_id=1, source_target_pairs={{0,16},{2,18},{4,20},{6,22},{8,24},{10,26},{12,28},{14,30},{16,0},... | collective-permute-start | bytes 884744 | tf_op jit(solution)/shard_map/ppermute | solution.py:458
  39.0 31.9 %collective-permute-start.17 = (bf16[2,2,48,768]{3,2,1,0:T(8,128)(2,1)S(1)}, bf16[2,2,48,768]{3,2,1,0:T(8,128)(2,1)S(1)}, u32[]{:S(2)}, u32[]{:S(2)}) collective-permute-start(bf16[2,2,48,768]{3,2,1,0:T(8,128)(2,1)S(1)} %pad_maximum_fusion.4), channel_id=1, source_target_pairs={{0,8},{2,10},{4,12},{6,14},{8,0},{10,2},{12,4},{14,6},{16,24},{18,... | collective-permute-start | bytes 884744 | tf_op jit(solution)/shard_map/ppermute | solution.py:458
  50.2 7.1 %collective-permute-start.13 = (bf16[4,48,768]{2,1,0:T(8,128)(2,1)S(1)}, bf16[4,48,768]{2,1,0:T(8,128)(2,1)S(1)}, u32[]{:S(2)}, u32[]{:S(2)}) collective-permute-start(bf16[4,48,768]{2,1,0:T(8,128)(2,1)S(1)} %get-tuple-element.144), channel_id=1, source_target_pairs={{0,2},{2,0},{4,6},{6,4},{8,10},{10,8},{12,14},{14,12},{16,18},{18,... | collective-permute-start | bytes 884744 | tf_op jit(solution)/shard_map/ppermute | solution.py:458
  51.7 8.2 %collective-permute-start.11 = (bf16[4,48,768]{2,1,0:T(8,128)(2,1)S(1)}, bf16[4,48,768]{2,1,0:T(8,128)(2,1)S(1)}, u32[]{:S(2)}, u32[]{:S(2)}) collective-permute-start(bf16[4,48,768]{2,1,0:T(8,128)(2,1)S(1)} %get-tuple-element.143), channel_id=1, source_target_pairs={{0,4},{2,6},{4,0},{6,2},{8,12},{10,14},{12,8},{14,10},{16,20},{18,... | collective-permute-start | bytes 884744 | tf_op jit(solution)/shard_map/ppermute | solution.py:458
  57.3 13.9 %collective-permute-start.14 = (bf16[8,48,768]{2,1,0:T(8,128)(2,1)S(1)}, bf16[8,48,768]{2,1,0:T(8,128)(2,1)S(1)}, u32[]{:S(2)}, u32[]{:S(2)}) collective-permute-start(bf16[8,48,768]{2,1,0:T(8,128)(2,1)S(1)} %constant_dynamic-update-slice_fusion.6.refs_2_), channel_id=1, source_target_pairs={{0,4},{2,6},{4,0},{6,2},{8,12},{10,14},{12,8},{14,10},{16,20},{18,... | collective-permute-start | bytes 1769480 | tf_op jit(solution)/shard_map/ppermute | solution.py:458
  59.9 11.3 %collective-permute-start.12 = (bf16[8,48,768]{2,1,0:T(8,128)(2,1)S(1)}, bf16[8,48,768]{2,1,0:T(8,128)(2,1)S(1)}, u32[]{:S(2)}, u32[]{:S(2)}) collective-permute-start(bf16[8,48,768]{2,1,0:T(8,128)(2,1)S(1)} %constant_dynamic-update-slice_fusion.4.refs_0_), channel_id=1, source_target_pairs={{0,2},{2,0},{4,6},{6,4},{8,10},{10,8},{12,14},{14,12},{16,18},{18,... | collective-permute-start | bytes 1769480 | tf_op jit(solution)/shard_map/ppermute | solution.py:458
  70.9 16.5 %collective-permute-start.7 = (bf16[544,768]{1,0:T(8,128)(2,1)S(1)}, bf16[544,768]{1,0:T(8,128)(2,1)S(1)}, u32[]{:S(2)}, u32[]{:S(2)}) collective-permute-start(bf16[544,768]{1,0:T(8,128)(2,1)S(1)} %get-tuple-element.140.own_ref), channel_id=1, source_target_pairs={{0,1},{1,0},{2,3},{3,2},{4,5},{5,4},{6,7},{7,6},{8,9},{9,8},{10,11... | collective-permute-start | bytes 2506760 | tf_op jit(solution)/shard_map/ppermute | solution.py:458
  71.2 15.8 %collective-permute-start.20 = (bf16[8,48,768]{2,1,0:T(8,128)(2,1)S(1)}, bf16[8,48,768]{2,1,0:T(8,128)(2,1)S(1)}, u32[]{:S(2)}, u32[]{:S(2)}) collective-permute-start(bf16[8,48,768]{2,1,0:T(8,128)(2,1)S(1)} %get-tuple-element.148.refs_0_), channel_id=1, source_target_pairs={{0,4},{2,6},{4,0},{6,2},{8,12},{10,14},{12,8},{14,10},{16,20},{18,... | collective-permute-start | bytes 1769480 | tf_op jit(solution)/shard_map/ppermute | solution.py:458
  71.7 15.4 %collective-permute-start.21 = (bf16[8,48,768]{2,1,0:T(8,128)(2,1)S(1)}, bf16[8,48,768]{2,1,0:T(8,128)(2,1)S(1)}, u32[]{:S(2)}, u32[]{:S(2)}) collective-permute-start(bf16[8,48,768]{2,1,0:T(8,128)(2,1)S(1)} %get-tuple-element.149.refs_2_), channel_id=1, source_target_pairs={{0,2},{2,0},{4,6},{6,4},{8,10},{10,8},{12,14},{14,12},{16,18},{18,... | collective-permute-start | bytes 1769480 | tf_op jit(solution)/shard_map/ppermute | solution.py:458
  139.6 13.1 %collective-permute-start.27 = (bf16[544,768]{1,0:T(8,128)(2,1)S(1)}, bf16[544,768]{1,0:T(8,128)(2,1)S(1)}, u32[]{:S(2)}, u32[]{:S(2)}) collective-permute-start(bf16[544,768]{1,0:T(8,128)(2,1)S(1)} %get-tuple-element.180.own_ref), channel_id=1, source_target_pairs={{0,1},{1,0},{2,3},{3,2},{4,5},{5,4},{6,7},{7,6},{8,9},{9,8},{10,11... | collective-permute-start | bytes 2506760 | tf_op jit(solution)/shard_map/ppermute | solution.py:458
  143.4 19.5 %collective-permute-start.32 = (bf16[8,48,768]{2,1,0:T(8,128)(2,1)S(1)}, bf16[8,48,768]{2,1,0:T(8,128)(2,1)S(1)}, u32[]{:S(2)}, u32[]{:S(2)}) collective-permute-start(bf16[8,48,768]{2,1,0:T(8,128)(2,1)S(1)} %get-tuple-element.195), channel_id=1, source_target_pairs={{0,4},{2,6},{4,0},{6,2},{8,12},{10,14},{12,8},{14,10},{16,20},{18,... | collective-permute-start | bytes 1769480 | tf_op jit(solution)/shard_map/ppermute | solution.py:458
  145.0 18.1 %collective-permute-start.29 = (bf16[8,48,768]{2,1,0:T(8,128)(2,1)S(1)}, bf16[8,48,768]{2,1,0:T(8,128)(2,1)S(1)}, u32[]{:S(2)}, u32[]{:S(2)}) collective-permute-start(bf16[8,48,768]{2,1,0:T(8,128)(2,1)S(1)} %get-tuple-element.188), channel_id=1, source_target_pairs={{0,2},{2,0},{4,6},{6,4},{8,10},{10,8},{12,14},{14,12},{16,18},{18,... | collective-permute-start | bytes 1769480 | tf_op jit(solution)/shard_map/ppermute | solution.py:458
  150.6 22.1 %collective-permute-start.31 = (bf16[8,48,768]{2,1,0:T(8,128)(2,1)S(1)}, bf16[8,48,768]{2,1,0:T(8,128)(2,1)S(1)}, u32[]{:S(2)}, u32[]{:S(2)}) collective-permute-start(bf16[8,48,768]{2,1,0:T(8,128)(2,1)S(1)} %get-tuple-element.193), channel_id=1, source_target_pairs={{0,2},{2,0},{4,6},{6,4},{8,10},{10,8},{12,14},{14,12},{16,18},{18,... | collective-permute-start | bytes 1769480 | tf_op jit(solution)/shard_map/ppermute | solution.py:458
  152.2 21.2 %collective-permute-start.33 = (bf16[8,48,768]{2,1,0:T(8,128)(2,1)S(1)}, bf16[8,48,768]{2,1,0:T(8,128)(2,1)S(1)}, u32[]{:S(2)}, u32[]{:S(2)}) collective-permute-start(bf16[8,48,768]{2,1,0:T(8,128)(2,1)S(1)} %get-tuple-element.199), channel_id=1, source_target_pairs={{0,4},{2,6},{4,0},{6,2},{8,12},{10,14},{12,8},{14,10},{16,20},{18,... | collective-permute-start | bytes 1769480 | tf_op jit(solution)/shard_map/ppermute | solution.py:458
  172.7 10.8 %collective-permute-start.34 = (bf16[4,48,768]{2,1,0:T(8,128)(2,1)S(1)}, bf16[4,48,768]{2,1,0:T(8,128)(2,1)S(1)}, u32[]{:S(2)}, u32[]{:S(2)}) collective-permute-start(bf16[4,48,768]{2,1,0:T(8,128)(2,1)S(1)} %slice.193), channel_id=1, source_target_pairs={{0,2},{2,0},{4,6},{6,4},{8,10},{10,8},{12,14},{14,12},{16,18},{18,... | collective-permute-start | bytes 884744 | tf_op jit(solution)/shard_map/ppermute | solution.py:458
  173.4 10.1 %collective-permute-start.30 = (bf16[4,48,768]{2,1,0:T(8,128)(2,1)S(1)}, bf16[4,48,768]{2,1,0:T(8,128)(2,1)S(1)}, u32[]{:S(2)}, u32[]{:S(2)}) collective-permute-start(bf16[4,48,768]{2,1,0:T(8,128)(2,1)S(1)} %slice.191), channel_id=1, source_target_pairs={{0,4},{2,6},{4,0},{6,2},{8,12},{10,14},{12,8},{14,10},{16,20},{18,... | collective-permute-start | bytes 884744 | tf_op jit(solution)/shard_map/ppermute | solution.py:458
  174.2 18.3 %collective-permute-start.39 = (bf16[4,48,768]{2,1,0:T(8,128)(2,1)S(1)}, bf16[4,48,768]{2,1,0:T(8,128)(2,1)S(1)}, u32[]{:S(2)}, u32[]{:S(2)}) collective-permute-start(bf16[4,48,768]{2,1,0:T(8,128)(2,1)S(1)} %slice.203), channel_id=1, source_target_pairs={{0,2},{2,0},{4,6},{6,4},{8,10},{10,8},{12,14},{14,12},{16,18},{18,... | collective-permute-start | bytes 884744 | tf_op jit(solution)/shard_map/ppermute | solution.py:458
  175.7 16.8 %collective-permute-start.38 = (bf16[4,48,768]{2,1,0:T(8,128)(2,1)S(1)}, bf16[4,48,768]{2,1,0:T(8,128)(2,1)S(1)}, u32[]{:S(2)}, u32[]{:S(2)}) collective-permute-start(bf16[4,48,768]{2,1,0:T(8,128)(2,1)S(1)} %slice.201), channel_id=1, source_target_pairs={{0,4},{2,6},{4,0},{6,2},{8,12},{10,14},{12,8},{14,10},{16,20},{18,... | collective-permute-start | bytes 884744 | tf_op jit(solution)/shard_map/ppermute | solution.py:458
  183.7 10.9 %collective-permute-start.37 = (bf16[48,1536]{1,0:T(8,128)(2,1)S(1)}, bf16[48,1536]{1,0:T(8,128)(2,1)S(1)}, u32[]{:S(2)}, u32[]{:S(2)}) collective-permute-start(bf16[48,1536]{1,0:T(8,128)(2,1)S(1)} %get-tuple-element.263), channel_id=1, source_target_pairs={{0,24},{2,26},{4,28},{6,30},{8,16},{10,18},{12,20},{14,22},{16,8},... | collective-permute-start | bytes 442376 | tf_op jit(solution)/shard_map/ppermute | solution.py:458
  185.5 13.1 %collective-permute-start.35 = (bf16[48,1536]{1,0:T(8,128)(2,1)S(1)}, bf16[48,1536]{1,0:T(8,128)(2,1)S(1)}, u32[]{:S(2)}, u32[]{:S(2)}) collective-permute-start(bf16[48,1536]{1,0:T(8,128)(2,1)S(1)} %get-tuple-element.265), channel_id=1, source_target_pairs={{0,8},{2,10},{4,12},{6,14},{8,0},{10,2},{12,4},{14,6},{16,24},{18,... | collective-permute-start | bytes 442376 | tf_op jit(solution)/shard_map/ppermute | solution.py:458
  192.5 14.9 %collective-permute-start.36 = (bf16[48,1536]{1,0:T(8,128)(2,1)S(1)}, bf16[48,1536]{1,0:T(8,128)(2,1)S(1)}, u32[]{:S(2)}, u32[]{:S(2)}) collective-permute-start(bf16[48,1536]{1,0:T(8,128)(2,1)S(1)} %get-tuple-element.266), channel_id=1, source_target_pairs={{0,16},{2,18},{4,20},{6,22},{8,24},{10,26},{12,28},{14,30},{16,0},... | collective-permute-start | bytes 442376 | tf_op jit(solution)/shard_map/ppermute | solution.py:458
  192.5 21.8 %collective-permute-start.43 = (bf16[8,48,768]{2,1,0:T(8,128)(2,1)S(1)}, bf16[8,48,768]{2,1,0:T(8,128)(2,1)S(1)}, u32[]{:S(2)}, u32[]{:S(2)}) collective-permute-start(bf16[8,48,768]{2,1,0:T(8,128)(2,1)S(1)} %get-tuple-element.212), channel_id=1, source_target_pairs={{0,2},{2,0},{4,6},{6,4},{8,10},{10,8},{12,14},{14,12},{16,18},{18,... | collective-permute-start | bytes 1769480 | tf_op jit(solution)/shard_map/ppermute | solution.py:458
  193.2 21.7 %collective-permute-start.45 = (bf16[8,48,768]{2,1,0:T(8,128)(2,1)S(1)}, bf16[8,48,768]{2,1,0:T(8,128)(2,1)S(1)}, u32[]{:S(2)}, u32[]{:S(2)}) collective-permute-start(bf16[8,48,768]{2,1,0:T(8,128)(2,1)S(1)} %get-tuple-element.217), channel_id=1, source_target_pairs={{0,4},{2,6},{4,0},{6,2},{8,12},{10,14},{12,8},{14,10},{16,20},{18,... | collective-permute-start | bytes 1769480 | tf_op jit(solution)/shard_map/ppermute | solution.py:458
  194.6 12.7 %collective-permute-start.42 = (bf16[48,1536]{1,0:T(8,128)(2,1)S(1)}, bf16[48,1536]{1,0:T(8,128)(2,1)S(1)}, u32[]{:S(2)}, u32[]{:S(2)}) collective-permute-start(bf16[48,1536]{1,0:T(8,128)(2,1)S(1)} %get-tuple-element.259), channel_id=1, source_target_pairs={{0,24},{2,26},{4,28},{6,30},{8,16},{10,18},{12,20},{14,22},{16,8},... | collective-permute-start | bytes 442376 | tf_op jit(solution)/shard_map/ppermute | solution.py:458
  198.6 9.0 %collective-permute-start.40 = (bf16[48,1536]{1,0:T(8,128)(2,1)S(1)}, bf16[48,1536]{1,0:T(8,128)(2,1)S(1)}, u32[]{:S(2)}, u32[]{:S(2)}) collective-permute-start(bf16[48,1536]{1,0:T(8,128)(2,1)S(1)} %get-tuple-element.261), channel_id=1, source_target_pairs={{0,8},{2,10},{4,12},{6,14},{8,0},{10,2},{12,4},{14,6},{16,24},{18,... | collective-permute-start | bytes 442376 | tf_op jit(solution)/shard_map/ppermute | solution.py:458
  207.4 6.9 %collective-permute-start.41 = (bf16[48,1536]{1,0:T(8,128)(2,1)S(1)}, bf16[48,1536]{1,0:T(8,128)(2,1)S(1)}, u32[]{:S(2)}, u32[]{:S(2)}) collective-permute-start(bf16[48,1536]{1,0:T(8,128)(2,1)S(1)} %get-tuple-element.262), channel_id=1, source_target_pairs={{0,16},{2,18},{4,20},{6,22},{8,24},{10,26},{12,28},{14,30},{16,0},... | collective-permute-start | bytes 442376 | tf_op jit(solution)/shard_map/ppermute | solution.py:458
  214.5 6.8 %collective-permute-start.44 = (bf16[4,48,768]{2,1,0:T(8,128)(2,1)S(1)}, bf16[4,48,768]{2,1,0:T(8,128)(2,1)S(1)}, u32[]{:S(2)}, u32[]{:S(2)}) collective-permute-start(bf16[4,48,768]{2,1,0:T(8,128)(2,1)S(1)} %slice.211), channel_id=1, source_target_pairs={{0,4},{2,6},{4,0},{6,2},{8,12},{10,14},{12,8},{14,10},{16,20},{18,... | collective-permute-start | bytes 884744 | tf_op jit(solution)/shard_map/ppermute | solution.py:458
  215.1 6.8 %collective-permute-start.46 = (bf16[4,48,768]{2,1,0:T(8,128)(2,1)S(1)}, bf16[4,48,768]{2,1,0:T(8,128)(2,1)S(1)}, u32[]{:S(2)}, u32[]{:S(2)}) collective-permute-start(bf16[4,48,768]{2,1,0:T(8,128)(2,1)S(1)} %slice.213), channel_id=1, source_target_pairs={{0,2},{2,0},{4,6},{6,4},{8,10},{10,8},{12,14},{14,12},{16,18},{18,... | collective-permute-start | bytes 884744 | tf_op jit(solution)/shard_map/ppermute | solution.py:458
  217.1 9.4 %collective-permute-start.28 = (bf16[544,768]{1,0:T(8,128)(2,1)S(1)}, bf16[544,768]{1,0:T(8,128)(2,1)S(1)}, u32[]{:S(2)}, u32[]{:S(2)}) collective-permute-start(bf16[544,768]{1,0:T(8,128)(2,1)S(1)} %get-tuple-element.184.own_ref), channel_id=1, source_target_pairs={{0,1},{1,0},{2,3},{3,2},{4,5},{5,4},{6,7},{7,6},{8,9},{9,8},{10,11... | collective-permute-start | bytes 2506760 | tf_op jit(solution)/shard_map/ppermute | solution.py:458
  222.0 7.1 %collective-permute-start.49 = (bf16[48,1536]{1,0:T(8,128)(2,1)S(1)}, bf16[48,1536]{1,0:T(8,128)(2,1)S(1)}, u32[]{:S(2)}, u32[]{:S(2)}) collective-permute-start(bf16[48,1536]{1,0:T(8,128)(2,1)S(1)} %get-tuple-element.255), channel_id=1, source_target_pairs={{0,24},{2,26},{4,28},{6,30},{8,16},{10,18},{12,20},{14,22},{16,8},... | collective-permute-start | bytes 442376 | tf_op jit(solution)/shard_map/ppermute | solution.py:458
  224.0 7.5 %collective-permute-start.47 = (bf16[48,1536]{1,0:T(8,128)(2,1)S(1)}, bf16[48,1536]{1,0:T(8,128)(2,1)S(1)}, u32[]{:S(2)}, u32[]{:S(2)}) collective-permute-start(bf16[48,1536]{1,0:T(8,128)(2,1)S(1)} %get-tuple-element.257), channel_id=1, source_target_pairs={{0,8},{2,10},{4,12},{6,14},{8,0},{10,2},{12,4},{14,6},{16,24},{18,... | collective-permute-start | bytes 442376 | tf_op jit(solution)/shard_map/ppermute | solution.py:458
  224.0 9.4 %collective-permute-start.48 = (bf16[48,1536]{1,0:T(8,128)(2,1)S(1)}, bf16[48,1536]{1,0:T(8,128)(2,1)S(1)}, u32[]{:S(2)}, u32[]{:S(2)}) collective-permute-start(bf16[48,1536]{1,0:T(8,128)(2,1)S(1)} %get-tuple-element.258), channel_id=1, source_target_pairs={{0,16},{2,18},{4,20},{6,22},{8,24},{10,26},{12,28},{14,30},{16,0},... | collective-permute-start | bytes 442376 | tf_op jit(solution)/shard_map/ppermute | solution.py:458
  234.0 5.3 %collective-permute-start.52 = (f32[24,768]{1,0:T(8,128)S(1)}, f32[24,768]{1,0:T(8,128)S(1)}, u32[]{:S(2)}, u32[]{:S(2)}) collective-permute-start(f32[24,768]{1,0:T(8,128)S(1)} %get-tuple-element.228), channel_id=1, source_target_pairs={{0,6},{2,4},{4,2},{6,0},{8,14},{10,12},{12,10},{14,8},{16,22},{18,... | collective-permute-start | bytes 221192 | tf_op jit(solution)/shard_map/ppermute | solution.py:458
  240.6 6.2 %collective-permute-start.55 = (f32[24,768]{1,0:T(8,128)S(1)}, f32[24,768]{1,0:T(8,128)S(1)}, u32[]{:S(2)}, u32[]{:S(2)}) collective-permute-start(f32[24,768]{1,0:T(8,128)S(1)} %add_add_fusion.1), channel_id=1, source_target_pairs={{0,24},{2,26},{4,28},{6,30},{8,16},{10,18},{12,20},{14,22},{16,8},... | collective-permute-start | bytes 221192 | tf_op jit(solution)/shard_map/ppermute | solution.py:458
  242.7 5.7 %collective-permute-start.54 = (f32[24,768]{1,0:T(8,128)S(1)}, f32[24,768]{1,0:T(8,128)S(1)}, u32[]{:S(2)}, u32[]{:S(2)}) collective-permute-start(f32[24,768]{1,0:T(8,128)S(1)} %add_add_fusion.1), channel_id=1, source_target_pairs={{0,16},{2,18},{4,20},{6,22},{8,24},{10,26},{12,28},{14,30},{16,0},... | collective-permute-start | bytes 221192 | tf_op jit(solution)/shard_map/ppermute | solution.py:458
  242.8 5.7 %collective-permute-start.53 = (f32[24,768]{1,0:T(8,128)S(1)}, f32[24,768]{1,0:T(8,128)S(1)}, u32[]{:S(2)}, u32[]{:S(2)}) collective-permute-start(f32[24,768]{1,0:T(8,128)S(1)} %add_add_fusion.1), channel_id=1, source_target_pairs={{0,8},{2,10},{4,12},{6,14},{8,0},{10,2},{12,4},{14,6},{16,24},{18,... | collective-permute-start | bytes 221192 | tf_op jit(solution)/shard_map/ppermute | solution.py:458
  (33 other events, 319.9 us)

commit v4 on v3

--- a/solution.py
+++ b/solution.py
@@ -437,8 +437,13 @@
             def rows_of(step, carry, left=left, right=right, start=start, size=size, at=at):
                 begin = pl.multiple_of(step * CHUNK, CHUNK)
                 total = None if base is None else refs[base][pl.ds(begin, CHUNK), start : start + size]
-                for one, two in zip(left, right):
-                    add = dot_tn(refs[one][:, pl.ds(begin, CHUNK)], refs[two][:, start : start + size])
+                tokens = refs[left[0]].shape[0] - 2 * PAD
+                operands = [(refs[a][:, pl.ds(begin, CHUNK)], refs[b][:, start : start + size]) for a, b in zip(left, right)]
+                if len(operands) > 1:
+                    tails = [jnp.concatenate([pair[i][tokens:] for pair in operands], axis=0) for i in range(2)]
+                    operands = [(a[:tokens], b[:tokens]) for a, b in operands] + [tails]
+                for one, two in operands:
+                    add = dot_tn(one, two)
                     total = add if total is None else total + add
                 total_ref[pl.ds(begin, CHUNK), at : at + size] = total
                 return carry

time: 256 us -> 255 us (level)
  waiting for transfers between devices: 92.7 us -> 95.5 us
    ppermute x57, waiting for transfers between devices: 92.7 us -> 95.5 us  [exchange(): return lax.ppermute(values, axis, [(i, i ^ flip) for i in range(size)])]
  transfers between devices with their start and end apart: 57 -> 57, of which waited for: 31 -> 32; matrix products, arithmetic and copies ran while one was open for 2% -> 2% of each run, Pallas kernels for 15% -> 14%
where the time goes in v4:
time: 255 us; the launch traced here: 252 us
  waiting for transfers between devices  95.5 us (37%)
  Pallas kernels  78.6 us (31%)
  starting transfers between devices  67.4 us (26%)
  local copies, waits for them, and re-layouts  6.33 us (2%)
    ppermute x57, waiting for transfers between devices, exchange(): return lax.ppermute(values, axis, [(i, i ^ flip) for i in range(size)])  95.5 us
    pallas_call x21, Pallas kernels, call(): pl.pallas_call(kernel, out_shape=[jax.ShapeDtypeStruct(s, d) for s, d in...  78.6 us
    ppermute x57, starting transfers between devices, exchange(): return lax.ppermute(values, axis, [(i, i ^ flip) for i in range(size)])  67.4 us
  transfers between devices with their start and end apart: 57, of which 32 were waited for; matrix products, arithmetic and copies ran while one was open for 2% of the time, Pallas kernels for 14%

profile of v4, /device:TPU:0, one launch (start us, length us, event | category | flops | bytes accessed | tf_op | source)
XLA Modules:
  0.0 252.0 jit_solution(12062866769499276685)
XLA Ops:
  2.5 5.1 %collective-permute-start.2 = (bf16[2,48,768]{2,1,0:T(8,128)(2,1)S(1)}, bf16[2,48,768]{2,1,0:T(8,128)(2,1)S(1)}, u32[]{:S(2)}, u32[]{:S(2)}) collective-permute-start(bf16[2,48,768]{2,1,0:T(8,128)(2,1)S(1)} %shard_map.364.refs_0_), channel_id=1, source_target_pairs={{0,24},{2,26},{4,28},{6,30},{8,16},{10,18},{12,20},{14,22},{16,8},... | collective-permute-start | bytes 442376 | tf_op jit(solution)/shard_map/ppermute | solution.py:463
  10.2 1.7 collective-permute-start.15
  16.3 3.8 %collective-permute-done.1.refs_2_ = bf16[2,48,768]{2,1,0:T(8,128)(2,1)S(1)} collective-permute-done((bf16[2,48,768]{2,1,0:T(8,128)(2,1)S(1)}, bf16[2,48,768]{2,1,0:T(8,128)(2,1)S(1)}, u32[]{:S(2)}, u32[]{:S(2)}) %collective-permute-start.1) | collective-permute-done | bytes 147488 | tf_op jit(solution)/shard_map/ppermute | solution.py:463
  20.1 2.8 %collective-permute-start.10 = (bf16[2,48,768]{2,1,0:T(8,128)(2,1)S(1)}, bf16[2,48,768]{2,1,0:T(8,128)(2,1)S(1)}, u32[]{:S(2)}, u32[]{:S(2)}) collective-permute-start(bf16[2,48,768]{2,1,0:T(8,128)(2,1)S(1)} %get-tuple-element.142), channel_id=1, source_target_pairs={{0,24},{2,26},{4,28},{6,30},{8,16},{10,18},{12,20},{14,22},{16,8},... | collective-permute-start | bytes 442376 | tf_op jit(solution)/shard_map/ppermute | solution.py:463
  22.9 1.7 collective-permute-start.8
  28.8 5.3 %collective-permute-done.9 = bf16[2,48,768]{2,1,0:T(8,128)(2,1)S(1)} collective-permute-done((bf16[2,48,768]{2,1,0:T(8,128)(2,1)S(1)}, bf16[2,48,768]{2,1,0:T(8,128)(2,1)S(1)}, u32[]{:S(2)}, u32[]{:S(2)}) %collective-permute-start.9) | collective-permute-done | bytes 147488 | tf_op jit(solution)/shard_map/ppermute | solution.py:463
  39.0 2.9 %collective-permute-start.17 = (bf16[2,2,48,768]{3,2,1,0:T(8,128)(2,1)S(1)}, bf16[2,2,48,768]{3,2,1,0:T(8,128)(2,1)S(1)}, u32[]{:S(2)}, u32[]{:S(2)}) collective-permute-start(bf16[2,2,48,768]{3,2,1,0:T(8,128)(2,1)S(1)} %pad_maximum_fusion.4), channel_id=1, source_target_pairs={{0,8},{2,10},{4,12},{6,14},{8,0},{10,2},{12,4},{14,6},{16,24},{18,... | collective-permute-start | bytes 884744 | tf_op jit(solution)/shard_map/ppermute | solution.py:463
  42.0 6.9 %collective-permute-done.6.refs_3_ = bf16[8,48,768]{2,1,0:T(8,128)(2,1)S(1)} collective-permute-done((bf16[8,48,768]{2,1,0:T(8,128)(2,1)S(1)}, bf16[8,48,768]{2,1,0:T(8,128)(2,1)S(1)}, u32[]{:S(2)}, u32[]{:S(2)}) %collective-permute-start.6) | collective-permute-done | bytes 589856 | tf_op jit(solution)/shard_map/ppermute | solution.py:463
  52.3 4.9 %collective-permute-done.13 = bf16[4,48,768]{2,1,0:T(8,128)(2,1)S(1)} collective-permute-done((bf16[4,48,768]{2,1,0:T(8,128)(2,1)S(1)}, bf16[4,48,768]{2,1,0:T(8,128)(2,1)S(1)}, u32[]{:S(2)}, u32[]{:S(2)}) %collective-permute-start.13) | collective-permute-done | bytes 294944 | tf_op jit(solution)/shard_map/ppermute | solution.py:463
  57.8 2.0 collective-permute-done.11
  60.0 2.9 %collective-permute-done.18 = bf16[2,2,48,768]{3,2,1,0:T(8,128)(2,1)S(1)} collective-permute-done((bf16[2,2,48,768]{3,2,1,0:T(8,128)(2,1)S(1)}, bf16[2,2,48,768]{3,2,1,0:T(8,128)(2,1)S(1)}, u32[]{:S(2)}, u32[]{:S(2)}) %collective-permute-start.18) | collective-permute-done | bytes 294944 | tf_op jit(solution)/shard_map/ppermute | solution.py:463
  63.6 7.3 %shard_map.367 = (bf16[544,768]{1,0:T(8,128)(2,1)S(1)}, bf16[544,768]{1,0:T(8,128)(2,1)S(1)}, bf16[544,1152]{1,0:T(8,128)(2,1)S(1)}, f32[544,128]{1,0:T(8,128)S(1)}, bf16[544,384]{1,0:T(8,128)(2,1)S(1)}) custom-call(bf16[512,768]{1,0:T(8,128)(2,1)S(1)} %get-tuple-element.254.token_ref, f32[16,768]{1,0:T(8,128)S(1)} %broadcast_select_fusion.mem_ref.keep_ref, ...), custom_call_target="tpu_custom_call" | custom-call | tf_op jit(solution)/shard_map/pallas_call | solution.py:66
  73.3 13.6 %collective-permute-done.20.refs_1_ = bf16[8,48,768]{2,1,0:T(8,128)(2,1)S(1)} collective-permute-done((bf16[8,48,768]{2,1,0:T(8,128)(2,1)S(1)}, bf16[8,48,768]{2,1,0:T(8,128)(2,1)S(1)}, u32[]{:S(2)}, u32[]{:S(2)}) %collective-permute-start.20) | collective-permute-done | bytes 589856 | tf_op jit(solution)/shard_map/ppermute | solution.py:463
  87.4 5.3 %shard_map.371 = (bf16[544,768]{1,0:T(8,128)(2,1)S(1)}, f32[544,768]{1,0:T(8,128)S(1)}, bf16[544,768]{1,0:T(8,128)(2,1)S(1)}, bf16[544,1536]{1,0:T(8,128)(2,1)S(1)}, bf16[544,1536]{1,0:T(8,128)(2,1)S(1)}) custom-call(bf16[512,768]{1,0:T(8,128)(2,1)S(1)} %get-tuple-element.254.token_ref, f32[16,768]{1,0:T(8,128)S(1)} %broadcast_select_fusion.mem_ref.keep_ref, ...), custom_call_target="tpu_custom_call" | custom-call | tf_op jit(solution)/shard_map/pallas_call | solution.py:66
  93.3 1.7 collective-permute-done.22.other_ref
  95.0 7.9 %shard_map.372 = (bf16[512,768]{1,0:T(8,128)(2,1)S(1)}, f32[16,768]{1,0:T(8,128)S(1)}, f32[544,768]{1,0:T(8,128)S(1)}, bf16[544,768]{1,0:T(8,128)(2,1)S(1)}, bf1...) custom-call(f32[544,768]{1,0:T(8,128)S(1)} %get-tuple-element.150.fi, ...), custom_call_target="tpu_custom_call" | custom-call | tf_op jit(solution)/shard_map/pallas_call | solution.py:66
  103.2 2.2 collective-permute-done.23.other_ref
  105.4 5.4 %shard_map.373 = (bf16[544,768]{1,0:T(8,128)(2,1)S(1)}, f32[544,768]{1,0:T(8,128)S(1)}, bf16[544,768]{1,0:T(8,128)(2,1)S(1)}, bf16[544,1536]{1,0:T(8,128)(2,1)S(1)}, bf16[544,1536]{1,0:T(8,128)(2,1)S(1)}) custom-call(bf16[512,768]{1,0:T(8,128)(2,1)S(1)} %get-tuple-element.253.token_ref, f32[16,768]{1,0:T(8,128)S(1)} %get-tuple-element.153.mem_ref, ...), custom_call_target="tpu_custom_call" | custom-call | tf_op jit(solution)/shard_map/pallas_call | solution.py:66
  111.2 2.1 collective-permute-done.24.refs_3_
  113.3 5.7 %shard_map.374 = (bf16[2,512,768]{2,1,0:T(8,128)(2,1)}, bf16[544,768]{1,0:T(8,128)(2,1)S(1)}, f32[544,768]{1,0:T(8,128)S(1)}, bf16[544,768]{1,0:T(8,128)(2,1)S(1...) custom-call(bf16[512,768]{1,0:T(8,128)(2,1)S(1)} %get-tuple-element.152.refs_0_, ...), custom_call_target="tpu_custom_call" | custom-call | tf_op jit(solution)/shard_map/pallas_call | solution.py:66
  119.2 2.4 shard_map.375.refs_2_
  121.6 10.1 %shard_map.376 = (bf16[544,768]{1,0:T(8,128)(2,1)S(1)}, f32[544,768]{1,0:T(8,128)S(1)}, bf16[544,768]{1,0:T(8,128)(2,1)S(1)}, bf16[544,1152]{1,0:T(8,128)(2,1)S(...) custom-call(f32[544,768]{1,0:T(8,128)S(1)} %get-tuple-element.162.dsecond_ref, ...), custom_call_target="tpu_custom_call" | custom-call | tf_op jit(solution)/shard_map/pallas_call | solution.py:66
  132.2 2.0 collective-permute-done.26.other_ref
  134.2 5.4 %shard_map.377 = (bf16[512,768]{1,0:T(8,128)(2,1)S(1)}, f32[16,768]{1,0:T(8,128)S(1)}, bf16[544,768]{1,0:T(8,128)(2,1)S(1)}, f32[544,768]{1,0:T(8,128)S(1)}, bf1...) custom-call(f32[544,768]{1,0:T(8,128)S(1)} %get-tuple-element.166.dfirs, ...), custom_call_target="tpu_custom_call" | custom-call | tf_op jit(solution)/shard_map/pallas_call | solution.py:66
  140.0 3.4 %shard_map.378 = (bf16[8,48,768]{2,1,0:T(8,128)(2,1)S(1)}, bf16[8,48,768]{2,1,0:T(8,128)(2,1)S(1)}, bf16[8,48,768]{2,1,0:T(8,128)(2,1)S(1)}, bf16[8,48,768]{2,1,0:T(8,128)(2,1)S(1)}) custom-call(s32[1]{0:T(128)} %bitcast.1.me_ref, bf16[544,768]{1,0:T(8,128)(2,1)S(1)} %get-tuple-element.171.refs_0_, bf16[544,1536]{1,0:T(8,128)(2,1)S(1)} %get-tuple-element.172.refs_1_, ...), custom_call_target="tpu_custom_call" | custom-call | tf_op jit(solution)/shard_map/pallas_call | solution.py:66
  143.4 1.6 collective-permute-start.32
  145.5 4.5 %shard_map.379 = (bf16[8,48,768]{2,1,0:T(8,128)(2,1)S(1)}, bf16[8,48,768]{2,1,0:T(8,128)(2,1)S(1)}, bf16[8,48,768]{2,1,0:T(8,128)(2,1)S(1)}, bf16[8,48,768]{2,1,0:T(8,128)(2,1)S(1)}) custom-call(s32[1]{0:T(128)} %bitcast.1.me_ref, bf16[544,768]{1,0:T(8,128)(2,1)S(1)} %get-tuple-element.174.refs_0_, bf16[544,768]{1,0:T(8,128)(2,1)S(1)} %get-tuple-element.175.refs_1_, ...), custom_call_target="tpu_custom_call" | custom-call | tf_op jit(solution)/shard_map/pallas_call | solution.py:66
  152.1 10.2 %shard_map.380 = (bf16[544,768]{1,0:T(8,128)(2,1)S(1)}, f32[544,768]{1,0:T(8,128)S(1)}, bf16[544,768]{1,0:T(8,128)(2,1)S(1)}, bf16[544,1152]{1,0:T(8,128)(2,1)S(...) custom-call(f32[544,768]{1,0:T(8,128)S(1)} %get-tuple-element.179.dsecond_ref, ...), custom_call_target="tpu_custom_call" | custom-call | tf_op jit(solution)/shard_map/pallas_call | solution.py:66
  162.6 10.1 %collective-permute-done.31 = bf16[8,48,768]{2,1,0:T(8,128)(2,1)S(1)} collective-permute-done((bf16[8,48,768]{2,1,0:T(8,128)(2,1)S(1)}, bf16[8,48,768]{2,1,0:T(8,128)(2,1)S(1)}, u32[]{:S(2)}, u32[]{:S(2)}) %collective-permute-start.31) | collective-permute-done | bytes 589856 | tf_op jit(solution)/shard_map/ppermute | solution.py:463
  177.3 5.6 %shard_map.382 = (bf16[8,48,768]{2,1,0:T(8,128)(2,1)S(1)}, bf16[8,48,768]{2,1,0:T(8,128)(2,1)S(1)}, bf16[8,48,768]{2,1,0:T(8,128)(2,1)S(1)}, bf16[8,48,768]{2,1,0:T(8,128)(2,1)S(1)}) custom-call(s32[1]{0:T(128)} %bitcast.1.me_ref, bf16[544,768]{1,0:T(8,128)(2,1)S(1)} %get-tuple-element.191.refs_0_, bf16[544,768]{1,0:T(8,128)(2,1)S(1)} %get-tuple-element.192.refs_1_, ...), custom_call_target="tpu_custom_call" | custom-call | tf_op jit(solution)/shard_map/pallas_call | solution.py:66
  183.6 1.7 collective-permute-start.37
  185.3 7.1 %collective-permute-start.35 = (bf16[48,1536]{1,0:T(8,128)(2,1)S(1)}, bf16[48,1536]{1,0:T(8,128)(2,1)S(1)}, u32[]{:S(2)}, u32[]{:S(2)}) collective-permute-start(bf16[48,1536]{1,0:T(8,128)(2,1)S(1)} %get-tuple-element.265), channel_id=1, source_target_pairs={{0,8},{2,10},{4,12},{6,14},{8,0},{10,2},{12,4},{14,6},{16,24},{18,... | collective-permute-start | bytes 442376 | tf_op jit(solution)/shard_map/ppermute | solution.py:463
  194.5 1.6 collective-permute-start.42
  196.1 3.5 %collective-permute-done.35.refs_1_ = bf16[48,1536]{1,0:T(8,128)(2,1)S(1)} collective-permute-done((bf16[48,1536]{1,0:T(8,128)(2,1)S(1)}, bf16[48,1536]{1,0:T(8,128)(2,1)S(1)}, u32[]{:S(2)}, u32[]{:S(2)}) %collective-permute-start.35) | collective-permute-done | bytes 147488 | tf_op jit(solution)/shard_map/ppermute | solution.py:463
  201.0 5.8 %collective-permute-done.36.refs_2_ = bf16[48,1536]{1,0:T(8,128)(2,1)S(1)} collective-permute-done((bf16[48,1536]{1,0:T(8,128)(2,1)S(1)}, bf16[48,1536]{1,0:T(8,128)(2,1)S(1)}, u32[]{:S(2)}, u32[]{:S(2)}) %collective-permute-start.36) | collective-permute-done | bytes 147488 | tf_op jit(solution)/shard_map/ppermute | solution.py:463
  207.3 6.5 %collective-permute-done.41.refs_6_ = bf16[48,1536]{1,0:T(8,128)(2,1)S(1)} collective-permute-done((bf16[48,1536]{1,0:T(8,128)(2,1)S(1)}, bf16[48,1536]{1,0:T(8,128)(2,1)S(1)}, u32[]{:S(2)}, u32[]{:S(2)}) %collective-permute-start.41) | collective-permute-done | bytes 147488 | tf_op jit(solution)/shard_map/ppermute | solution.py:463
  214.5 2.1 collective-permute-start.46
  216.5 4.3 %collective-permute-done.44 = bf16[4,48,768]{2,1,0:T(8,128)(2,1)S(1)} collective-permute-done((bf16[4,48,768]{2,1,0:T(8,128)(2,1)S(1)}, bf16[4,48,768]{2,1,0:T(8,128)(2,1)S(1)}, u32[]{:S(2)}, u32[]{:S(2)}) %collective-permute-start.44) | collective-permute-done | bytes 294944 | tf_op jit(solution)/shard_map/ppermute | solution.py:463
  221.4 2.5 %collective-permute-start.49 = (bf16[48,1536]{1,0:T(8,128)(2,1)S(1)}, bf16[48,1536]{1,0:T(8,128)(2,1)S(1)}, u32[]{:S(2)}, u32[]{:S(2)}) collective-permute-start(bf16[48,1536]{1,0:T(8,128)(2,1)S(1)} %get-tuple-element.255), channel_id=1, source_target_pairs={{0,24},{2,26},{4,28},{6,30},{8,16},{10,18},{12,20},{14,22},{16,8},... | collective-permute-start | bytes 442376 | tf_op jit(solution)/shard_map/ppermute | solution.py:463
  223.9 1.9 collective-permute-start.48
  225.8 1.9 shard_map.381
  228.5 2.1 collective-permute-done.47.refs_9_
  230.6 2.2 collective-permute-done.48.refs_10_
  237.0 1.8 collective-permute-done.52
  240.1 2.1 collective-permute-start.55
  242.2 2.3 collective-permute-start.53
  244.5 1.8 collective-permute-done.55
  249.4 2.3 shard_map.384
  (183 shorter events, 49.5 us)
Async XLA Ops:
  2.5 13.8 %collective-permute-start.2 = (bf16[2,48,768]{2,1,0:T(8,128)(2,1)S(1)}, bf16[2,48,768]{2,1,0:T(8,128)(2,1)S(1)}, u32[]{:S(2)}, u32[]{:S(2)}) collective-permute-start(bf16[2,48,768]{2,1,0:T(8,128)(2,1)S(1)} %shard_map.364.refs_0_), channel_id=1, source_target_pairs={{0,24},{2,26},{4,28},{6,30},{8,16},{10,18},{12,20},{14,22},{16,8},... | collective-permute-start | bytes 442376 | tf_op jit(solution)/shard_map/ppermute | solution.py:463
  7.6 12.5 %collective-permute-start.1 = (bf16[2,48,768]{2,1,0:T(8,128)(2,1)S(1)}, bf16[2,48,768]{2,1,0:T(8,128)(2,1)S(1)}, u32[]{:S(2)}, u32[]{:S(2)}) collective-permute-start(bf16[2,48,768]{2,1,0:T(8,128)(2,1)S(1)} %shard_map.364.refs_0_), channel_id=1, source_target_pairs={{0,16},{2,18},{4,20},{6,22},{8,24},{10,26},{12,28},{14,30},{16,0},... | collective-permute-start | bytes 442376 | tf_op jit(solution)/shard_map/ppermute | solution.py:463
  7.6 12.5 %collective-permute-start = (bf16[2,48,768]{2,1,0:T(8,128)(2,1)S(1)}, bf16[2,48,768]{2,1,0:T(8,128)(2,1)S(1)}, u32[]{:S(2)}, u32[]{:S(2)}) collective-permute-start(bf16[2,48,768]{2,1,0:T(8,128)(2,1)S(1)} %shard_map.364.refs_0_), channel_id=1, source_target_pairs={{0,8},{2,10},{4,12},{6,14},{8,0},{10,2},{12,4},{14,6},{16,24},{18,... | collective-permute-start | bytes 442376 | tf_op jit(solution)/shard_map/ppermute | solution.py:463
  10.2 4.8 %collective-permute-start.15 = (bf16[48,768]{1,0:T(8,128)(2,1)S(1)}, bf16[48,768]{1,0:T(8,128)(2,1)S(1)}, u32[]{:S(2)}, u32[]{:S(2)}) collective-permute-start(bf16[48,768]{1,0:T(8,128)(2,1)S(1)} %get-tuple-element.145), channel_id=1, source_target_pairs={{0,2},{2,0},{4,6},{6,4},{8,10},{10,8},{12,14},{14,12},{16,18},{18,... | collective-permute-start | bytes 221192 | tf_op jit(solution)/shard_map/ppermute | solution.py:463
  20.1 8.6 %collective-permute-start.10 = (bf16[2,48,768]{2,1,0:T(8,128)(2,1)S(1)}, bf16[2,48,768]{2,1,0:T(8,128)(2,1)S(1)}, u32[]{:S(2)}, u32[]{:S(2)}) collective-permute-start(bf16[2,48,768]{2,1,0:T(8,128)(2,1)S(1)} %get-tuple-element.142), channel_id=1, source_target_pairs={{0,24},{2,26},{4,28},{6,30},{8,16},{10,18},{12,20},{14,22},{16,8},... | collective-permute-start | bytes 442376 | tf_op jit(solution)/shard_map/ppermute | solution.py:463
  22.9 11.2 %collective-permute-start.9 = (bf16[2,48,768]{2,1,0:T(8,128)(2,1)S(1)}, bf16[2,48,768]{2,1,0:T(8,128)(2,1)S(1)}, u32[]{:S(2)}, u32[]{:S(2)}) collective-permute-start(bf16[2,48,768]{2,1,0:T(8,128)(2,1)S(1)} %get-tuple-element.142), channel_id=1, source_target_pairs={{0,16},{2,18},{4,20},{6,22},{8,24},{10,26},{12,28},{14,30},{16,0},... | collective-permute-start | bytes 442376 | tf_op jit(solution)/shard_map/ppermute | solution.py:463
  22.9 14.5 %collective-permute-start.8 = (bf16[2,48,768]{2,1,0:T(8,128)(2,1)S(1)}, bf16[2,48,768]{2,1,0:T(8,128)(2,1)S(1)}, u32[]{:S(2)}, u32[]{:S(2)}) collective-permute-start(bf16[2,48,768]{2,1,0:T(8,128)(2,1)S(1)} %get-tuple-element.142), channel_id=1, source_target_pairs={{0,8},{2,10},{4,12},{6,14},{8,0},{10,2},{12,4},{14,6},{16,24},{18,... | collective-permute-start | bytes 442376 | tf_op jit(solution)/shard_map/ppermute | solution.py:463
  24.6 11.1 %collective-permute-start.3 = (bf16[4,48,768]{2,1,0:T(8,128)(2,1)S(1)}, bf16[4,48,768]{2,1,0:T(8,128)(2,1)S(1)}, u32[]{:S(2)}, u32[]{:S(2)}) collective-permute-start(bf16[4,48,768]{2,1,0:T(8,128)(2,1)S(1)} %get-tuple-element.136), channel_id=1, source_target_pairs={{0,4},{2,6},{4,0},{6,2},{8,12},{10,14},{12,8},{14,10},{16,20},{18,... | collective-permute-start | bytes 884744 | tf_op jit(solution)/shard_map/ppermute | solution.py:463
  26.2 7.9 %collective-permute-start.5 = (bf16[4,48,768]{2,1,0:T(8,128)(2,1)S(1)}, bf16[4,48,768]{2,1,0:T(8,128)(2,1)S(1)}, u32[]{:S(2)}, u32[]{:S(2)}) collective-permute-start(bf16[4,48,768]{2,1,0:T(8,128)(2,1)S(1)} %get-tuple-element.137), channel_id=1, source_target_pairs={{0,2},{2,0},{4,6},{6,4},{8,10},{10,8},{12,14},{14,12},{16,18},{18,... | collective-permute-start | bytes 884744 | tf_op jit(solution)/shard_map/ppermute | solution.py:463
  34.2 14.7 %collective-permute-start.6 = (bf16[8,48,768]{2,1,0:T(8,128)(2,1)S(1)}, bf16[8,48,768]{2,1,0:T(8,128)(2,1)S(1)}, u32[]{:S(2)}, u32[]{:S(2)}) collective-permute-start(bf16[8,48,768]{2,1,0:T(8,128)(2,1)S(1)} %constant_dynamic-update-slice_fusion.2.refs_2_), channel_id=1, source_target_pairs={{0,4},{2,6},{4,0},{6,2},{8,12},{10,14},{12,8},{14,10},{16,20},{18,... | collective-permute-start | bytes 1769480 | tf_op jit(solution)/shard_map/ppermute | solution.py:463
  35.8 14.4 %collective-permute-start.4 = (bf16[8,48,768]{2,1,0:T(8,128)(2,1)S(1)}, bf16[8,48,768]{2,1,0:T(8,128)(2,1)S(1)}, u32[]{:S(2)}, u32[]{:S(2)}) collective-permute-start(bf16[8,48,768]{2,1,0:T(8,128)(2,1)S(1)} %constant_dynamic-update-slice_fusion.refs_0_), channel_id=1, source_target_pairs={{0,2},{2,0},{4,6},{6,4},{8,10},{10,8},{12,14},{14,12},{16,18},{18,... | collective-permute-start | bytes 1769480 | tf_op jit(solution)/shard_map/ppermute | solution.py:463
  37.4 14.3 %collective-permute-start.19 = (bf16[2,2,48,768]{3,2,1,0:T(8,128)(2,1)S(1)}, bf16[2,2,48,768]{3,2,1,0:T(8,128)(2,1)S(1)}, u32[]{:S(2)}, u32[]{:S(2)}) collective-permute-start(bf16[2,2,48,768]{3,2,1,0:T(8,128)(2,1)S(1)} %pad_maximum_fusion.4), channel_id=1, source_target_pairs={{0,24},{2,26},{4,28},{6,30},{8,16},{10,18},{12,20},{14,22},{16,8},... | collective-permute-start | bytes 884744 | tf_op jit(solution)/shard_map/ppermute | solution.py:463
  39.0 23.9 %collective-permute-start.18 = (bf16[2,2,48,768]{3,2,1,0:T(8,128)(2,1)S(1)}, bf16[2,2,48,768]{3,2,1,0:T(8,128)(2,1)S(1)}, u32[]{:S(2)}, u32[]{:S(2)}) collective-permute-start(bf16[2,2,48,768]{3,2,1,0:T(8,128)(2,1)S(1)} %pad_maximum_fusion.4), channel_id=1, source_target_pairs={{0,16},{2,18},{4,20},{6,22},{8,24},{10,26},{12,28},{14,30},{16,0},... | collective-permute-start | bytes 884744 | tf_op jit(solution)/shard_map/ppermute | solution.py:463
  39.0 31.9 %collective-permute-start.17 = (bf16[2,2,48,768]{3,2,1,0:T(8,128)(2,1)S(1)}, bf16[2,2,48,768]{3,2,1,0:T(8,128)(2,1)S(1)}, u32[]{:S(2)}, u32[]{:S(2)}) collective-permute-start(bf16[2,2,48,768]{3,2,1,0:T(8,128)(2,1)S(1)} %pad_maximum_fusion.4), channel_id=1, source_target_pairs={{0,8},{2,10},{4,12},{6,14},{8,0},{10,2},{12,4},{14,6},{16,24},{18,... | collective-permute-start | bytes 884744 | tf_op jit(solution)/shard_map/ppermute | solution.py:463
  50.2 7.1 %collective-permute-start.13 = (bf16[4,48,768]{2,1,0:T(8,128)(2,1)S(1)}, bf16[4,48,768]{2,1,0:T(8,128)(2,1)S(1)}, u32[]{:S(2)}, u32[]{:S(2)}) collective-permute-start(bf16[4,48,768]{2,1,0:T(8,128)(2,1)S(1)} %get-tuple-element.144), channel_id=1, source_target_pairs={{0,2},{2,0},{4,6},{6,4},{8,10},{10,8},{12,14},{14,12},{16,18},{18,... | collective-permute-start | bytes 884744 | tf_op jit(solution)/shard_map/ppermute | solution.py:463
  51.7 8.2 %collective-permute-start.11 = (bf16[4,48,768]{2,1,0:T(8,128)(2,1)S(1)}, bf16[4,48,768]{2,1,0:T(8,128)(2,1)S(1)}, u32[]{:S(2)}, u32[]{:S(2)}) collective-permute-start(bf16[4,48,768]{2,1,0:T(8,128)(2,1)S(1)} %get-tuple-element.143), channel_id=1, source_target_pairs={{0,4},{2,6},{4,0},{6,2},{8,12},{10,14},{12,8},{14,10},{16,20},{18,... | collective-permute-start | bytes 884744 | tf_op jit(solution)/shard_map/ppermute | solution.py:463
  57.3 13.9 %collective-permute-start.14 = (bf16[8,48,768]{2,1,0:T(8,128)(2,1)S(1)}, bf16[8,48,768]{2,1,0:T(8,128)(2,1)S(1)}, u32[]{:S(2)}, u32[]{:S(2)}) collective-permute-start(bf16[8,48,768]{2,1,0:T(8,128)(2,1)S(1)} %constant_dynamic-update-slice_fusion.6.refs_2_), channel_id=1, source_target_pairs={{0,4},{2,6},{4,0},{6,2},{8,12},{10,14},{12,8},{14,10},{16,20},{18,... | collective-permute-start | bytes 1769480 | tf_op jit(solution)/shard_map/ppermute | solution.py:463
  59.9 11.3 %collective-permute-start.12 = (bf16[8,48,768]{2,1,0:T(8,128)(2,1)S(1)}, bf16[8,48,768]{2,1,0:T(8,128)(2,1)S(1)}, u32[]{:S(2)}, u32[]{:S(2)}) collective-permute-start(bf16[8,48,768]{2,1,0:T(8,128)(2,1)S(1)} %constant_dynamic-update-slice_fusion.4.refs_0_), channel_id=1, source_target_pairs={{0,2},{2,0},{4,6},{6,4},{8,10},{10,8},{12,14},{14,12},{16,18},{18,... | collective-permute-start | bytes 1769480 | tf_op jit(solution)/shard_map/ppermute | solution.py:463
  70.9 16.5 %collective-permute-start.7 = (bf16[544,768]{1,0:T(8,128)(2,1)S(1)}, bf16[544,768]{1,0:T(8,128)(2,1)S(1)}, u32[]{:S(2)}, u32[]{:S(2)}) collective-permute-start(bf16[544,768]{1,0:T(8,128)(2,1)S(1)} %get-tuple-element.140.own_ref), channel_id=1, source_target_pairs={{0,1},{1,0},{2,3},{3,2},{4,5},{5,4},{6,7},{7,6},{8,9},{9,8},{10,11... | collective-permute-start | bytes 2506760 | tf_op jit(solution)/shard_map/ppermute | solution.py:463
  71.2 15.8 %collective-permute-start.20 = (bf16[8,48,768]{2,1,0:T(8,128)(2,1)S(1)}, bf16[8,48,768]{2,1,0:T(8,128)(2,1)S(1)}, u32[]{:S(2)}, u32[]{:S(2)}) collective-permute-start(bf16[8,48,768]{2,1,0:T(8,128)(2,1)S(1)} %get-tuple-element.148.refs_0_), channel_id=1, source_target_pairs={{0,4},{2,6},{4,0},{6,2},{8,12},{10,14},{12,8},{14,10},{16,20},{18,... | collective-permute-start | bytes 1769480 | tf_op jit(solution)/shard_map/ppermute | solution.py:463
  71.7 15.4 %collective-permute-start.21 = (bf16[8,48,768]{2,1,0:T(8,128)(2,1)S(1)}, bf16[8,48,768]{2,1,0:T(8,128)(2,1)S(1)}, u32[]{:S(2)}, u32[]{:S(2)}) collective-permute-start(bf16[8,48,768]{2,1,0:T(8,128)(2,1)S(1)} %get-tuple-element.149.refs_2_), channel_id=1, source_target_pairs={{0,2},{2,0},{4,6},{6,4},{8,10},{10,8},{12,14},{14,12},{16,18},{18,... | collective-permute-start | bytes 1769480 | tf_op jit(solution)/shard_map/ppermute | solution.py:463
  139.6 12.5 %collective-permute-start.27 = (bf16[544,768]{1,0:T(8,128)(2,1)S(1)}, bf16[544,768]{1,0:T(8,128)(2,1)S(1)}, u32[]{:S(2)}, u32[]{:S(2)}) collective-permute-start(bf16[544,768]{1,0:T(8,128)(2,1)S(1)} %get-tuple-element.180.own_ref), channel_id=1, source_target_pairs={{0,1},{1,0},{2,3},{3,2},{4,5},{5,4},{6,7},{7,6},{8,9},{9,8},{10,11... | collective-permute-start | bytes 2506760 | tf_op jit(solution)/shard_map/ppermute | solution.py:463
  143.4 18.9 %collective-permute-start.32 = (bf16[8,48,768]{2,1,0:T(8,128)(2,1)S(1)}, bf16[8,48,768]{2,1,0:T(8,128)(2,1)S(1)}, u32[]{:S(2)}, u32[]{:S(2)}) collective-permute-start(bf16[8,48,768]{2,1,0:T(8,128)(2,1)S(1)} %get-tuple-element.195), channel_id=1, source_target_pairs={{0,4},{2,6},{4,0},{6,2},{8,12},{10,14},{12,8},{14,10},{16,20},{18,... | collective-permute-start | bytes 1769480 | tf_op jit(solution)/shard_map/ppermute | solution.py:463
  145.0 17.5 %collective-permute-start.29 = (bf16[8,48,768]{2,1,0:T(8,128)(2,1)S(1)}, bf16[8,48,768]{2,1,0:T(8,128)(2,1)S(1)}, u32[]{:S(2)}, u32[]{:S(2)}) collective-permute-start(bf16[8,48,768]{2,1,0:T(8,128)(2,1)S(1)} %get-tuple-element.188), channel_id=1, source_target_pairs={{0,2},{2,0},{4,6},{6,4},{8,10},{10,8},{12,14},{14,12},{16,18},{18,... | collective-permute-start | bytes 1769480 | tf_op jit(solution)/shard_map/ppermute | solution.py:463
  150.0 22.7 %collective-permute-start.31 = (bf16[8,48,768]{2,1,0:T(8,128)(2,1)S(1)}, bf16[8,48,768]{2,1,0:T(8,128)(2,1)S(1)}, u32[]{:S(2)}, u32[]{:S(2)}) collective-permute-start(bf16[8,48,768]{2,1,0:T(8,128)(2,1)S(1)} %get-tuple-element.193), channel_id=1, source_target_pairs={{0,2},{2,0},{4,6},{6,4},{8,10},{10,8},{12,14},{14,12},{16,18},{18,... | collective-permute-start | bytes 1769480 | tf_op jit(solution)/shard_map/ppermute | solution.py:463
  151.6 21.9 %collective-permute-start.33 = (bf16[8,48,768]{2,1,0:T(8,128)(2,1)S(1)}, bf16[8,48,768]{2,1,0:T(8,128)(2,1)S(1)}, u32[]{:S(2)}, u32[]{:S(2)}) collective-permute-start(bf16[8,48,768]{2,1,0:T(8,128)(2,1)S(1)} %get-tuple-element.199), channel_id=1, source_target_pairs={{0,4},{2,6},{4,0},{6,2},{8,12},{10,14},{12,8},{14,10},{16,20},{18,... | collective-permute-start | bytes 1769480 | tf_op jit(solution)/shard_map/ppermute | solution.py:463
  172.7 10.2 %collective-permute-start.34 = (bf16[4,48,768]{2,1,0:T(8,128)(2,1)S(1)}, bf16[4,48,768]{2,1,0:T(8,128)(2,1)S(1)}, u32[]{:S(2)}, u32[]{:S(2)}) collective-permute-start(bf16[4,48,768]{2,1,0:T(8,128)(2,1)S(1)} %slice.193), channel_id=1, source_target_pairs={{0,2},{2,0},{4,6},{6,4},{8,10},{10,8},{12,14},{14,12},{16,18},{18,... | collective-permute-start | bytes 884744 | tf_op jit(solution)/shard_map/ppermute | solution.py:463
  173.4 10.0 %collective-permute-start.30 = (bf16[4,48,768]{2,1,0:T(8,128)(2,1)S(1)}, bf16[4,48,768]{2,1,0:T(8,128)(2,1)S(1)}, u32[]{:S(2)}, u32[]{:S(2)}) collective-permute-start(bf16[4,48,768]{2,1,0:T(8,128)(2,1)S(1)} %slice.191), channel_id=1, source_target_pairs={{0,4},{2,6},{4,0},{6,2},{8,12},{10,14},{12,8},{14,10},{16,20},{18,... | collective-permute-start | bytes 884744 | tf_op jit(solution)/shard_map/ppermute | solution.py:463
  174.2 18.3 %collective-permute-start.39 = (bf16[4,48,768]{2,1,0:T(8,128)(2,1)S(1)}, bf16[4,48,768]{2,1,0:T(8,128)(2,1)S(1)}, u32[]{:S(2)}, u32[]{:S(2)}) collective-permute-start(bf16[4,48,768]{2,1,0:T(8,128)(2,1)S(1)} %slice.203), channel_id=1, source_target_pairs={{0,2},{2,0},{4,6},{6,4},{8,10},{10,8},{12,14},{14,12},{16,18},{18,... | collective-permute-start | bytes 884744 | tf_op jit(solution)/shard_map/ppermute | solution.py:463
  175.7 16.8 %collective-permute-start.38 = (bf16[4,48,768]{2,1,0:T(8,128)(2,1)S(1)}, bf16[4,48,768]{2,1,0:T(8,128)(2,1)S(1)}, u32[]{:S(2)}, u32[]{:S(2)}) collective-permute-start(bf16[4,48,768]{2,1,0:T(8,128)(2,1)S(1)} %slice.201), channel_id=1, source_target_pairs={{0,4},{2,6},{4,0},{6,2},{8,12},{10,14},{12,8},{14,10},{16,20},{18,... | collective-permute-start | bytes 884744 | tf_op jit(solution)/shard_map/ppermute | solution.py:463
  183.6 10.9 %collective-permute-start.37 = (bf16[48,1536]{1,0:T(8,128)(2,1)S(1)}, bf16[48,1536]{1,0:T(8,128)(2,1)S(1)}, u32[]{:S(2)}, u32[]{:S(2)}) collective-permute-start(bf16[48,1536]{1,0:T(8,128)(2,1)S(1)} %get-tuple-element.263), channel_id=1, source_target_pairs={{0,24},{2,26},{4,28},{6,30},{8,16},{10,18},{12,20},{14,22},{16,8},... | collective-permute-start | bytes 442376 | tf_op jit(solution)/shard_map/ppermute | solution.py:463
  185.3 14.3 %collective-permute-start.35 = (bf16[48,1536]{1,0:T(8,128)(2,1)S(1)}, bf16[48,1536]{1,0:T(8,128)(2,1)S(1)}, u32[]{:S(2)}, u32[]{:S(2)}) collective-permute-start(bf16[48,1536]{1,0:T(8,128)(2,1)S(1)} %get-tuple-element.265), channel_id=1, source_target_pairs={{0,8},{2,10},{4,12},{6,14},{8,0},{10,2},{12,4},{14,6},{16,24},{18,... | collective-permute-start | bytes 442376 | tf_op jit(solution)/shard_map/ppermute | solution.py:463
  192.5 14.3 %collective-permute-start.36 = (bf16[48,1536]{1,0:T(8,128)(2,1)S(1)}, bf16[48,1536]{1,0:T(8,128)(2,1)S(1)}, u32[]{:S(2)}, u32[]{:S(2)}) collective-permute-start(bf16[48,1536]{1,0:T(8,128)(2,1)S(1)} %get-tuple-element.266), channel_id=1, source_target_pairs={{0,16},{2,18},{4,20},{6,22},{8,24},{10,26},{12,28},{14,30},{16,0},... | collective-permute-start | bytes 442376 | tf_op jit(solution)/shard_map/ppermute | solution.py:463
  192.5 21.3 %collective-permute-start.43 = (bf16[8,48,768]{2,1,0:T(8,128)(2,1)S(1)}, bf16[8,48,768]{2,1,0:T(8,128)(2,1)S(1)}, u32[]{:S(2)}, u32[]{:S(2)}) collective-permute-start(bf16[8,48,768]{2,1,0:T(8,128)(2,1)S(1)} %get-tuple-element.212), channel_id=1, source_target_pairs={{0,2},{2,0},{4,6},{6,4},{8,10},{10,8},{12,14},{14,12},{16,18},{18,... | collective-permute-start | bytes 1769480 | tf_op jit(solution)/shard_map/ppermute | solution.py:463
  193.1 21.2 %collective-permute-start.45 = (bf16[8,48,768]{2,1,0:T(8,128)(2,1)S(1)}, bf16[8,48,768]{2,1,0:T(8,128)(2,1)S(1)}, u32[]{:S(2)}, u32[]{:S(2)}) collective-permute-start(bf16[8,48,768]{2,1,0:T(8,128)(2,1)S(1)} %get-tuple-element.217), channel_id=1, source_target_pairs={{0,4},{2,6},{4,0},{6,2},{8,12},{10,14},{12,8},{14,10},{16,20},{18,... | collective-permute-start | bytes 1769480 | tf_op jit(solution)/shard_map/ppermute | solution.py:463
  194.5 12.3 %collective-permute-start.42 = (bf16[48,1536]{1,0:T(8,128)(2,1)S(1)}, bf16[48,1536]{1,0:T(8,128)(2,1)S(1)}, u32[]{:S(2)}, u32[]{:S(2)}) collective-permute-start(bf16[48,1536]{1,0:T(8,128)(2,1)S(1)} %get-tuple-element.259), channel_id=1, source_target_pairs={{0,24},{2,26},{4,28},{6,30},{8,16},{10,18},{12,20},{14,22},{16,8},... | collective-permute-start | bytes 442376 | tf_op jit(solution)/shard_map/ppermute | solution.py:463
  199.6 7.7 %collective-permute-start.40 = (bf16[48,1536]{1,0:T(8,128)(2,1)S(1)}, bf16[48,1536]{1,0:T(8,128)(2,1)S(1)}, u32[]{:S(2)}, u32[]{:S(2)}) collective-permute-start(bf16[48,1536]{1,0:T(8,128)(2,1)S(1)} %get-tuple-element.261), channel_id=1, source_target_pairs={{0,8},{2,10},{4,12},{6,14},{8,0},{10,2},{12,4},{14,6},{16,24},{18,... | collective-permute-start | bytes 442376 | tf_op jit(solution)/shard_map/ppermute | solution.py:463
  206.8 7.0 %collective-permute-start.41 = (bf16[48,1536]{1,0:T(8,128)(2,1)S(1)}, bf16[48,1536]{1,0:T(8,128)(2,1)S(1)}, u32[]{:S(2)}, u32[]{:S(2)}) collective-permute-start(bf16[48,1536]{1,0:T(8,128)(2,1)S(1)} %get-tuple-element.262), channel_id=1, source_target_pairs={{0,16},{2,18},{4,20},{6,22},{8,24},{10,26},{12,28},{14,30},{16,0},... | collective-permute-start | bytes 442376 | tf_op jit(solution)/shard_map/ppermute | solution.py:463
  214.0 6.8 %collective-permute-start.44 = (bf16[4,48,768]{2,1,0:T(8,128)(2,1)S(1)}, bf16[4,48,768]{2,1,0:T(8,128)(2,1)S(1)}, u32[]{:S(2)}, u32[]{:S(2)}) collective-permute-start(bf16[4,48,768]{2,1,0:T(8,128)(2,1)S(1)} %slice.211), channel_id=1, source_target_pairs={{0,4},{2,6},{4,0},{6,2},{8,12},{10,14},{12,8},{14,10},{16,20},{18,... | collective-permute-start | bytes 884744 | tf_op jit(solution)/shard_map/ppermute | solution.py:463
  214.5 6.8 %collective-permute-start.46 = (bf16[4,48,768]{2,1,0:T(8,128)(2,1)S(1)}, bf16[4,48,768]{2,1,0:T(8,128)(2,1)S(1)}, u32[]{:S(2)}, u32[]{:S(2)}) collective-permute-start(bf16[4,48,768]{2,1,0:T(8,128)(2,1)S(1)} %slice.213), channel_id=1, source_target_pairs={{0,2},{2,0},{4,6},{6,4},{8,10},{10,8},{12,14},{14,12},{16,18},{18,... | collective-permute-start | bytes 884744 | tf_op jit(solution)/shard_map/ppermute | solution.py:463
  216.5 9.3 %collective-permute-start.28 = (bf16[544,768]{1,0:T(8,128)(2,1)S(1)}, bf16[544,768]{1,0:T(8,128)(2,1)S(1)}, u32[]{:S(2)}, u32[]{:S(2)}) collective-permute-start(bf16[544,768]{1,0:T(8,128)(2,1)S(1)} %get-tuple-element.184.own_ref), channel_id=1, source_target_pairs={{0,1},{1,0},{2,3},{3,2},{4,5},{5,4},{6,7},{7,6},{8,9},{9,8},{10,11... | collective-permute-start | bytes 2506760 | tf_op jit(solution)/shard_map/ppermute | solution.py:463
  221.4 7.1 %collective-permute-start.49 = (bf16[48,1536]{1,0:T(8,128)(2,1)S(1)}, bf16[48,1536]{1,0:T(8,128)(2,1)S(1)}, u32[]{:S(2)}, u32[]{:S(2)}) collective-permute-start(bf16[48,1536]{1,0:T(8,128)(2,1)S(1)} %get-tuple-element.255), channel_id=1, source_target_pairs={{0,24},{2,26},{4,28},{6,30},{8,16},{10,18},{12,20},{14,22},{16,8},... | collective-permute-start | bytes 442376 | tf_op jit(solution)/shard_map/ppermute | solution.py:463
  223.9 6.7 %collective-permute-start.47 = (bf16[48,1536]{1,0:T(8,128)(2,1)S(1)}, bf16[48,1536]{1,0:T(8,128)(2,1)S(1)}, u32[]{:S(2)}, u32[]{:S(2)}) collective-permute-start(bf16[48,1536]{1,0:T(8,128)(2,1)S(1)} %get-tuple-element.257), channel_id=1, source_target_pairs={{0,8},{2,10},{4,12},{6,14},{8,0},{10,2},{12,4},{14,6},{16,24},{18,... | collective-permute-start | bytes 442376 | tf_op jit(solution)/shard_map/ppermute | solution.py:463
  223.9 8.9 %collective-permute-start.48 = (bf16[48,1536]{1,0:T(8,128)(2,1)S(1)}, bf16[48,1536]{1,0:T(8,128)(2,1)S(1)}, u32[]{:S(2)}, u32[]{:S(2)}) collective-permute-start(bf16[48,1536]{1,0:T(8,128)(2,1)S(1)} %get-tuple-element.258), channel_id=1, source_target_pairs={{0,16},{2,18},{4,20},{6,22},{8,24},{10,26},{12,28},{14,30},{16,0},... | collective-permute-start | bytes 442376 | tf_op jit(solution)/shard_map/ppermute | solution.py:463
  233.4 5.3 %collective-permute-start.52 = (f32[24,768]{1,0:T(8,128)S(1)}, f32[24,768]{1,0:T(8,128)S(1)}, u32[]{:S(2)}, u32[]{:S(2)}) collective-permute-start(f32[24,768]{1,0:T(8,128)S(1)} %get-tuple-element.228), channel_id=1, source_target_pairs={{0,6},{2,4},{4,2},{6,0},{8,14},{10,12},{12,10},{14,8},{16,22},{18,... | collective-permute-start | bytes 221192 | tf_op jit(solution)/shard_map/ppermute | solution.py:463
  240.1 6.2 %collective-permute-start.55 = (f32[24,768]{1,0:T(8,128)S(1)}, f32[24,768]{1,0:T(8,128)S(1)}, u32[]{:S(2)}, u32[]{:S(2)}) collective-permute-start(f32[24,768]{1,0:T(8,128)S(1)} %add_add_fusion.1), channel_id=1, source_target_pairs={{0,24},{2,26},{4,28},{6,30},{8,16},{10,18},{12,20},{14,22},{16,8},... | collective-permute-start | bytes 221192 | tf_op jit(solution)/shard_map/ppermute | solution.py:463
  242.2 5.7 %collective-permute-start.54 = (f32[24,768]{1,0:T(8,128)S(1)}, f32[24,768]{1,0:T(8,128)S(1)}, u32[]{:S(2)}, u32[]{:S(2)}) collective-permute-start(f32[24,768]{1,0:T(8,128)S(1)} %add_add_fusion.1), channel_id=1, source_target_pairs={{0,16},{2,18},{4,20},{6,22},{8,24},{10,26},{12,28},{14,30},{16,0},... | collective-permute-start | bytes 221192 | tf_op jit(solution)/shard_map/ppermute | solution.py:463
  242.2 5.7 %collective-permute-start.53 = (f32[24,768]{1,0:T(8,128)S(1)}, f32[24,768]{1,0:T(8,128)S(1)}, u32[]{:S(2)}, u32[]{:S(2)}) collective-permute-start(f32[24,768]{1,0:T(8,128)S(1)} %add_add_fusion.1), channel_id=1, source_target_pairs={{0,8},{2,10},{4,12},{6,14},{8,0},{10,2},{12,4},{14,6},{16,24},{18,... | collective-permute-start | bytes 221192 | tf_op jit(solution)/shard_map/ppermute | solution.py:463
  (33 other events, 320.0 us)
